TPU v7x, 32 devices: a whole 2x2x4 slice. The times are simulated.
32 devices in a mesh: head: 2 (over x), blk: 16 (over z, y, core).
Axes of the slice: x: 2, y: 2, z: 4, core: 2. Of those that a mesh axis runs over, the one named last changes fastest.
Arguments:
- hidden_states: bfloat16 [16384, 768], P(('head', 'blk')), may hold values from -6 to 6
- owner_rows: int32 [16384], P(('head', 'blk')), may hold values from 0 to 16383, as said below
- lengths: int32 [4], replicated, may hold values from 1005 to 8534
- attention_weight: bfloat16 [768, 2304], P(('head', 'blk')), may hold values from -0.21875 to 0.21875
- output_weight: bfloat16 [768, 768], P(('head', 'blk')), may hold values from -1.25 to 1.25
- upward_weight: bfloat16 [768, 3072], P(('head', 'blk')), may hold values from -0.21875 to 0.21875
- downward_weight: bfloat16 [3072, 768], P(('head', 'blk')), may hold values from -0.109375 to 0.109375
- query_bias: bfloat16 [768], P(('head', 'blk')), may hold values from -3 to 3
- value_bias: bfloat16 [768], P(('head', 'blk')), may hold values from -3 to 3
- output_bias: bfloat16 [768], P(('head', 'blk')), may hold values from -3 to 3
- upward_bias: bfloat16 [3072], P(('head', 'blk')), may hold values from -3 to 3
- downward_bias: bfloat16 [768], P(('head', 'blk')), may hold values from -3 to 3
- first_gain: bfloat16 [768], P(('head', 'blk')), may hold values from 0.5 to 1.5
- first_shift: bfloat16 [768], P(('head', 'blk')), may hold values from -3 to 3
- second_gain: bfloat16 [768], P(('head', 'blk')), may hold values from 0.5 to 1.5
- second_shift: bfloat16 [768], P(('head', 'blk')), may hold values from -3 to 3
- output_cotangent: bfloat16 [16384, 768], P(('head', 'blk')), may hold values from -6 to 6
Outputs:
- layer_output: bfloat16 [16384, 768], P(('head', 'blk'))
- grad_hidden: float32 [16384, 768], P(('head', 'blk'))
- grad_attention_weight: float32 [768, 2304], P(('head', 'blk'))
- grad_output_weight: float32 [768, 768], P(('head', 'blk'))
- grad_upward_weight: float32 [768, 3072], P(('head', 'blk'))
- grad_downward_weight: float32 [3072, 768], P(('head', 'blk'))
- grad_query_bias: float32 [768], P(('head', 'blk'))
- grad_value_bias: float32 [768], P(('head', 'blk'))
- grad_output_bias: float32 [768], P(('head', 'blk'))
- grad_upward_bias: float32 [3072], P(('head', 'blk'))
- grad_downward_bias: float32 [768], P(('head', 'blk'))
- grad_first_gain: float32 [768], P(('head', 'blk'))
- grad_first_shift: float32 [768], P(('head', 'blk'))
- grad_second_gain: float32 [768], P(('head', 'blk'))
- grad_second_shift: float32 [768], P(('head', 'blk'))
Inputs may be any that keep to these rules, and one draw needn't show every extreme that they name: Each packed row appears once. For every i, owner_rows[i] // 512 = (i // 512 % 16) * 2 + i // 512 // 16.
All inputs are finite; a program needn't handle non-finite values.
Results may differ from a plain program's by a relative error of at most 0.013.
The roundings to bfloat16 on the way count: a program that leaves them out, or rounds other values in their place, can miss the bound.
Values may be sent and summed in bfloat16 or wider, within the bound.
No kernel may reach another device: no remote copies, remote signals or barrier semaphores. Data moves between devices by JAX's collectives and lax.ppermute only.
A program may use at most 192 MiB of HBM per device.

v0:
```python
import jax
import jax.numpy as jnp
from jax import lax
from jax.sharding import PartitionSpec as P

DH = 64
SEG_TOK = 502
MEMR = 10
MAX_FULL = 16
QBLOCK = 512


norm_eps = 1e-12
masked_score = -1e30
score_scale = 0.125
root_half = 0.7071067811865476
inverse_root_two_pi = 0.3989422804014327


def padded(block, sides, width):
    for axis, dim in sides:
        count = lax.axis_size(axis)
        forward = [(i, i + 1) for i in range(count - 1)]
        backward = [(target, source) for source, target in forward]
        low = lax.ppermute(
            lax.slice_in_dim(block, block.shape[dim] - width, None, axis=dim), axis, forward
        )
        high = lax.ppermute(lax.slice_in_dim(block, 0, width, axis=dim), axis, backward)
        block = jnp.concatenate([low, block, high], axis=dim)
    return block


def segment_ids(positions, lengths):
    segment_count = (lengths + SEG_TOK - 1) // SEG_TOK
    sequence_rows = lengths + 2 * MEMR * segment_count
    row_ends = jnp.cumsum(sequence_rows, dtype=jnp.int32)
    row_starts = row_ends - sequence_rows
    inside = (
        (positions[:, None] >= row_starts[None, :]) & (positions[:, None] < row_ends[None, :])
    ).astype(jnp.int32)
    sequence_index = jnp.sum(
        inside * jnp.arange(lengths.shape[0], dtype=jnp.int32)[None, :], axis=1, dtype=jnp.int32
    )
    sequence_first = jnp.sum(inside * row_starts[None, :], axis=1, dtype=jnp.int32)
    found_rows = jnp.sum(inside, axis=1, dtype=jnp.int32)
    within = (positions - sequence_first) // (SEG_TOK + 2 * MEMR)
    return jnp.where(found_rows > 0, sequence_index * (MAX_FULL + 2) + within, -1)


def normalize(summed):
    row_mean = jnp.mean(summed, axis=-1, keepdims=True)
    centered = summed - row_mean
    variance = jnp.mean(centered * centered, axis=-1, keepdims=True)
    inverse_std = lax.rsqrt(variance + norm_eps)
    return (centered * inverse_std, inverse_std)


def normalize_back(grad_normed, normed, inverse_std):
    grad_mean = jnp.mean(grad_normed, axis=-1, keepdims=True)
    cross_mean = jnp.mean(grad_normed * normed, axis=-1, keepdims=True)
    return inverse_std * (grad_normed - grad_mean - normed * cross_mean)


def head_major(values, groups):
    return values.reshape(values.shape[0], groups, DH).transpose(1, 0, 2)


def row_major(values):
    return values.transpose(1, 0, 2).reshape(values.shape[1], values.shape[0] * values.shape[2])


def local(
    hidden_states,
    owner_rows,
    lengths,
    attention_weight,
    output_weight,
    upward_weight,
    downward_weight,
    query_bias,
    value_bias,
    output_bias,
    upward_bias,
    downward_bias,
    first_gain,
    first_shift,
    second_gain,
    second_shift,
    output_cotangent,
):
    row_count, model_width = hidden_states.shape
    slot_index = owner_rows % row_count
    gather_order = (
        jnp.zeros((row_count,), jnp.int32)
        .at[slot_index]
        .set(jnp.arange(row_count, dtype=jnp.int32))
    )
    states = jnp.take(hidden_states, gather_order, axis=0)
    grad_result = jnp.take(output_cotangent, gather_order, axis=0).astype(jnp.float32)
    gathered = (
        lax.all_gather(attention_weight, ("head", "blk"), axis=0, tiled=True),
        lax.all_gather(output_weight, ("head", "blk"), axis=0, tiled=True),
        lax.all_gather(upward_weight, ("head", "blk"), axis=0, tiled=True),
        lax.all_gather(downward_weight, ("head", "blk"), axis=0, tiled=True),
        lax.all_gather(query_bias, ("head", "blk"), axis=0, tiled=True),
        lax.all_gather(value_bias, ("head", "blk"), axis=0, tiled=True),
        lax.all_gather(output_bias, ("head", "blk"), axis=0, tiled=True),
        lax.all_gather(upward_bias, ("head", "blk"), axis=0, tiled=True),
        lax.all_gather(downward_bias, ("head", "blk"), axis=0, tiled=True),
        lax.all_gather(first_gain, ("head", "blk"), axis=0, tiled=True),
        lax.all_gather(first_shift, ("head", "blk"), axis=0, tiled=True),
        lax.all_gather(second_gain, ("head", "blk"), axis=0, tiled=True),
        lax.all_gather(second_shift, ("head", "blk"), axis=0, tiled=True),
    )
    triple_weight, mixer_weight, upward_full, downward_full = (
        gathered[0],
        gathered[1],
        gathered[2],
        gathered[3],
    )
    small_params = [element.astype(jnp.float32) for element in gathered[4:]]
    (
        bias_query,
        bias_value,
        bias_output,
        bias_upward,
        bias_downward,
        gain_one,
        shift_one,
        gain_two,
        shift_two,
    ) = small_params
    head_split = lax.axis_size("head")
    part_width = model_width // head_split
    groups = part_width // DH
    group_rows = head_split * row_count
    margin = SEG_TOK + 2 * MEMR - 1
    key_span = QBLOCK + 2 * margin
    block_count = group_rows // QBLOCK
    item_count = block_count * groups
    first_row = lax.axis_index("blk") * group_rows
    query_segments = segment_ids(first_row + jnp.arange(group_rows, dtype=jnp.int32), lengths)
    key_segments = segment_ids(
        first_row - margin + jnp.arange(group_rows + 2 * margin, dtype=jnp.int32), lengths
    )
    bias_joint = jnp.concatenate([bias_query, jnp.zeros((model_width,), jnp.float32), bias_value])
    projected = (
        jnp.dot(states, triple_weight, preferred_element_type=jnp.float32) + bias_joint
    ).astype(jnp.bfloat16)
    grouped = lax.all_to_all(
        projected.reshape(row_count, 3, head_split, part_width),
        "head",
        split_axis=2,
        concat_axis=0,
        tiled=True,
    )
    grouped = grouped.reshape(group_rows, 3, part_width)
    extended = padded(grouped[:, 1:], (("blk", 0),), margin)
    query_heads = head_major(grouped[:, 0], groups)
    key_heads = head_major(extended[:, 0], groups)
    value_heads = head_major(extended[:, 1], groups)

    def pieces(item_index):
        head_index = item_index % groups
        block_start = item_index // groups * QBLOCK
        query_part = lax.dynamic_slice(query_heads, (head_index, block_start, 0), (1, QBLOCK, DH))[
            0
        ]
        key_part = lax.dynamic_slice(key_heads, (head_index, block_start, 0), (1, key_span, DH))[0]
        value_part = lax.dynamic_slice(
            value_heads, (head_index, block_start, 0), (1, key_span, DH)
        )[0]
        allowed = (
            lax.dynamic_slice_in_dim(query_segments, block_start, QBLOCK)[:, None]
            == lax.dynamic_slice_in_dim(key_segments, block_start, key_span)[None, :]
        )
        scores = (
            jnp.einsum("qd,kd->qk", query_part, key_part, preferred_element_type=jnp.float32)
            * score_scale
        )
        scores = jnp.where(allowed, scores, masked_score)
        return (head_index, block_start, query_part, key_part, value_part, scores)

    def forward_item(item_index):
        head_index, block_start, query_part, key_part, value_part, scores = pieces(item_index)
        row_max = jnp.max(scores, axis=1, keepdims=True)
        exp_scores = jnp.exp(scores - row_max)
        row_total = jnp.sum(exp_scores, axis=1, keepdims=True)
        weights = (exp_scores / row_total).astype(jnp.bfloat16)
        return (
            jnp.dot(weights, value_part, preferred_element_type=jnp.float32),
            row_max[:, 0],
            row_total[:, 0],
        )

    attn_mix, row_maxes, row_totals = lax.map(forward_item, jnp.arange(item_count, dtype=jnp.int32))
    attn_mix = (
        attn_mix.reshape(block_count, groups, QBLOCK, DH)
        .transpose(0, 2, 1, 3)
        .reshape(group_rows, 1, part_width)
        .astype(jnp.bfloat16)
    )
    attended = lax.all_to_all(attn_mix, "head", split_axis=0, concat_axis=1, tiled=True).reshape(
        row_count, model_width
    )
    branch = jnp.dot(attended, mixer_weight, preferred_element_type=jnp.float32) + bias_output
    normed_one, scale_one = normalize(states.astype(jnp.float32) + branch)
    first_norm = normed_one * gain_one + shift_one
    inner_rows = first_norm.astype(jnp.bfloat16)
    lifted = jnp.dot(inner_rows, upward_full, preferred_element_type=jnp.float32) + bias_upward
    activated = jax.nn.gelu(lifted, approximate=False).astype(jnp.bfloat16)
    branch_two = (
        jnp.dot(activated, downward_full, preferred_element_type=jnp.float32) + bias_downward
    )
    normed_two, scale_two = normalize(first_norm + branch_two)
    result = normed_two * gain_two + shift_two
    layer_output = jnp.take(result.astype(jnp.bfloat16), slot_index, axis=0)
    again_weights = (
        lax.all_gather(attention_weight, ("head", "blk"), axis=0, tiled=True),
        lax.all_gather(output_weight, ("head", "blk"), axis=0, tiled=True),
        lax.all_gather(upward_weight, ("head", "blk"), axis=0, tiled=True),
        lax.all_gather(downward_weight, ("head", "blk"), axis=0, tiled=True),
    )
    back_triple, back_mixer, back_upward, back_downward = (
        again_weights[0],
        again_weights[1],
        again_weights[2],
        again_weights[3],
    )
    grad_second_gain = jnp.sum(grad_result * normed_two, axis=0)
    grad_second_shift = jnp.sum(grad_result, axis=0)
    grad_mid = normalize_back(grad_result * gain_two, normed_two, scale_two)
    grad_down_rows = grad_mid.astype(jnp.bfloat16)
    grad_downward_bias = jnp.sum(grad_down_rows.astype(jnp.float32), axis=0)
    grad_downward_weight = jnp.einsum(
        "rf,rd->fd", activated, grad_down_rows, preferred_element_type=jnp.float32
    )
    grad_activated = jnp.einsum(
        "rd,fd->rf", grad_down_rows, back_downward, preferred_element_type=jnp.float32
    )
    gelu_slope = 0.5 * (1.0 + lax.erf(lifted * root_half)) + lifted * inverse_root_two_pi * jnp.exp(
        -0.5 * lifted * lifted
    )
    grad_lifted = (grad_activated * gelu_slope).astype(jnp.bfloat16)
    grad_upward_bias = jnp.sum(grad_lifted.astype(jnp.float32), axis=0)
    grad_upward_weight = jnp.einsum(
        "rd,rf->df", inner_rows, grad_lifted, preferred_element_type=jnp.float32
    )
    grad_first = (
        jnp.einsum("rf,df->rd", grad_lifted, back_upward, preferred_element_type=jnp.float32)
        + grad_mid
    )
    grad_first_gain = jnp.sum(grad_first * normed_one, axis=0)
    grad_first_shift = jnp.sum(grad_first, axis=0)
    grad_residual = normalize_back(grad_first * gain_one, normed_one, scale_one)
    grad_branch = grad_residual.astype(jnp.bfloat16)
    grad_output_bias = jnp.sum(grad_branch.astype(jnp.float32), axis=0)
    grad_output_weight = jnp.einsum(
        "rd,re->de", attended, grad_branch, preferred_element_type=jnp.float32
    )
    grad_attended = jnp.einsum(
        "re,de->rd", grad_branch, back_mixer, preferred_element_type=jnp.float32
    ).astype(jnp.bfloat16)
    grad_rows = lax.all_to_all(
        grad_attended.reshape(row_count, head_split, part_width),
        "head",
        split_axis=1,
        concat_axis=0,
        tiled=True,
    )
    grad_heads = head_major(grad_rows.reshape(group_rows, part_width), groups)

    def backward_item(item_index, carry):
        grad_query, grad_key, grad_value = carry
        head_index, block_start, query_part, key_part, value_part, scores = pieces(item_index)
        grad_part = lax.dynamic_slice(grad_heads, (head_index, block_start, 0), (1, QBLOCK, DH))[0]
        probabilities = (
            jnp.exp(scores - row_maxes[item_index][:, None]) / row_totals[item_index][:, None]
        )
        weights = probabilities.astype(jnp.bfloat16)
        grad_probs = jnp.einsum(
            "qd,kd->qk", grad_part, value_part, preferred_element_type=jnp.float32
        )
        shared = jnp.sum(probabilities * grad_probs, axis=1, keepdims=True)
        grad_scores = (probabilities * (grad_probs - shared)).astype(jnp.bfloat16)
        query_term = (
            jnp.dot(grad_scores, key_part, preferred_element_type=jnp.float32) * score_scale
        )
        key_term = (
            jnp.einsum("qk,qd->kd", grad_scores, query_part, preferred_element_type=jnp.float32)
            * score_scale
        )
        value_term = jnp.einsum("qk,qd->kd", weights, grad_part, preferred_element_type=jnp.float32)
        grad_query = lax.dynamic_update_slice(
            grad_query, query_term[None], (head_index, block_start, 0)
        )
        key_before = lax.dynamic_slice(grad_key, (head_index, block_start, 0), (1, key_span, DH))
        grad_key = lax.dynamic_update_slice(
            grad_key, key_before + key_term[None], (head_index, block_start, 0)
        )
        value_before = lax.dynamic_slice(
            grad_value, (head_index, block_start, 0), (1, key_span, DH)
        )
        grad_value = lax.dynamic_update_slice(
            grad_value, value_before + value_term[None], (head_index, block_start, 0)
        )
        return (grad_query, grad_key, grad_value)

    start_query = jnp.zeros((groups, group_rows, DH), jnp.float32)
    start_keys = jnp.zeros((groups, group_rows + 2 * margin, DH), jnp.float32)
    grad_query, grad_key, grad_value = lax.fori_loop(
        0, item_count, backward_item, (start_query, start_keys, start_keys)
    )
    pair_grad = jnp.stack([row_major(grad_key), row_major(grad_value)], axis=1)
    margin_grads = jnp.concatenate([pair_grad[:margin], pair_grad[margin + group_rows :]], axis=0)
    returned = padded(margin_grads.astype(jnp.bfloat16), (("blk", 0),), margin).astype(
        margin_grads.dtype
    )
    own_grads = pair_grad[margin : margin + group_rows]
    own_grads = own_grads.at[:margin].add(returned[:margin])
    own_grads = own_grads.at[group_rows - margin :].add(returned[3 * margin :])
    head_grads = jnp.concatenate([row_major(grad_query)[:, None], own_grads], axis=1).astype(
        jnp.bfloat16
    )
    grad_joint = lax.all_to_all(
        head_grads.reshape(group_rows, 3, 1, part_width),
        "head",
        split_axis=0,
        concat_axis=2,
        tiled=True,
    )
    grad_joint = grad_joint.reshape(row_count, 3 * model_width)
    grad_attention_weight = jnp.einsum(
        "rd,rc->dc", states, grad_joint, preferred_element_type=jnp.float32
    )
    joint_wide = grad_joint.astype(jnp.float32)
    grad_query_bias = jnp.sum(joint_wide[:, :model_width], axis=0)
    grad_value_bias = jnp.sum(joint_wide[:, 2 * model_width :], axis=0)
    grad_input = (
        jnp.einsum("rc,dc->rd", grad_joint, back_triple, preferred_element_type=jnp.float32)
        + grad_residual
    )
    grad_hidden = jnp.take(grad_input, slot_index, axis=0)
    reduced = (
        lax.psum_scatter(grad_attention_weight, ("head", "blk"), scatter_dimension=0, tiled=True),
        lax.psum_scatter(grad_output_weight, ("head", "blk"), scatter_dimension=0, tiled=True),
        lax.psum_scatter(grad_upward_weight, ("head", "blk"), scatter_dimension=0, tiled=True),
        lax.psum_scatter(grad_downward_weight, ("head", "blk"), scatter_dimension=0, tiled=True),
        lax.psum_scatter(grad_query_bias, ("head", "blk"), scatter_dimension=0, tiled=True),
        lax.psum_scatter(grad_value_bias, ("head", "blk"), scatter_dimension=0, tiled=True),
        lax.psum_scatter(grad_output_bias, ("head", "blk"), scatter_dimension=0, tiled=True),
        lax.psum_scatter(grad_upward_bias, ("head", "blk"), scatter_dimension=0, tiled=True),
        lax.psum_scatter(grad_downward_bias, ("head", "blk"), scatter_dimension=0, tiled=True),
        lax.psum_scatter(grad_first_gain, ("head", "blk"), scatter_dimension=0, tiled=True),
        lax.psum_scatter(grad_first_shift, ("head", "blk"), scatter_dimension=0, tiled=True),
        lax.psum_scatter(grad_second_gain, ("head", "blk"), scatter_dimension=0, tiled=True),
        lax.psum_scatter(grad_second_shift, ("head", "blk"), scatter_dimension=0, tiled=True),
    )
    return (
        layer_output,
        grad_hidden,
        reduced[0],
        reduced[1],
        reduced[2],
        reduced[3],
        reduced[4],
        reduced[5],
        reduced[6],
        reduced[7],
        reduced[8],
        reduced[9],
        reduced[10],
        reduced[11],
        reduced[12],
    )


def solution(mesh):
    return jax.shard_map(
        local,
        mesh=mesh,
        in_specs=(
            P(("head", "blk"), None),
            P(("head", "blk")),
            P(),
            P(("head", "blk"), None),
            P(("head", "blk"), None),
            P(("head", "blk"), None),
            P(("head", "blk"), None),
            P(("head", "blk")),
            P(("head", "blk")),
            P(("head", "blk")),
            P(("head", "blk")),
            P(("head", "blk")),
            P(("head", "blk")),
            P(("head", "blk")),
            P(("head", "blk")),
            P(("head", "blk")),
            P(("head", "blk"), None),
        ),
        out_specs=(
            P(("head", "blk"), None),
            P(("head", "blk"), None),
            P(("head", "blk"), None),
            P(("head", "blk"), None),
            P(("head", "blk"), None),
            P(("head", "blk"), None),
            P(("head", "blk")),
            P(("head", "blk")),
            P(("head", "blk")),
            P(("head", "blk")),
            P(("head", "blk")),
            P(("head", "blk")),
            P(("head", "blk")),
            P(("head", "blk")),
            P(("head", "blk")),
        ),
        check_vma=False,
    )
```

profile of v0, /device:TPU:0, one launch (start us, length us, event | category | flops | bytes accessed | tf_op | source)
XLA Modules:
  0.0 1122.5 jit_solution(16868481704428519942)
XLA Ops:
  17.0 42.5 %all-reduce.19 = (bf16[768]{0:T(1024)(128)(2,1)S(1)}, bf16[768]{0:T(1024)(128)(2,1)S(1)}, bf16[768]{0:T(1024)(128)(2,1)S(1)}, bf16[768]{0:T(1024)(128)(2,1)S(1)}...) all-reduce(bf16[768]{0:T(1024)(128)(2,1)S(1)} %dynamic-update-slice, ...), channel_id=1, replica_groups=mesh['head'=2,'blk'=16] {'head','blk'}, use_global_device_ids=true, to_apply=%add.1 | all-reduce | flops 9216 | bytes 36864
  65.3 8.5 all-gather.5.cloned.1.call-done
  73.8 5.5 fusion.59
  79.2 4.6 reshape.285
  85.5 5.0 all-to-all-start
  91.4 30.3 %all-to-all-done = bf16[512,3,2,384]{3,0,1,2:T(8,128)(2,1)} async-done(((bf16[512,3,2,384]{3,0,1,2:T(8,128)(2,1)}), bf16[512,3,2,384]{3,0,1,2:T(8,128)(2,1)}, u32[]{:S(2)}, u32[]{:S(2)}) %all-to-all-start) | async-done | bytes 2359328 | tf_op jit(solution)/shard_map/all_to_all | solution.py:150
  138.4 15.3 %concatenate.34 = bf16[2066,2,384]{2,0,1:T(8,128)(2,1)S(1)} concatenate(bf16[521,2,384]{2,0,1:T(8,128)(2,1)} %copy.120, bf16[1024,2,384]{2,0,1:T(8,128)(2,1)} %slice.119, bf16[521,2,384]{2,0,1:T(8,128)(2,1)} %copy.121), dimensions={0} | concatenate | bytes 6346752 | tf_op jit(solution)/shard_map/concatenate | solution.py:29
  155.7 3.8 copy.122
  159.5 3.7 copy.125
  163.2 3.8 copy.123
  166.9 4.5 copy.126
  171.4 88.1 %while.37 = (s32[]{:T(128)}, bf16[12,512,64]{1,2,0:T(8,128)(2,1)}, f32[12,512]{1,0:T(8,128)S(1)}, f32[12,512]{1,0:T(8,128)S(1)}, s32[12]{0:T(128)S(1)}, /*index=...) while((s32[]{:T(128)}, bf16[12,512,64]{1,2,0:T(8,128)(2,1)}, ...), condition=%wide.region_11.13_spmd, body=%wide.region_8.12_spmd.sunk | while | flops 210845728 | bytes 10656329 | solution.py:196
  259.5 3.4 copy.148
  270.4 4.7 all-to-all-start.1
  277.2 5.9 all-to-all-done.1
  290.4 19.3 %fusion.46 = (bf16[512,3072]{1,0:T(8,128)(2,1)}, f32[512,3072]{1,0:T(8,128)}) fusion(f32[3072]{0:T(1024)S(1)} %convert_element_type.147, bf16[768,3072]{1,0:T(8,128)(2,1)} %all-gather.9.cloned.1.call-done, f32[512,768]{1,0:T(8,128)S(1)} %get-tuple-element.675, f32[768]{0:T(1024)S(1)} %convert_element_type.145, f32[768]{0:T(1024)S(1)} %convert_element_type.144, ...), kind=kOutput, calls=%fused_computation.69 | convolution fusion | flops 2521694208 | bytes 15751168 | tf_op jit(solution)/shard_map/dot_general | solution.py:210
  309.6 6.2 fusion.98
  318.7 4.9 convert_reduce_fusion
  330.6 3.5 all-to-all-start.2
  334.2 7.9 all-to-all-done.2
  349.3 219.6 %while.38 = (s32[]{:T(128)}, bf16[6,1024,64]{1,2,0:T(8,128)(2,1)}, f32[6,2066,64]{1,2,0:T(8,128)}, f32[6,2066,64]{1,2,0:T(8,128)}, s32[1024]{0:T(1024)S(1)}, /*i...) while((s32[]{:T(128)}, bf16[6,1024,64]{1,2,0:T(8,128)(2,1)}, ...), condition=%wide.region_22.24_spmd, body=%wide.region_20.23_spmd.sunk | while | flops 518297504 | bytes 28882556 | solution.py:311
  359.0 3.3 dynamic_update_slice.62
  364.7 3.3 dynamic_update_slice.63
  377.7 3.3 dynamic_update_slice.62
  383.5 3.3 dynamic_update_slice.63
  402.1 3.3 dynamic_update_slice.63
  415.1 3.3 dynamic_update_slice.62
  433.8 3.3 dynamic_update_slice.62
  452.5 3.3 dynamic_update_slice.62
  458.2 3.3 dynamic_update_slice.63
  568.9 3.4 fusion.43
  575.0 14.3 %collective-permute-start.2 = (bf16[521,2,384]{2,1,0:T(2,128)(2,1)}, bf16[521,2,384]{2,1,0:T(2,128)(2,1)}, u32[]{:S(2)}, u32[]{:S(2)}) collective-permute-start(bf16[521,2,384]{2,1,0:T(2,128)(2,1)} %copy.136), channel_id=1, source_target_pairs={{0,1},{1,2},{2,3},{3,4},{4,5},{5,6},{6,7},{7,8},{8,9},{9,10},{10,1... | collective-permute-start | bytes 2400776 | tf_op jit(solution)/shard_map/ppermute | solution.py:25
  593.0 3.8 fusion.81
  596.9 4.0 fusion.60
  607.2 7.3 concatenate.36
  621.8 10.8 scatter-add.6
  632.6 4.7 fusion.66
  637.3 16.2 %scatter-add.9 = f32[1024,2,1,384]{0,3,1,2:T(8,128)S(1)} dynamic-update-slice(f32[1024,2,1,384]{0,3,1,2:T(8,128)S(1)} %bitcast.183, f32[521,2,1,384]{0,3,1,2:T(8,128)} %fusion.66, s32[]{:T(128)} %constant.433.clone.1, s32[]{:T(128)} %constant.386.clone.1, s32[]{:T(128)} %constant.386.clone.1, s32[]{:T(128)} %constant.386.clone.1) | dynamic-update-slice | bytes 3201028 | tf_op jit(solution)/shard_map/scatter-add | solution.py:321
  656.5 4.9 copy.141
  661.4 33.9 %all_to_all.60 = bf16[1024,3,1,384]{3,1,2,0:T(4,128)(2,1)S(1)} all-to-all(bf16[1024,3,1,384]{3,1,2,0:T(4,128)(2,1)S(1)} %copy.141), channel_id=1, replica_groups=mesh['head'=2,'blk'=16] {'head'}, dimensions={0} | all-to-all | bytes 4718592 | tf_op jit(solution)/shard_map/all_to_all | solution.py:325
  700.0 5.1 fusion.87
  705.1 8.9 fusion.88
  714.3 8.7 fusion.84
  733.4 3.8 convolution_add_fusion.1
  742.2 50.2 %all-reduce.18 = (f32[768]{0:T(1024)S(1)}, f32[768]{0:T(1024)S(1)}, f32[768]{0:T(1024)S(1)}, f32[3072]{0:T(1024)S(1)}, f32[768]{0:T(1024)S(1)}, /*index=5*/f32[7...) all-reduce(f32[768]{0:T(1024)S(1)} %get-tuple-element.578, ...), channel_id=6, replica_groups=mesh['head'=2,'blk'=16] {'head','blk'}, use_global_device_ids=true, to_apply=%region_28.30.clone | all-reduce | flops 9216 | bytes 73728
  798.9 32.9 %reduce-scatter.5.cloned.1.call-done = f32[24,2304]{1,0:T(8,128)} async-done(((f32[768,2304]{1,0:T(8,128)}), f32[24,2304]{1,0:T(8,128)}) %reduce-scatter.5.cloned.1.call-update) | async-done | bytes 221200 | tf_op jit(solution)/shard_map/reduce_scatter | solution.py:345
  831.8 141.1 %reduce-scatter.9.cloned.1.call-done = f32[24,3072]{1,0:T(8,128)} async-done(((f32[768,3072]{1,0:T(8,128)}), f32[24,3072]{1,0:T(8,128)}) %reduce-scatter.9.cloned.1.call-update) | async-done | bytes 294928 | tf_op jit(solution)/shard_map/reduce_scatter | solution.py:347
  972.9 142.3 %reduce-scatter.11.cloned.1.call-done = f32[96,768]{1,0:T(8,128)} async-done(((f32[3072,768]{1,0:T(8,128)}), f32[96,768]{1,0:T(8,128)}) %reduce-scatter.11.cloned.1.call-update) | async-done | bytes 294928 | tf_op jit(solution)/shard_map/reduce_scatter | solution.py:348
  (427 shorter events, 373.6 us)
Async XLA Ops:
  7.2 56.0 %copy-start = (bf16[512,768]{1,0:T(8,128)(2,1)S(1)}, bf16[512,768]{1,0:T(8,128)(2,1)}, u32[]{:S(2)}) copy-start(bf16[512,768]{1,0:T(8,128)(2,1)} %param.27) | copy-start | bytes 2359300
  7.2 66.6 %all-gather.5.cloned.1.call-start = ((), (), s32[]{:S(2)}) async-start(), calls=%async_computation.8 | async-start | bytes 3649536 | tf_op jit(solution)/shard_map/all_gather | solution.py:101
  7.9 279.4 %all-gather.7.cloned.1.call-start = ((), (), s32[]{:S(2)}) async-start(), calls=%async_computation.9 | async-start | bytes 1216512 | tf_op jit(solution)/shard_map/all_gather | solution.py:102
  8.7 281.7 %all-gather.9.cloned.1.call-start = ((), (), s32[]{:S(2)}) async-start(), calls=%async_computation.10 | async-start | bytes 4866048 | tf_op jit(solution)/shard_map/all_gather | solution.py:103
  60.7 2.5 copy-start.20
  65.2 8.5 copy-start.18
  85.5 5.6 copy-start.26
  85.5 36.1 %all-to-all-start = ((bf16[512,3,2,384]{3,0,1,2:T(8,128)(2,1)}), bf16[512,3,2,384]{3,0,1,2:T(8,128)(2,1)}, u32[]{:S(2)}, u32[]{:S(2)}) async-start(bf16[512,3,2,384]{3,0,1,2:T(8,128)(2,1)} %copy.115), calls=%async_computation | async-start | bytes 4718592 | tf_op jit(solution)/shard_map/all_to_all | solution.py:150
  90.6 219.1 %all-gather.11.cloned.1.call-start = ((), (), s32[]{:S(2)}) async-start(), calls=%async_computation.11 | async-start | bytes 4866048 | tf_op jit(solution)/shard_map/all_gather | solution.py:104
  125.3 8.8 collective-permute-start
  129.0 7.2 collective-permute-start.1
  259.5 3.4 copy-start.11
  266.2 9.0 copy-start.5
  270.4 12.8 %all-to-all-start.1 = ((bf16[2,2,98304]{2,1,0:T(2,128)(2,1)}), bf16[2,2,98304]{2,1,0:T(2,128)(2,1)}, u32[]{:S(2)}, u32[]{:S(2)}) async-start(bf16[2,2,98304]{2,1,0:T(2,128)(2,1)} %reshape.361), calls=%async_computation.1 | async-start | bytes 1572864 | tf_op jit(solution)/shard_map/all_to_all | solution.py:203
  287.3 3.0 copy-start.17
  290.0 36.8 %copy-start.13 = (f32[512,768]{1,0:T(8,128)}, f32[512,768]{1,0:T(8,128)S(1)}, u32[]{:S(2)}) copy-start(f32[512,768]{1,0:T(8,128)S(1)} %get-tuple-element.675) | copy-start | bytes 4718596
  309.6 9.0 copy-start.28
  316.1 2.5 copy-start.23
  317.0 6.6 slice-start
  318.7 4.9 copy-start.12
  318.7 5.0 slice-start.1
  323.6 3.2 copy-start.27
  326.8 1.7 copy-start.25
  327.3 1.2 copy-start.14
  330.6 11.5 %all-to-all-start.2 = ((bf16[512,2,384]{0,2,1:T(8,128)(2,1)}), bf16[512,2,384]{0,2,1:T(8,128)(2,1)S(1)}, u32[]{:S(2)}, u32[]{:S(2)}) async-start(bf16[512,2,384]{0,2,1:T(8,128)(2,1)} %bitcast.37), calls=%async_computation.2 | async-start | bytes 1572864 | tf_op jit(solution)/shard_map/all_to_all | solution.py:264
  334.1 464.8 %reduce-scatter.7.cloned.1.call-start = ((), (), s32[]{:S(2)}) async-start(), calls=%async_computation.13 | async-start | bytes 2433024 | tf_op jit(solution)/shard_map/reduce_scatter | solution.py:346
  572.8 16.4 %copy-start.9 = (bf16[521,2,384]{0,2,1:T(8,128)(2,1)}, bf16[521,2,384]{0,2,1:T(8,128)(2,1)S(1)}, u32[]{:S(2)}) copy-start(bf16[521,2,384]{0,2,1:T(8,128)(2,1)S(1)} %get-tuple-element.667) | copy-start | bytes 2400772
  572.8 16.4 %copy-start.10 = (bf16[521,2,384]{0,2,1:T(8,128)(2,1)}, bf16[521,2,384]{0,2,1:T(8,128)(2,1)S(1)}, u32[]{:S(2)}) copy-start(bf16[521,2,384]{0,2,1:T(8,128)(2,1)S(1)} %get-tuple-element.668) | copy-start | bytes 2400772
  575.0 26.0 %collective-permute-start.2 = (bf16[521,2,384]{2,1,0:T(2,128)(2,1)}, bf16[521,2,384]{2,1,0:T(2,128)(2,1)}, u32[]{:S(2)}, u32[]{:S(2)}) collective-permute-start(bf16[521,2,384]{2,1,0:T(2,128)(2,1)} %copy.136), channel_id=1, source_target_pairs={{0,1},{1,2},{2,3},{3,4},{4,5},{5,6},{6,7},{7,8},{8,9},{9,10},{10,1... | collective-permute-start | bytes 2400776 | tf_op jit(solution)/shard_map/ppermute | solution.py:25
  591.2 5.7 copy-start.2
  591.2 12.8 %collective-permute-start.3 = (bf16[521,2,384]{2,1,0:T(2,128)(2,1)}, bf16[521,2,384]{2,1,0:T(2,128)(2,1)}, u32[]{:S(2)}, u32[]{:S(2)}) collective-permute-start(bf16[521,2,384]{2,1,0:T(2,128)(2,1)} %copy.137), channel_id=1, source_target_pairs={{1,0},{2,1},{3,2},{4,3},{5,4},{6,5},{7,6},{8,7},{9,8},{10,9},{11,1... | collective-permute-start | bytes 2400776 | tf_op jit(solution)/shard_map/ppermute | solution.py:28
  596.9 234.9 %reduce-scatter.5.cloned.1.call-start = ((), (), s32[]{:S(2)}) async-start(), calls=%async_computation.12 | async-start | bytes 7299072 | tf_op jit(solution)/shard_map/reduce_scatter | solution.py:345
  614.5 5.3 copy-start.3
  617.1 2.8 copy-start.8
  632.6 4.7 copy-start.6
  697.0 2.9 copy-start.19
  700.0 29.1 %copy-start.7 = (bf16[512,3,2,1,384]{0,4,2,1,3:T(8,128)(2,1)}, bf16[512,3,2,1,384]{0,4,2,1,3:T(8,128)(2,1)S(1)}, u32[]{:S(2)}) copy-start(bf16[512,3,2,1,384]{0,4,2,1,3:T(8,128)(2,1)S(1)} %copy.143) | copy-start | bytes 7077892
  705.1 267.8 %reduce-scatter.9.cloned.1.call-start = ((), (), s32[]{:S(2)}) async-start(), calls=%async_computation.14 | async-start | bytes 9732096 | tf_op jit(solution)/shard_map/reduce_scatter | solution.py:347
  714.0 401.2 %reduce-scatter.11.cloned.1.call-start = ((), (), s32[]{:S(2)}) async-start(), calls=%async_computation.15 | async-start | bytes 9732096 | tf_op jit(solution)/shard_map/reduce_scatter | solution.py:348
  723.0 0.7 copy-start.21
  723.0 1.2 copy-start.4
  724.2 2.7 copy-start.22
  729.1 3.1 copy-start.15
  729.1 4.4 copy-start.24
  737.2 378.0 %copy-start.1 = (bf16[512,768]{1,0:T(8,128)(2,1)S(1)}, bf16[512,768]{1,0:T(8,128)(2,1)}, u32[]{:S(2)}) copy-start(bf16[512,768]{1,0:T(8,128)(2,1)} %param.27) | copy-start | bytes 2359300
  739.8 57.8 %copy-start.16 = (f32[512,768]{1,0:T(8,128)S(1)}, f32[512,768]{1,0:T(8,128)}, u32[]{:S(2)}) copy-start(f32[512,768]{1,0:T(8,128)} %gather_fusion) | copy-start | bytes 4718596
Sparse Core Ops, SparseCore 0:
  10.9 62.7 all-gather.4
  76.7 53.7 all-gather.6
  133.4 62.5 all-gather.8
  198.7 62.3 all-gather.10
  597.0 100.8 reduce-scatter.6
  705.2 126.5 reduce-scatter.4
  838.3 134.5 reduce-scatter.8
  980.4 134.7 reduce-scatter.10
where the time goes:
time: 1140 us; the launch traced here: 1120 us
  waiting for transfers between devices  372 us (33%)
  matrix products  253 us (22%)
  local copies, waits for them, and re-layouts  245 us (21%)
  blocking collectives  127 us (11%)
  other arithmetic  53 us (5%)
  starting transfers between devices  33.5 us (3%)
  loops' own time  24.6 us (2%)
  between operations  15.3 us (1%)
    reduce_scatter x1, waiting for transfers between devices, local(): lax.psum_scatter(grad_downward_weight, ('head', 'blk'), scatter_dimension...  142 us
    reduce_scatter x1, waiting for transfers between devices, local(): lax.psum_scatter(grad_upward_weight, ('head', 'blk'), scatter_dimension=0...  141 us
    unnamed x2, blocking collectives  92.7 us
    dot_general x24, matrix products, pieces(): jnp.einsum('qd,kd->qk', query_part, key_part, preferred_element_type=jnp....  48.6 us
    dynamic_update_slice x12, local copies, waits for them, and re-layouts, backward_item(): lax.dynamic_update_slice(grad_key, key_before + key_term[None], (head_ind...  37.1 us
    dynamic_update_slice x12, local copies, waits for them, and re-layouts, backward_item(): lax.dynamic_update_slice(grad_value, value_before + value_term[None], (he...  37 us
    all_to_all x1, blocking collectives, local(): lax.all_to_all(head_grads.reshape(group_rows, 3, 1, part_width), 'head',...  33.9 us
    reduce_scatter x1, waiting for transfers between devices, local(): lax.psum_scatter(grad_attention_weight, ('head', 'blk'), scatter_dimensio...  32.9 us
  transfers between devices with their start and end apart: 15, of which 7 were waited for; matrix products, arithmetic and copies ran while one was open for 26% of the time, Pallas kernels for 0%

commit v1 on v0

v1 whole, which is shorter than its diff:
```python
import functools

import jax
import jax.numpy as jnp
import numpy as np
from jax import lax
from jax.experimental import pallas as pl
from jax.experimental.pallas import tpu as pltpu
from jax.sharding import PartitionSpec as P

DH = 64
SEG_TOK = 502
MEMR = 10
SEG_ROWS = SEG_TOK + 2 * MEMR
AXES = ("head", "blk")
TILE = 128
PAIR = 2 * DH
WINDOW = 544

norm_eps = 1e-12
masked_score = -1e30
score_scale = 0.125
root_half = 0.7071067811865476
inverse_root_two_pi = 0.3989422804014327
f32 = jnp.float32
bf16 = jnp.bfloat16


def swap(block, bit, count):
    return lax.ppermute(block, AXES, [(i, i ^ bit) for i in range(count)])


def gathered(shard, order, count, me):
    held, have = shard, []
    for bit in order:
        axis = sum(b > bit for b in have)
        have.append(bit)
        other = jnp.expand_dims(swap(held, bit, count), axis)
        own = jnp.expand_dims(held, axis)
        held = jnp.where(
            (me & bit) == 0,
            jnp.concatenate([own, other], axis=axis),
            jnp.concatenate([other, own], axis=axis),
        )
    return held.reshape((count * shard.shape[0],) + shard.shape[1:])


def reduced(blocks, order, count, me):
    have = sorted(order, reverse=True)
    held = blocks.reshape((2,) * len(have) + blocks.shape[1:])
    for step, bit in enumerate(order):
        axis = have.index(bit)
        have.remove(bit)
        mine = ((me & bit) != 0).astype(jnp.int32)
        keep = lax.dynamic_index_in_dim(held, mine, axis, keepdims=False)
        send = lax.dynamic_index_in_dim(held, 1 - mine, axis, keepdims=False)
        total = keep.astype(f32) + swap(send, bit, count).astype(f32)
        held = total if not have else total.astype(blocks.dtype)
    return held


def segment_at(lengths_ref, sequences, position):
    start = jnp.int32(0)
    low = jnp.int32(0)
    high = jnp.int32(0)
    for i in range(sequences):
        tokens = lengths_ref[i]
        end = start + tokens + 2 * MEMR * lax.div(tokens + (SEG_TOK - 1), jnp.int32(SEG_TOK))
        inside = (position >= start) & (position < end)
        first = start + lax.div(position - start, jnp.int32(SEG_ROWS)) * SEG_ROWS
        low = jnp.where(inside, first, low)
        high = jnp.where(inside, jnp.minimum(first + SEG_ROWS, end), high)
        start = end
    return low, high


def over_segments(lengths_ref, sequences, first_row, rows, side, body):
    def step(position):
        low, high = segment_at(lengths_ref, sequences, position)
        high = jnp.maximum(high, position + 1)
        low_at = low - first_row + side
        high_at = high - first_row + side
        window = jnp.minimum(lax.div(low_at, jnp.int32(16)) * 16, rows + 2 * side - WINDOW)
        window = pl.multiple_of(jnp.maximum(window, 0), 16)
        tile_from = lax.div(jnp.maximum(low - first_row, 0), jnp.int32(TILE))
        tile_to = lax.div(jnp.minimum(high - first_row, rows) + TILE - 1, jnp.int32(TILE))
        body(low_at, high_at, window, tile_from, tile_to)
        return high

    lax.while_loop(lambda position: position < first_row + rows, step, first_row)


def two_heads(block):
    lane = lax.broadcasted_iota(jnp.int32, block.shape, 1)
    zero = jnp.zeros_like(block)
    return jnp.concatenate(
        [jnp.where(lane < DH, block, zero), jnp.where(lane < DH, zero, block)], axis=0
    )


def own_blocks(product):
    return jnp.concatenate([product[:DH, :TILE], product[DH:, TILE:]], axis=0).T


def key_bias(low_at, high_at, window):
    row = lax.broadcasted_iota(jnp.int32, (WINDOW, 2 * TILE), 0) + window
    return jnp.where((row >= low_at) & (row < high_at), 0.0, masked_score)


def rows_inside(tile, low_at, high_at, side, shape, dim):
    at = lax.broadcasted_iota(jnp.int32, shape, dim)
    if dim == 1:
        at = at & (TILE - 1)
    at = at + (tile * TILE + side)
    return (at >= low_at) & (at < high_at)


NT = (((1,), (1,)), ((), ()))
NN = (((1,), (0,)), ((), ()))


def mul(left, right, dims=NN):
    return lax.dot_general(left, right, dims, preferred_element_type=f32)


def forward_kernel(
    sequences, side, lengths_ref, first_ref, q_ref, k_ref, v_ref, o_ref, stat_ref, bias_ref, vt_ref
):
    rows = q_ref.shape[0]
    stat_ref[...] = jnp.zeros_like(stat_ref)
    o_ref[...] = jnp.zeros_like(o_ref)

    def segment(low_at, high_at, window, tile_from, tile_to):
        bias_ref[...] = key_bias(low_at, high_at, window)
        vt_ref[...] = v_ref[pl.ds(window, WINDOW), :].T

        def one(tile, carry):
            at = pl.ds(pl.multiple_of(tile * TILE, TILE), TILE)
            wide = pl.ds(pl.multiple_of(tile * 2 * TILE, 2 * TILE), 2 * TILE)
            queries = two_heads(q_ref[at, :])
            scores = mul(k_ref[pl.ds(window, WINDOW), :], queries, NT) + bias_ref[...]
            top = jnp.max(scores, axis=0, keepdims=True)
            raised = jnp.exp(scores - top)
            inverse = 1.0 / jnp.sum(raised, axis=0, keepdims=True)
            weights = (raised * inverse).astype(bf16)
            mixed = own_blocks(mul(vt_ref[...], weights)).astype(bf16)
            here = rows_inside(tile, low_at, high_at, side, (TILE, PAIR), 0)
            o_ref[at, :] = jnp.where(here, mixed, o_ref[at, :])
            there = rows_inside(tile, low_at, high_at, side, (1, 2 * TILE), 1)
            stat_ref[0, 0:1, wide] = jnp.where(there, top, stat_ref[0, 0:1, wide])
            stat_ref[0, 1:2, wide] = jnp.where(there, inverse, stat_ref[0, 1:2, wide])
            return carry

        lax.fori_loop(tile_from, tile_to, one, 0)

    over_segments(lengths_ref, sequences, first_ref[0], rows, side, segment)


def backward_kernel(
    sequences,
    side,
    lengths_ref,
    first_ref,
    q_ref,
    k_ref,
    v_ref,
    g_ref,
    stat_ref,
    dq_ref,
    dk_ref,
    dv_ref,
    bias_ref,
    kt_ref,
    dq_acc,
    dk_acc,
    dv_acc,
):
    rows = q_ref.shape[0]
    dq_acc[...] = jnp.zeros_like(dq_acc)
    dk_acc[...] = jnp.zeros_like(dk_acc)
    dv_acc[...] = jnp.zeros_like(dv_acc)

    def segment(low_at, high_at, window, tile_from, tile_to):
        bias_ref[...] = key_bias(low_at, high_at, window)
        keys_at = pl.ds(window, WINDOW)
        kt_ref[...] = k_ref[keys_at, :].T

        def one(tile, carry):
            at = pl.ds(pl.multiple_of(tile * TILE, TILE), TILE)
            wide = pl.ds(pl.multiple_of(tile * 2 * TILE, 2 * TILE), 2 * TILE)
            queries = two_heads(q_ref[at, :])
            grads = two_heads(g_ref[at, :])
            there = rows_inside(tile, low_at, high_at, side, (1, 2 * TILE), 1)
            top = jnp.where(there, stat_ref[0, 0:1, wide], -masked_score)
            inverse = jnp.where(there, stat_ref[0, 1:2, wide], 0.0)
            scores = mul(k_ref[keys_at, :], queries, NT) + bias_ref[...]
            probs = jnp.exp(scores - top) * inverse
            grad_probs = mul(v_ref[keys_at, :], grads, NT)
            shared = jnp.sum(probs * grad_probs, axis=0, keepdims=True)
            grad_scores = (probs * (grad_probs - shared)).astype(bf16)
            dv_acc[keys_at, :] += mul(probs.astype(bf16), grads)
            dk_acc[keys_at, :] += mul(grad_scores, queries)
            dq_acc[at, :] += own_blocks(mul(kt_ref[...], grad_scores))
            return carry

        lax.fori_loop(tile_from, tile_to, one, 0)

    over_segments(lengths_ref, sequences, first_ref[0], rows, side, segment)
    dq_ref[...] = (dq_acc[...] * score_scale).astype(bf16)
    dk_ref[...] = dk_acc[...].astype(bf16)
    dv_ref[...] = dv_acc[...].astype(bf16)


def attention_forward(lengths, first, queries, keys, values, side):
    rows, width = queries.shape
    pairs = width // PAIR
    column = lambda n: pl.BlockSpec((n, PAIR), lambda h, *_: (0, h))
    return pl.pallas_call(
        functools.partial(forward_kernel, lengths.shape[0], side),
        name="attention_forward",
        out_shape=(
            jax.ShapeDtypeStruct((rows, width), bf16),
            jax.ShapeDtypeStruct((pairs, 8, 2 * rows), f32),
        ),
        grid_spec=pltpu.PrefetchScalarGridSpec(
            num_scalar_prefetch=2,
            grid=(pairs,),
            in_specs=[column(rows), column(keys.shape[0]), column(keys.shape[0])],
            out_specs=[column(rows), pl.BlockSpec((1, 8, 2 * rows), lambda h, *_: (h, 0, 0))],
            scratch_shapes=[
                pltpu.VMEM((WINDOW, 2 * TILE), f32),
                pltpu.VMEM((PAIR, WINDOW), bf16),
            ],
        ),
        compiler_params=pltpu.CompilerParams(vmem_limit_bytes=48 * 2**20),
    )(lengths, first, queries, keys, values)


def attention_backward(lengths, first, queries, keys, values, grads, stats, side):
    rows, width = queries.shape
    wide = keys.shape[0]
    pairs = width // PAIR
    column = lambda n: pl.BlockSpec((n, PAIR), lambda h, *_: (0, h))
    return pl.pallas_call(
        functools.partial(backward_kernel, lengths.shape[0], side),
        name="attention_backward",
        out_shape=(
            jax.ShapeDtypeStruct((rows, width), bf16),
            jax.ShapeDtypeStruct((wide, width), bf16),
            jax.ShapeDtypeStruct((wide, width), bf16),
        ),
        grid_spec=pltpu.PrefetchScalarGridSpec(
            num_scalar_prefetch=2,
            grid=(pairs,),
            in_specs=[
                column(rows),
                column(wide),
                column(wide),
                column(rows),
                pl.BlockSpec((1, 8, 2 * rows), lambda h, *_: (h, 0, 0)),
            ],
            out_specs=[column(rows), column(wide), column(wide)],
            scratch_shapes=[
                pltpu.VMEM((WINDOW, 2 * TILE), f32),
                pltpu.VMEM((PAIR, WINDOW), bf16),
                pltpu.VMEM((rows, PAIR), f32),
                pltpu.VMEM((wide, PAIR), f32),
                pltpu.VMEM((wide, PAIR), f32),
            ],
        ),
        compiler_params=pltpu.CompilerParams(vmem_limit_bytes=48 * 2**20),
    )(lengths, first, queries, keys, values, grads, stats)


def normalize(summed):
    row_mean = jnp.mean(summed, axis=-1, keepdims=True)
    centered = summed - row_mean
    variance = jnp.mean(centered * centered, axis=-1, keepdims=True)
    inverse_std = lax.rsqrt(variance + norm_eps)
    return (centered * inverse_std, inverse_std)


def normalize_back(grad_normed, normed, inverse_std):
    grad_mean = jnp.mean(grad_normed, axis=-1, keepdims=True)
    cross_mean = jnp.mean(grad_normed * normed, axis=-1, keepdims=True)
    return inverse_std * (grad_normed - grad_mean - normed * cross_mean)


def local(
    hidden_states,
    owner_rows,
    lengths,
    attention_weight,
    output_weight,
    upward_weight,
    downward_weight,
    query_bias,
    value_bias,
    output_bias,
    upward_bias,
    downward_bias,
    first_gain,
    first_shift,
    second_gain,
    second_shift,
    output_cotangent,
):
    rows, width = hidden_states.shape
    heads_axis, blocks_axis = lax.axis_size("head"), lax.axis_size("blk")
    count = heads_axis * blocks_axis
    me = lax.axis_index(AXES)
    place = lax.axis_index("blk") * heads_axis + lax.axis_index("head")
    first = (place * rows).astype(jnp.int32).reshape(1)
    bits = [1 << b for b in range((count - 1).bit_length())]
    far = [b for b in bits if b not in (1, 2, blocks_axis)]
    order_a = tuple(far + [2, blocks_axis, 1])
    order_b = tuple(far + [blocks_axis, 2, 1])
    back_a = order_a[::-1]
    back_b = order_b[::-1]

    def shift(block, by):
        index_of = lambda q: q % heads_axis * blocks_axis + q // heads_axis
        pairs = [
            (index_of(q), index_of(q + by)) for q in range(count) if 0 <= q + by < count
        ]
        return lax.ppermute(block, AXES, pairs)

    slot_index = owner_rows % rows
    pick = (slot_index[None, :] == jnp.arange(rows, dtype=jnp.int32)[:, None]).astype(bf16)
    states = jnp.dot(pick, hidden_states, preferred_element_type=f32).astype(bf16)
    grad_result = jnp.dot(pick, output_cotangent, preferred_element_type=f32)

    thin = -(-max(SEG_ROWS - 1 - rows, 0) // 16) * 16
    near = min(rows, -(-(SEG_ROWS - 1) // 16) * 16)
    side = near + thin
    parts = [
        shift(states[rows - near :], 1),
        states,
        shift(states[:near], -1),
    ]
    if thin:
        parts = [shift(states[rows - thin :], 2), *parts, shift(states[:thin], -2)]
    reach = jnp.concatenate(parts, axis=0)

    half = 3 * width // 2
    weight_a = gathered(attention_weight[:, :half], order_a, count, me)
    weight_b = gathered(attention_weight[:, half:], order_b, count, me)
    triple_weight = jnp.concatenate([weight_a, weight_b], axis=1)
    small = (
        query_bias,
        value_bias,
        output_bias,
        downward_bias,
        first_gain,
        first_shift,
        second_gain,
        second_shift,
        upward_bias,
    )
    small_widths = [s.shape[0] for s in small]
    small_ends = np.cumsum(small_widths)
    packed = jnp.concatenate(small)
    packed = jnp.pad(packed, (0, -packed.shape[0] % 128))
    packed_all = gathered(packed[None], order_a, count, me).astype(f32)
    (
        bias_query,
        bias_value,
        bias_output,
        bias_downward,
        gain_one,
        shift_one,
        gain_two,
        shift_two,
        bias_upward,
    ) = [
        packed_all[:, end - n : end].reshape(count * n)
        for end, n in zip(small_ends, small_widths)
    ]
    mixer_weight = gathered(output_weight, order_a, count, me)
    upward_full = gathered(upward_weight, order_a, count, me)
    downward_full = gathered(downward_weight, order_b, count, me)

    queries = (
        (jnp.dot(states, triple_weight[:, :width], preferred_element_type=f32) + bias_query)
        .astype(bf16) * jnp.asarray(score_scale, bf16)
    )
    keys = jnp.dot(reach, triple_weight[:, width : 2 * width], preferred_element_type=f32).astype(bf16)
    values = (
        jnp.dot(reach, triple_weight[:, 2 * width :], preferred_element_type=f32) + bias_value
    ).astype(bf16)
    attended, stats = attention_forward(lengths, first, queries, keys, values, side)

    branch = jnp.dot(attended, mixer_weight, preferred_element_type=f32) + bias_output
    normed_one, scale_one = normalize(states.astype(f32) + branch)
    first_norm = normed_one * gain_one + shift_one
    inner_rows = first_norm.astype(bf16)
    lifted = jnp.dot(inner_rows, upward_full, preferred_element_type=f32) + bias_upward
    activated = jax.nn.gelu(lifted, approximate=False).astype(bf16)
    branch_two = jnp.dot(activated, downward_full, preferred_element_type=f32) + bias_downward
    normed_two, scale_two = normalize(first_norm + branch_two)
    result = normed_two * gain_two + shift_two
    layer_output = jnp.take(result.astype(bf16), slot_index, axis=0)

    grad_second_gain = jnp.sum(grad_result * normed_two, axis=0)
    grad_second_shift = jnp.sum(grad_result, axis=0)
    grad_mid = normalize_back(grad_result * gain_two, normed_two, scale_two)
    grad_down_rows = grad_mid.astype(bf16)
    grad_downward_bias = jnp.sum(grad_down_rows.astype(f32), axis=0)
    grad_downward_weight = jnp.einsum(
        "rf,rd->fd", activated, grad_down_rows, preferred_element_type=f32
    ).astype(bf16)
    grad_activated = jnp.einsum(
        "rd,fd->rf", grad_down_rows, downward_full, preferred_element_type=f32
    )
    gelu_slope = 0.5 * (1.0 + lax.erf(lifted * root_half)) + lifted * inverse_root_two_pi * jnp.exp(
        -0.5 * lifted * lifted
    )
    grad_lifted = (grad_activated * gelu_slope).astype(bf16)
    grad_upward_bias = jnp.sum(grad_lifted.astype(f32), axis=0)
    grad_upward_weight = jnp.einsum(
        "rd,rf->df", inner_rows, grad_lifted, preferred_element_type=f32
    ).astype(bf16)
    grad_first = (
        jnp.einsum("rf,df->rd", grad_lifted, upward_full, preferred_element_type=f32) + grad_mid
    )
    grad_first_gain = jnp.sum(grad_first * normed_one, axis=0)
    grad_first_shift = jnp.sum(grad_first, axis=0)
    grad_residual = normalize_back(grad_first * gain_one, normed_one, scale_one)
    grad_branch = grad_residual.astype(bf16)
    grad_output_bias = jnp.sum(grad_branch.astype(f32), axis=0)
    grad_output_weight = jnp.einsum(
        "rd,re->de", attended, grad_branch, preferred_element_type=f32
    ).astype(bf16)
    grad_attended = jnp.einsum(
        "re,de->rd", grad_branch, mixer_weight, preferred_element_type=f32
    ).astype(bf16)
    by_device = lambda grad: grad.reshape((count, grad.shape[0] // count) + grad.shape[1:])
    out_downward = reduced(by_device(grad_downward_weight), back_b, count, me)
    out_upward = reduced(by_device(grad_upward_weight), back_a, count, me)
    out_mixer = reduced(by_device(grad_output_weight), back_b, count, me)

    grad_query, grad_key, grad_value = attention_backward(
        lengths, first, queries, keys, values, grad_attended, stats, side
    )
    grad_triple = jnp.concatenate(
        [
            jnp.einsum("rd,rc->dc", states, grad_query, preferred_element_type=f32),
            jnp.einsum("rd,rc->dc", reach, grad_key, preferred_element_type=f32),
            jnp.einsum("rd,rc->dc", reach, grad_value, preferred_element_type=f32),
        ],
        axis=1,
    ).astype(bf16)
    grad_query_bias = jnp.sum(grad_query.astype(f32), axis=0)
    grad_value_bias = jnp.sum(grad_value.astype(f32), axis=0)
    grad_reach = jnp.einsum(
        "rc,dc->rd", grad_key, triple_weight[:, width : 2 * width], preferred_element_type=f32
    ) + jnp.einsum(
        "rc,dc->rd", grad_value, triple_weight[:, 2 * width :], preferred_element_type=f32
    )
    from_right = shift(grad_reach[thin : side].astype(bf16), -1).astype(f32)
    from_left = shift(grad_reach[side + rows : side + rows + near].astype(bf16), 1).astype(f32)
    grad_input = (
        grad_reach[side : side + rows]
        + jnp.einsum("rc,dc->rd", grad_query, triple_weight[:, :width], preferred_element_type=f32)
        + grad_residual
    )
    grad_input = (
        grad_input
        + jnp.pad(from_right, ((rows - near, 0), (0, 0)))
        + jnp.pad(from_left, ((0, rows - near), (0, 0)))
    )
    if thin:
        far_right = shift(grad_reach[:thin].astype(bf16), -2).astype(f32)
        far_left = shift(grad_reach[side + rows + near :].astype(bf16), 2).astype(f32)
        grad_input = (
            grad_input
            + jnp.pad(far_right, ((rows - thin, 0), (0, 0)))
            + jnp.pad(far_left, ((0, rows - thin), (0, 0)))
        )
    grad_hidden = jnp.take(grad_input, slot_index, axis=0)

    out_a = reduced(by_device(grad_triple[:, :half]), back_a, count, me)
    out_b = reduced(by_device(grad_triple[:, half:]), back_b, count, me)
    out_triple = jnp.concatenate([out_a, out_b], axis=1)
    grads_small = (
        grad_query_bias,
        grad_value_bias,
        grad_output_bias,
        grad_downward_bias,
        grad_first_gain,
        grad_first_shift,
        grad_second_gain,
        grad_second_shift,
        grad_upward_bias,
    )
    packed_grads = jnp.concatenate([by_device(g) for g in grads_small], axis=1)
    packed_grads = jnp.pad(packed_grads, ((0, 0), (0, -packed_grads.shape[1] % 128)))
    summed = reduced(packed_grads, back_a, count, me)
    (
        out_query,
        out_value,
        out_output,
        out_down_bias,
        out_gain_one,
        out_shift_one,
        out_gain_two,
        out_shift_two,
        out_up_bias,
    ) = [summed[end - n : end] for end, n in zip(small_ends, small_widths)]
    return (
        layer_output,
        grad_hidden,
        out_triple,
        out_mixer,
        out_upward,
        out_downward,
        out_query,
        out_value,
        out_output,
        out_up_bias,
        out_down_bias,
        out_gain_one,
        out_shift_one,
        out_gain_two,
        out_shift_two,
    )


def solution(mesh):
    matrix, vector = P(AXES, None), P(AXES)
    return jax.shard_map(
        local,
        mesh=mesh,
        in_specs=(matrix, vector, P(), *[matrix] * 4, *[vector] * 9, matrix),
        out_specs=(*[matrix] * 6, *[vector] * 9),
        check_vma=False,
    )
```

time: 1140 us -> 511 us (0.45); the launches traced: 1120 us -> 508 us
  waiting for transfers between devices: 372 us -> 174 us
  local copies, waits for them, and re-layouts: 245 us -> 54.3 us
  matrix products: 253 us -> 75.5 us
  blocking collectives: 127 us -> 0 us
  starting transfers between devices: 33.5 us -> 111 us
  Pallas kernels: 0 us -> 45.9 us
  loops' own time: 24.6 us -> 0 us
  between operations: 15.3 us -> 2.57 us
    reduce_scatter x4 -> x0, waiting for transfers between devices: 316 us -> none  [the longest x1 142 us: local(): lax.psum_scatter(grad_downward_weight, ('head', 'blk'), scatter_dimension...]
    dot_general x95 -> x19, matrix products: 244 us -> 70.7 us  [the longest x1 17.8 us: local(): jnp.dot(inner_rows, upward_full, preferred_element_type=f32) + bias_upward]
    ppermute x4 -> x68, waiting for transfers between devices: 0.01 us -> 174 us  [the longest x60 172 us: swap(): return lax.ppermute(block, AXES, [(i, i ^ bit) for i in range(count)])]
    unnamed x2 -> x0, blocking collectives: 92.7 us -> none
    ppermute x4 -> x68, starting transfers between devices: 19.7 us -> 111 us  [the longest x60 89.8 us: swap(): return lax.ppermute(block, AXES, [(i, i ^ bit) for i in range(count)])]
    dynamic_update_slice x48 -> x0, local copies, waits for them, and re-layouts: 75.2 us -> none  [the longest x12 37.1 us: backward_item(): lax.dynamic_update_slice(grad_key, key_before + key_term[None], (head_ind...]
    pallas_call x0 -> x2, Pallas kernels: none -> 45.9 us  [the longest x1 24.3 us: attention_backward(): pl.pallas_call(functools.partial(backward_kernel, lengths.shape[0], side)...]
    all_to_all x3 -> x0, waiting for transfers between devices: 44.1 us -> none  [the longest x1 30.3 us: local(): lax.all_to_all(projected.reshape(row_count, 3, head_split, part_width), '...]
  transfers between devices with their start and end apart: 15 -> 68, of which waited for: 7 -> 34; matrix products, arithmetic and copies ran while one was open for 26% -> 21% of each run, Pallas kernels for 0% -> 4%
where the time goes in v1:
time: 511 us; the launch traced here: 508 us
  waiting for transfers between devices  174 us (34%)
  starting transfers between devices  111 us (22%)
  matrix products  75.5 us (15%)
  local copies, waits for them, and re-layouts  54.3 us (11%)
  Pallas kernels  45.9 us (9%)
  other arithmetic  45.2 us (9%)
    ppermute x60, waiting for transfers between devices, swap(): return lax.ppermute(block, AXES, [(i, i ^ bit) for i in range(count)])  172 us
    ppermute x60, starting transfers between devices, swap(): return lax.ppermute(block, AXES, [(i, i ^ bit) for i in range(count)])  89.8 us
    pallas_call x1, Pallas kernels, attention_backward(): pl.pallas_call(functools.partial(backward_kernel, lengths.shape[0], side)...  24.3 us
    ppermute x8, starting transfers between devices, shift(): return lax.ppermute(block, AXES, pairs)  21.6 us
    pallas_call x1, Pallas kernels, attention_forward(): pl.pallas_call(functools.partial(forward_kernel, lengths.shape[0], side),...  21.6 us
    dot_general x1, matrix products, local(): jnp.dot(inner_rows, upward_full, preferred_element_type=f32) + bias_upward  17.8 us
    select_n x51, other arithmetic, gathered(): jnp.where(me & bit == 0, jnp.concatenate([own, other], axis=axis), jnp.co...  15.9 us
    dynamic_slice x6, local copies, waits for them, and re-layouts, reduced(): keep = lax.dynamic_index_in_dim(held, mine, axis, keepdims=False)  13.4 us
  transfers between devices with their start and end apart: 68, of which 34 were waited for; matrix products, arithmetic and copies ran while one was open for 21% of the time, Pallas kernels for 4%

profile of v1, /device:TPU:0, one launch (start us, length us, event | category | flops | bytes accessed | tf_op | source)
XLA Modules:
  0.0 508.4 jit_solution(1052909633232479321)
XLA Ops:
  3.9 4.9 collective-permute-start.11
  11.6 4.2 collective-permute-start
  19.3 6.8 %collective-permute-done.5 = bf16[1,384]{1,0:T(2,128)(2,1)S(1)} collective-permute-done((bf16[1,384]{1,0:T(2,128)(2,1)S(1)}, bf16[1,384]{1,0:T(2,128)(2,1)S(1)}, u32[]{:S(2)}, u32[]{:S(2)}) %collective-permute-start.5) | collective-permute-done | bytes 800 | tf_op jit(solution)/shard_map/ppermute | solution.py:30
  30.8 3.6 collective-permute-done.7
  34.5 8.7 %collective-permute-done.8 = bf16[2,2,2,1,384]{4,1,0,3,2:T(2,128)(2,1)S(1)} collective-permute-done((bf16[2,2,2,1,384]{4,1,0,3,2:T(2,128)(2,1)S(1)}, bf16[2,2,2,1,384]{4,1,0,3,2:T(2,128)(2,1)S(1)}, u32[]{:S(2)}, u32[]{:S(2)}) %collective-permute-start.8) | collective-permute-done | bytes 6176 | tf_op jit(solution)/shard_map/ppermute | solution.py:30
  73.8 3.3 collective-permute-start.20
  83.0 4.2 collective-permute-done.29
  91.2 5.0 collective-permute-done.15
  97.8 4.6 collective-permute-done.16
  102.5 5.8 %collective-permute-done.2 = bf16[2,2,24,1152]{3,2,1,0:T(8,128)(2,1)S(1)} collective-permute-done((bf16[2,2,24,1152]{3,2,1,0:T(8,128)(2,1)S(1)}, bf16[2,2,24,1152]{3,2,1,0:T(8,128)(2,1)S(1)}, u32[]{:S(2)}, u32[]{:S(2)}) %collective-permute-start.2) | collective-permute-done | bytes 221216 | tf_op jit(solution)/shard_map/ppermute | solution.py:30
  113.1 5.2 %collective-permute-done.30 = bf16[2,96,768]{2,1,0:T(8,128)(2,1)S(1)} collective-permute-done((bf16[2,96,768]{2,1,0:T(8,128)(2,1)S(1)}, bf16[2,96,768]{2,1,0:T(8,128)(2,1)S(1)}, u32[]{:S(2)}, u32[]{:S(2)}) %collective-permute-start.30) | collective-permute-done | bytes 294944 | tf_op jit(solution)/shard_map/ppermute | solution.py:30
  123.5 7.9 %collective-permute-done.3 = bf16[2,2,2,24,1152]{4,3,2,1,0:T(8,128)(2,1)S(1)} collective-permute-done((bf16[2,2,2,24,1152]{4,3,2,1,0:T(8,128)(2,1)S(1)}, bf16[2,2,2,24,1152]{4,3,2,1,0:T(8,128)(2,1)S(1)}, u32[]{:S(2)}, u32[]{:S(2)}) %collective-permute-start.3) | collective-permute-done | bytes 442400 | tf_op jit(solution)/shard_map/ppermute | solution.py:30
  133.6 6.9 %collective-permute-done.31 = bf16[2,2,96,768]{3,2,1,0:T(8,128)(2,1)S(1)} collective-permute-done((bf16[2,2,96,768]{3,2,1,0:T(8,128)(2,1)S(1)}, bf16[2,2,96,768]{3,2,1,0:T(8,128)(2,1)S(1)}, u32[]{:S(2)}, u32[]{:S(2)}) %collective-permute-start.31) | collective-permute-done | bytes 589856 | tf_op jit(solution)/shard_map/ppermute | solution.py:30
  148.2 3.6 add_convert_fusion.v_ref
  154.3 13.8 %collective-permute-done.27 = bf16[2,2,2,24,3072]{4,3,2,1,0:T(8,128)(2,1)S(1)} collective-permute-done((bf16[2,2,2,24,3072]{4,3,2,1,0:T(8,128)(2,1)S(1)}, bf16[2,2,2,24,3072]{4,3,2,1,0:T(8,128)(2,1)S(1)}, u32[]{:S(2)}, u32[]{:S(2)}) %collective-permute-start.27) | collective-permute-done | bytes 1179680 | tf_op jit(solution)/shard_map/ppermute | solution.py:30
  170.7 21.6 %attention_forward.1 = (bf16[512,768]{1,0:T(8,128)(2,1)S(1)}, f32[6,8,1024]{2,1,0:T(8,128)S(1)}) custom-call(s32[4]{0:T(128)S(1)} %copy-done.3, s32[1]{0:T(128)} %bitcast.first_ref, bf16[512,768]{1,0:T(8,128)(2,1)S(1)} %fusion.28.q_ref, bf16[1568,768]{1,0:T(8,128)(2,1)S(1)} %convolution_convert_fusion.2.k_ref, bf16[1568,768]{1,0:T(8,128)(2,1)} %add_convert_fusion.v_ref), custom_call_target="tpu_custom_call" | custom-call | tf_op jit(solution)/shard_map/attention_forward/pallas_call | solution.py:218
  192.6 5.9 %collective-permute-start.33 = (bf16[2,2,2,2,96,768]{5,4,3,2,1,0:T(8,128)(2,1)S(1)}, bf16[2,2,2,2,96,768]{5,4,3,2,1,0:T(8,128)(2,1)S(1)}, u32[]{:S(2)}, u32[]{:S(2)}) collective-permute-start(bf16[2,2,2,2,96,768]{5,4,3,2,1,0:T(8,128)(2,1)S(1)} %maximum_select_fusion.3), channel_id=1, source_target_pairs={{0,1},{1,0},{2,3},{3,2},{4,5},{5,4},{6,7},{7,6},{8,9},{9,8},{10,11... | collective-permute-start | bytes 7077896 | tf_op jit(solution)/shard_map/ppermute | solution.py:30
  200.9 3.0 maximum_select_fusion
  204.5 17.8 %fusion.2 = (bf16[512,3072]{1,0:T(8,128)(2,1)S(1)}, f32[512,3072]{1,0:T(8,128)}) fusion(f32[3072]{0:T(1024)S(1)} %copy-done.29, bf16[768,3072]{1,0:T(8,128)(2,1)S(1)} %bitcast.400, f32[512,768]{1,0:T(8,128)S(1)} %get-tuple-element.93, f32[768]{0:T(1024)S(1)} %add.369, f32[768]{0:T(1024)S(1)} %mul.153, f32[512]{0:T(512)S(1)} %add_rsqrt_fusion.1, ...), kind=kOutput, calls=%fused_computation.6 | convolution fusion | flops 2521694208 | bytes 15751168 | tf_op jit(solution)/shard_map/dot_general | solution.py:397
  227.2 4.7 convolution_convert_fusion
  231.9 6.3 %convert_reduce_fusion = (f32[3072]{0:T(1024)S(1)}, bf16[512,3072]{1,0:T(8,128)(2,1)S(1)}) fusion(f32[512,3072]{1,0:T(8,128)} %get-tuple-element.95, f32[3072]{0:T(1024)S(1)} %copy-done.29, bf16[3072,768]{1,0:T(8,128)(2,1)S(1)} %bitcast.403, f32[512,768]{1,0:T(8,128)S(1)} %get-tuple-element.36), kind=kOutput, calls=%fused_computation.12 | convolution fusion | flops 2436756480 | bytes 15753216 | tf_op jit(solution)/shard_map/rd,fd->rf/dot_general | solution.py:412
  238.3 3.1 multiply_reduce_fusion.1
  241.4 4.9 convolution_convert_fusion.1
  249.6 24.3 %attention_backward.1 = (bf16[512,768]{1,0:T(8,128)(2,1)S(1)}, bf16[1568,768]{1,0:T(8,128)(2,1)S(1)}, bf16[1568,768]{1,0:T(8,128)(2,1)}) custom-call(s32[4]{0:T(128)S(1)} %copy-done.3, s32[1]{0:T(128)} %bitcast.first_ref, bf16[512,768]{1,0:T(8,128)(2,1)S(1)} %fusion.28.q_ref, bf16[1568,768]{1,0:T(8,128)(2,1)} %copy-done.2, ...), custom_call_target="tpu_custom_call" | custom-call | tf_op jit(solution)/shard_map/attention_backward/pallas_call | solution.py:244
  276.3 3.5 convolution_convert_fusion.5
  281.8 3.5 convolution_convert_fusion.6
  285.2 4.3 fusion.70
  290.6 6.5 %collective-permute-start.63 = (f32[2,2,2,2,384]{4,3,2,1,0:T(2,128)S(1)}, f32[2,2,2,2,384]{4,3,2,1,0:T(2,128)S(1)}, u32[]{:S(2)}, u32[]{:S(2)}) collective-permute-start(f32[2,2,2,2,384]{4,3,2,1,0:T(2,128)S(1)} %bitcast.467), channel_id=1, source_target_pairs={{0,1},{1,0},{2,3},{3,2},{4,5},{5,4},{6,7},{7,6},{8,9},{9,8},{10,11... | collective-permute-start | bytes 73736 | tf_op jit(solution)/shard_map/ppermute | solution.py:30
  297.0 5.2 %constant_dynamic-slice_fusion.11 = (bf16[2,2,2,2,1,96,768]{6,5,4,3,2,1,0:T(8,128)(2,1)}, bf16[2,2,2,2,1,96,768]{6,5,4,3,2,1,0:T(8,128)(2,1)}) fusion(bf16[2,2,2,2,2,96,768]{6,5,4,3,2,1,0:T(8,128)(2,1)} %bitcast.399, s32[]{:T(128)S(6)} %select_n.956, s32[]{:T(128)S(6)} %select_n.957), kind=kLoop, calls=%fused_computation.241 | loop fusion | bytes 9437192 | tf_op jit(solution)/shard_map/jit(dynamic_index_in_dim)/dynamic_slice | solution.py:55
  303.8 3.9 copy.114
  307.6 3.0 constant_dynamic-slice_fusion.17
  310.7 7.0 %fusion.81 = (bf16[1568,768]{1,0:T(8,128)(2,1)S(1)}, f32[1568,768]{1,0:T(8,128)}) fusion(f32[1568,768]{1,0:T(8,128)} %fusion.70, bf16[1568,768]{1,0:T(8,128)(2,1)S(1)} %copy-done.5, bf16[768,1152]{1,0:T(8,128)(2,1)} %bitcast.388), kind=kOutput, calls=%fused_computation.302 | convolution fusion | flops 1852096512 | bytes 15630336 | tf_op jit(solution)/shard_map/rc,dc->rd/dot_general | solution.py:457
  327.0 12.0 %collective-permute-start.65 = (f32[2,2,384]{2,1,0:T(2,128)S(1)}, f32[2,2,384]{2,1,0:T(2,128)S(1)}, u32[]{:S(2)}, u32[]{:S(2)}) collective-permute-start(f32[2,2,384]{2,1,0:T(2,128)S(1)} %bitcast.476), channel_id=1, source_target_pairs={{0,2},{1,3},{2,0},{3,1},{4,6},{5,7},{6,4},{7,5},{8,10},{9,11},{10,... | collective-permute-start | bytes 18440 | tf_op jit(solution)/shard_map/ppermute | solution.py:30
  342.4 5.4 %collective-permute-start.35 = (bf16[512,768]{1,0:T(8,128)(2,1)}, bf16[512,768]{1,0:T(8,128)(2,1)}, u32[]{:S(2)}, u32[]{:S(2)}) collective-permute-start(bf16[512,768]{1,0:T(8,128)(2,1)} %get-tuple-element.48), channel_id=1, source_target_pairs={{0,16},{16,1},{1,17},{17,2},{2,18},{18,3},{3,19},{19,4},{4,20},{20... | collective-permute-start | bytes 2359304 | tf_op jit(solution)/shard_map/ppermute | solution.py:326
  351.0 3.5 collective-permute-done.66
  354.7 4.2 constant_dynamic-slice_fusion.13
  364.1 3.0 collective-permute-start.37
  371.9 8.3 %collective-permute-start.49 = (bf16[2,2,2,24,768]{4,3,2,1,0:T(8,128)(2,1)S(1)}, bf16[2,2,2,24,768]{4,3,2,1,0:T(8,128)(2,1)S(1)}, u32[]{:S(2)}, u32[]{:S(2)}) collective-permute-start(bf16[2,2,2,24,768]{4,3,2,1,0:T(8,128)(2,1)S(1)} %dynamic-slice_bitcast_fusion.9), channel_id=1, source_target_pairs={{0,2},{1,3},{2,0},{3,1},{4,6},{5,7},{6,4},{7,5},{8,10},{9,11},{10,... | collective-permute-start | bytes 884744 | tf_op jit(solution)/shard_map/ppermute | solution.py:30
  396.1 3.8 collective-permute-done.51
  405.8 7.0 %collective-permute-done.44 = bf16[2,2,2,24,1152]{4,3,2,1,0:T(8,128)(2,1)S(1)} collective-permute-done((bf16[2,2,2,24,1152]{4,3,2,1,0:T(8,128)(2,1)S(1)}, bf16[2,2,2,24,1152]{4,3,2,1,0:T(8,128)(2,1)S(1)}, u32[]{:S(2)}, u32[]{:S(2)}) %collective-permute-start.44) | collective-permute-done | bytes 442400 | tf_op jit(solution)/shard_map/ppermute | solution.py:30
  419.6 3.8 collective-permute-done.41
  435.9 20.2 %collective-permute-done.59 = bf16[2,2,2,96,768]{4,3,2,1,0:T(8,128)(2,1)S(1)} collective-permute-done((bf16[2,2,2,96,768]{4,3,2,1,0:T(8,128)(2,1)S(1)}, bf16[2,2,2,96,768]{4,3,2,1,0:T(8,128)(2,1)S(1)}, u32[]{:S(2)}, u32[]{:S(2)}) %collective-permute-start.59) | collective-permute-done | bytes 1179680 | tf_op jit(solution)/shard_map/ppermute | solution.py:30
  456.8 6.0 %collective-permute-done.54 = bf16[2,2,2,24,3072]{4,3,1,0,2:T(8,128)(2,1)S(1)} collective-permute-done((bf16[2,2,2,24,3072]{4,3,1,0,2:T(8,128)(2,1)S(1)}, bf16[2,2,2,24,3072]{4,3,1,0,2:T(8,128)(2,1)S(1)}, u32[]{:S(2)}, u32[]{:S(2)}) %collective-permute-start.54) | collective-permute-done | bytes 1179680 | tf_op jit(solution)/shard_map/ppermute | solution.py:30
  465.3 7.6 %collective-permute-done.60 = bf16[2,2,96,768]{3,2,1,0:T(8,128)(2,1)S(1)} collective-permute-done((bf16[2,2,96,768]{3,2,1,0:T(8,128)(2,1)S(1)}, bf16[2,2,96,768]{3,2,1,0:T(8,128)(2,1)S(1)}, u32[]{:S(2)}, u32[]{:S(2)}) %collective-permute-start.60) | collective-permute-done | bytes 589856 | tf_op jit(solution)/shard_map/ppermute | solution.py:30
  473.1 3.4 collective-permute-start.61
  478.5 16.5 %collective-permute-done.61 = bf16[2,96,768]{2,1,0:T(8,128)(2,1)S(1)} collective-permute-done((bf16[2,96,768]{2,1,0:T(8,128)(2,1)S(1)}, bf16[2,96,768]{2,1,0:T(8,128)(2,1)S(1)}, u32[]{:S(2)}, u32[]{:S(2)}) %collective-permute-start.61) | collective-permute-done | bytes 294944 | tf_op jit(solution)/shard_map/ppermute | solution.py:30
  495.9 5.4 %collective-permute-done.56 = bf16[2,24,3072]{2,1,0:T(8,128)(2,1)S(1)} collective-permute-done((bf16[2,24,3072]{2,1,0:T(8,128)(2,1)S(1)}, bf16[2,24,3072]{2,1,0:T(8,128)(2,1)S(1)}, u32[]{:S(2)}, u32[]{:S(2)}) %collective-permute-start.56) | collective-permute-done | bytes 294944 | tf_op jit(solution)/shard_map/ppermute | solution.py:30
  501.4 3.0 collective-permute-done.62
  (408 shorter events, 175.7 us)
Async XLA Ops:
  3.9 118.3 %collective-permute-start.11 = (bf16[512,768]{1,0:T(8,128)(2,1)S(1)}, bf16[512,768]{1,0:T(8,128)(2,1)S(1)}, u32[]{:S(2)}, u32[]{:S(2)}) collective-permute-start(bf16[512,768]{1,0:T(8,128)(2,1)S(1)} %convolution_convert_fusion.8), channel_id=1, source_target_pairs={{0,16},{16,1},{1,17},{17,2},{2,18},{18,3},{3,19},{19,4},{4,20},{20... | collective-permute-start | bytes 2359304 | tf_op jit(solution)/shard_map/ppermute | solution.py:326
  8.8 113.6 %collective-permute-start.12 = (bf16[512,768]{1,0:T(8,128)(2,1)S(1)}, bf16[512,768]{1,0:T(8,128)(2,1)S(1)}, u32[]{:S(2)}, u32[]{:S(2)}) collective-permute-start(bf16[512,768]{1,0:T(8,128)(2,1)S(1)} %convolution_convert_fusion.8), channel_id=1, source_target_pairs={{16,0},{1,16},{17,1},{2,17},{18,2},{3,18},{19,3},{4,19},{20,4},{5,... | collective-permute-start | bytes 2359304 | tf_op jit(solution)/shard_map/ppermute | solution.py:326
  11.6 57.7 %collective-permute-start = (bf16[24,1152]{1,0:T(8,128)(2,1)}, bf16[24,1152]{1,0:T(8,128)(2,1)S(1)}, u32[]{:S(2)}, u32[]{:S(2)}) collective-permute-start(bf16[24,1152]{1,0:T(8,128)(2,1)} %get-tuple-element.71), channel_id=1, source_target_pairs={{0,4},{1,5},{2,6},{3,7},{4,0},{5,1},{6,2},{7,3},{8,12},{9,13},{10,... | collective-permute-start | bytes 165896 | tf_op jit(solution)/shard_map/ppermute | solution.py:30
  15.8 57.9 %collective-permute-start.14 = (bf16[24,1152]{1,0:T(8,128)(2,1)}, bf16[24,1152]{1,0:T(8,128)(2,1)}, u32[]{:S(2)}, u32[]{:S(2)}) collective-permute-start(bf16[24,1152]{1,0:T(8,128)(2,1)} %get-tuple-element.70), channel_id=1, source_target_pairs={{0,4},{1,5},{2,6},{3,7},{4,0},{5,1},{6,2},{7,3},{8,12},{9,13},{10,... | collective-permute-start | bytes 165896 | tf_op jit(solution)/shard_map/ppermute | solution.py:30
  16.1 10.1 %collective-permute-start.5 = (bf16[1,384]{1,0:T(2,128)(2,1)S(1)}, bf16[1,384]{1,0:T(2,128)(2,1)S(1)}, u32[]{:S(2)}, u32[]{:S(2)}) collective-permute-start(bf16[1,384]{1,0:T(2,128)(2,1)S(1)} %broadcast_in_dim.159), channel_id=1, source_target_pairs={{0,4},{1,5},{2,6},{3,7},{4,0},{5,1},{6,2},{7,3},{8,12},{9,13},{10,... | collective-permute-start | bytes 2312 | tf_op jit(solution)/shard_map/ppermute | solution.py:30
  34.4 8.8 %collective-permute-start.8 = (bf16[2,2,2,1,384]{4,1,0,3,2:T(2,128)(2,1)S(1)}, bf16[2,2,2,1,384]{4,1,0,3,2:T(2,128)(2,1)S(1)}, u32[]{:S(2)}, u32[]{:S(2)}) collective-permute-start(bf16[2,2,2,1,384]{4,1,0,3,2:T(2,128)(2,1)S(1)} %broadcast_select_fusion.5), channel_id=1, source_target_pairs={{0,16},{1,17},{2,18},{3,19},{4,20},{5,21},{6,22},{7,23},{8,24},{9,... | collective-permute-start | bytes 18440 | tf_op jit(solution)/shard_map/ppermute | solution.py:30
  44.8 15.9 %collective-permute-start.10 = (bf16[16,768]{1,0:T(8,128)(2,1)}, bf16[16,768]{1,0:T(8,128)(2,1)}, u32[]{:S(2)}, u32[]{:S(2)}) collective-permute-start(bf16[16,768]{1,0:T(8,128)(2,1)} %get-tuple-element.61), channel_id=1, source_target_pairs={{0,1},{16,17},{1,2},{17,18},{2,3},{18,19},{3,4},{19,20},{4,5},{20,... | collective-permute-start | bytes 73736 | tf_op jit(solution)/shard_map/ppermute | solution.py:326
  65.3 58.0 %collective-permute-start.13 = (bf16[16,768]{1,0:T(8,128)(2,1)}, bf16[16,768]{1,0:T(8,128)(2,1)S(1)}, u32[]{:S(2)}, u32[]{:S(2)}) collective-permute-start(bf16[16,768]{1,0:T(8,128)(2,1)} %get-tuple-element.60), channel_id=1, source_target_pairs={{1,0},{17,16},{2,1},{18,17},{3,2},{19,18},{4,3},{20,19},{5,4},{21,... | collective-permute-start | bytes 73736 | tf_op jit(solution)/shard_map/ppermute | solution.py:326
  69.4 12.0 %collective-permute-start.24 = (bf16[24,3072]{1,0:T(8,128)(2,1)S(1)}, bf16[24,3072]{1,0:T(8,128)(2,1)S(1)}, u32[]{:S(2)}, u32[]{:S(2)}) collective-permute-start(bf16[24,3072]{1,0:T(8,128)(2,1)S(1)} %copy-done.19), channel_id=1, source_target_pairs={{0,4},{1,5},{2,6},{3,7},{4,0},{5,1},{6,2},{7,3},{8,12},{9,13},{10,... | collective-permute-start | bytes 442376 | tf_op jit(solution)/shard_map/ppermute | solution.py:30
  81.4 8.1 %collective-permute-start.1 = (bf16[2,24,1152]{2,1,0:T(8,128)(2,1)S(1)}, bf16[2,24,1152]{2,1,0:T(8,128)(2,1)S(1)}, u32[]{:S(2)}, u32[]{:S(2)}) collective-permute-start(bf16[2,24,1152]{2,1,0:T(8,128)(2,1)S(1)} %maximum_select_fusion.29), channel_id=1, source_target_pairs={{0,8},{1,9},{2,10},{3,11},{4,12},{5,13},{6,14},{7,15},{8,0},{9,1},... | collective-permute-start | bytes 331784 | tf_op jit(solution)/shard_map/ppermute | solution.py:30
  87.2 9.0 %collective-permute-start.15 = (bf16[2,24,1152]{2,1,0:T(8,128)(2,1)S(1)}, bf16[2,24,1152]{2,1,0:T(8,128)(2,1)S(1)}, u32[]{:S(2)}, u32[]{:S(2)}) collective-permute-start(bf16[2,24,1152]{2,1,0:T(8,128)(2,1)S(1)} %maximum_select_fusion.31), channel_id=1, source_target_pairs={{0,8},{1,9},{2,10},{3,11},{4,12},{5,13},{6,14},{7,15},{8,0},{9,1},... | collective-permute-start | bytes 331784 | tf_op jit(solution)/shard_map/ppermute | solution.py:30
  96.2 15.4 %collective-permute-start.25 = (bf16[2,24,3072]{2,1,0:T(8,128)(2,1)S(1)}, bf16[2,24,3072]{2,1,0:T(8,128)(2,1)S(1)}, u32[]{:S(2)}, u32[]{:S(2)}) collective-permute-start(bf16[2,24,3072]{2,1,0:T(8,128)(2,1)S(1)} %maximum_select_fusion.21), channel_id=1, source_target_pairs={{0,8},{1,9},{2,10},{3,11},{4,12},{5,13},{6,14},{7,15},{8,0},{9,1},... | collective-permute-start | bytes 884744 | tf_op jit(solution)/shard_map/ppermute | solution.py:30
  108.3 10.0 %collective-permute-start.30 = (bf16[2,96,768]{2,1,0:T(8,128)(2,1)S(1)}, bf16[2,96,768]{2,1,0:T(8,128)(2,1)S(1)}, u32[]{:S(2)}, u32[]{:S(2)}) collective-permute-start(bf16[2,96,768]{2,1,0:T(8,128)(2,1)S(1)} %maximum_select_fusion.23), channel_id=1, source_target_pairs={{0,8},{1,9},{2,10},{3,11},{4,12},{5,13},{6,14},{7,15},{8,0},{9,1},... | collective-permute-start | bytes 884744 | tf_op jit(solution)/shard_map/ppermute | solution.py:30
  111.6 8.1 %collective-permute-start.22 = (bf16[2,2,2,24,768]{4,3,2,1,0:T(8,128)(2,1)S(1)}, bf16[2,2,2,24,768]{4,3,2,1,0:T(8,128)(2,1)S(1)}, u32[]{:S(2)}, u32[]{:S(2)}) collective-permute-start(bf16[2,2,2,24,768]{4,3,2,1,0:T(8,128)(2,1)S(1)} %maximum_select_fusion.19), channel_id=1, source_target_pairs={{0,16},{1,17},{2,18},{3,19},{4,20},{5,21},{6,22},{7,23},{8,24},{9,... | collective-permute-start | bytes 884744 | tf_op jit(solution)/shard_map/ppermute | solution.py:30
  118.3 13.1 %collective-permute-start.3 = (bf16[2,2,2,24,1152]{4,3,2,1,0:T(8,128)(2,1)S(1)}, bf16[2,2,2,24,1152]{4,3,2,1,0:T(8,128)(2,1)S(1)}, u32[]{:S(2)}, u32[]{:S(2)}) collective-permute-start(bf16[2,2,2,24,1152]{4,3,2,1,0:T(8,128)(2,1)S(1)} %maximum_select_fusion.16), channel_id=1, source_target_pairs={{0,16},{1,17},{2,18},{3,19},{4,20},{5,21},{6,22},{7,23},{8,24},{9,... | collective-permute-start | bytes 1327112 | tf_op jit(solution)/shard_map/ppermute | solution.py:30
  119.7 13.4 %collective-permute-start.17 = (bf16[2,2,2,24,1152]{4,3,2,1,0:T(8,128)(2,1)S(1)}, bf16[2,2,2,24,1152]{4,3,2,1,0:T(8,128)(2,1)S(1)}, u32[]{:S(2)}, u32[]{:S(2)}) collective-permute-start(bf16[2,2,2,24,1152]{4,3,2,1,0:T(8,128)(2,1)S(1)} %maximum_select_fusion.18), channel_id=1, source_target_pairs={{0,2},{1,3},{2,0},{3,1},{4,6},{5,7},{6,4},{7,5},{8,10},{9,11},{10,... | collective-permute-start | bytes 1327112 | tf_op jit(solution)/shard_map/ppermute | solution.py:30
  122.2 20.6 %collective-permute-start.26 = (bf16[2,2,24,3072]{3,2,1,0:T(8,128)(2,1)S(1)}, bf16[2,2,24,3072]{3,2,1,0:T(8,128)(2,1)S(1)}, u32[]{:S(2)}, u32[]{:S(2)}) collective-permute-start(bf16[2,2,24,3072]{3,2,1,0:T(8,128)(2,1)S(1)} %maximum_select_fusion.13), channel_id=1, source_target_pairs={{0,2},{1,3},{2,0},{3,1},{4,6},{5,7},{6,4},{7,5},{8,10},{9,11},{10,... | collective-permute-start | bytes 1769480 | tf_op jit(solution)/shard_map/ppermute | solution.py:30
  122.4 18.1 %collective-permute-start.31 = (bf16[2,2,96,768]{3,2,1,0:T(8,128)(2,1)S(1)}, bf16[2,2,96,768]{3,2,1,0:T(8,128)(2,1)S(1)}, u32[]{:S(2)}, u32[]{:S(2)}) collective-permute-start(bf16[2,2,96,768]{3,2,1,0:T(8,128)(2,1)S(1)} %maximum_select_fusion.15), channel_id=1, source_target_pairs={{0,16},{1,17},{2,18},{3,19},{4,20},{5,21},{6,22},{7,23},{8,24},{9,... | collective-permute-start | bytes 1769480 | tf_op jit(solution)/shard_map/ppermute | solution.py:30
  123.4 23.7 %collective-permute-start.23 = (bf16[2,2,2,2,24,768]{5,4,3,2,1,0:T(8,128)(2,1)S(1)}, bf16[2,2,2,2,24,768]{5,4,3,2,1,0:T(8,128)(2,1)S(1)}, u32[]{:S(2)}, u32[]{:S(2)}) collective-permute-start(bf16[2,2,2,2,24,768]{5,4,3,2,1,0:T(8,128)(2,1)S(1)} %maximum_select_fusion.12), channel_id=1, source_target_pairs={{0,1},{1,0},{2,3},{3,2},{4,5},{5,4},{6,7},{7,6},{8,9},{9,8},{10,11... | collective-permute-start | bytes 1769480 | tf_op jit(solution)/shard_map/ppermute | solution.py:30
  131.6 20.2 %collective-permute-start.4 = (bf16[2,2,2,2,24,1152]{5,4,3,2,1,0:T(8,128)(2,1)S(1)}, bf16[2,2,2,2,24,1152]{5,4,3,2,1,0:T(8,128)(2,1)S(1)}, u32[]{:S(2)}, u32[]{:S(2)}) collective-permute-start(bf16[2,2,2,2,24,1152]{5,4,3,2,1,0:T(8,128)(2,1)S(1)} %maximum_select_fusion.9), channel_id=1, source_target_pairs={{0,1},{1,0},{2,3},{3,2},{4,5},{5,4},{6,7},{7,6},{8,9},{9,8},{10,11... | collective-permute-start | bytes 2654216 | tf_op jit(solution)/shard_map/ppermute | solution.py:30
  133.2 13.9 %collective-permute-start.18 = (bf16[2,2,2,2,24,1152]{5,4,2,1,0,3:T(8,128)(2,1)S(1)}, bf16[2,2,2,2,24,1152]{5,4,2,1,0,3:T(8,128)(2,1)S(1)}, u32[]{:S(2)}, u32[]{:S(2)}) collective-permute-start(bf16[2,2,2,2,24,1152]{5,4,2,1,0,3:T(8,128)(2,1)S(1)} %maximum_select_fusion.11), channel_id=1, source_target_pairs={{0,1},{1,0},{2,3},{3,2},{4,5},{5,4},{6,7},{7,6},{8,9},{9,8},{10,11... | collective-permute-start | bytes 2654216 | tf_op jit(solution)/shard_map/ppermute | solution.py:30
  142.9 25.1 %collective-permute-start.27 = (bf16[2,2,2,24,3072]{4,3,2,1,0:T(8,128)(2,1)S(1)}, bf16[2,2,2,24,3072]{4,3,2,1,0:T(8,128)(2,1)S(1)}, u32[]{:S(2)}, u32[]{:S(2)}) collective-permute-start(bf16[2,2,2,24,3072]{4,3,2,1,0:T(8,128)(2,1)S(1)} %maximum_select_fusion.7), channel_id=1, source_target_pairs={{0,16},{1,17},{2,18},{3,19},{4,20},{5,21},{6,22},{7,23},{8,24},{9,... | collective-permute-start | bytes 3538952 | tf_op jit(solution)/shard_map/ppermute | solution.py:30
  144.9 47.4 %collective-permute-start.32 = (bf16[2,2,2,96,768]{4,3,2,1,0:T(8,128)(2,1)}, bf16[2,2,2,96,768]{4,3,2,1,0:T(8,128)(2,1)S(1)}, u32[]{:S(2)}, u32[]{:S(2)}) collective-permute-start(bf16[2,2,2,96,768]{4,3,2,1,0:T(8,128)(2,1)} %maximum_select_fusion.8), channel_id=1, source_target_pairs={{0,2},{1,3},{2,0},{3,1},{4,6},{5,7},{6,4},{7,5},{8,10},{9,11},{10,... | collective-permute-start | bytes 3538952 | tf_op jit(solution)/shard_map/ppermute | solution.py:30
  169.9 30.9 %collective-permute-start.28 = (bf16[2,2,2,2,24,3072]{5,4,3,2,1,0:T(8,128)(2,1)}, bf16[2,2,2,2,24,3072]{5,4,3,2,1,0:T(8,128)(2,1)}, u32[]{:S(2)}, u32[]{:S(2)}) collective-permute-start(bf16[2,2,2,2,24,3072]{5,4,3,2,1,0:T(8,128)(2,1)} %maximum_select_fusion.2), channel_id=1, source_target_pairs={{0,1},{1,0},{2,3},{3,2},{4,5},{5,4},{6,7},{7,6},{8,9},{9,8},{10,11... | collective-permute-start | bytes 7077896 | tf_op jit(solution)/shard_map/ppermute | solution.py:30
  192.6 11.2 %collective-permute-start.33 = (bf16[2,2,2,2,96,768]{5,4,3,2,1,0:T(8,128)(2,1)S(1)}, bf16[2,2,2,2,96,768]{5,4,3,2,1,0:T(8,128)(2,1)S(1)}, u32[]{:S(2)}, u32[]{:S(2)}) collective-permute-start(bf16[2,2,2,2,96,768]{5,4,3,2,1,0:T(8,128)(2,1)S(1)} %maximum_select_fusion.3), channel_id=1, source_target_pairs={{0,1},{1,0},{2,3},{3,2},{4,5},{5,4},{6,7},{7,6},{8,9},{9,8},{10,11... | collective-permute-start | bytes 7077896 | tf_op jit(solution)/shard_map/ppermute | solution.py:30
  290.6 31.0 %collective-permute-start.63 = (f32[2,2,2,2,384]{4,3,2,1,0:T(2,128)S(1)}, f32[2,2,2,2,384]{4,3,2,1,0:T(2,128)S(1)}, u32[]{:S(2)}, u32[]{:S(2)}) collective-permute-start(f32[2,2,2,2,384]{4,3,2,1,0:T(2,128)S(1)} %bitcast.467), channel_id=1, source_target_pairs={{0,1},{1,0},{2,3},{3,2},{4,5},{5,4},{6,7},{7,6},{8,9},{9,8},{10,11... | collective-permute-start | bytes 73736 | tf_op jit(solution)/shard_map/ppermute | solution.py:30
  321.6 105.6 %collective-permute-start.58 = (bf16[2,2,2,2,96,768]{5,4,2,1,0,3:T(8,128)(2,1)}, bf16[2,2,2,2,96,768]{5,4,2,1,0,3:T(8,128)(2,1)}, u32[]{:S(2)}, u32[]{:S(2)}) collective-permute-start(bf16[2,2,2,2,96,768]{5,4,2,1,0,3:T(8,128)(2,1)} %bitcast.370), channel_id=1, source_target_pairs={{0,1},{1,0},{2,3},{3,2},{4,5},{5,4},{6,7},{7,6},{8,9},{9,8},{10,11... | collective-permute-start | bytes 7077896 | tf_op jit(solution)/shard_map/ppermute | solution.py:30
  324.3 39.9 %collective-permute-start.48 = (bf16[2,2,2,2,24,768]{5,4,2,1,0,3:T(8,128)(2,1)}, bf16[2,2,2,2,24,768]{5,4,2,1,0,3:T(8,128)(2,1)}, u32[]{:S(2)}, u32[]{:S(2)}) collective-permute-start(bf16[2,2,2,2,24,768]{5,4,2,1,0,3:T(8,128)(2,1)} %bitcast.373), channel_id=1, source_target_pairs={{0,1},{1,0},{2,3},{3,2},{4,5},{5,4},{6,7},{7,6},{8,9},{9,8},{10,11... | collective-permute-start | bytes 1769480 | tf_op jit(solution)/shard_map/ppermute | solution.py:30
  327.0 22.9 %collective-permute-start.65 = (f32[2,2,384]{2,1,0:T(2,128)S(1)}, f32[2,2,384]{2,1,0:T(2,128)S(1)}, u32[]{:S(2)}, u32[]{:S(2)}) collective-permute-start(f32[2,2,384]{2,1,0:T(2,128)S(1)} %bitcast.476), channel_id=1, source_target_pairs={{0,2},{1,3},{2,0},{3,1},{4,6},{5,7},{6,4},{7,5},{8,10},{9,11},{10,... | collective-permute-start | bytes 18440 | tf_op jit(solution)/shard_map/ppermute | solution.py:30
  341.1 27.9 %collective-permute-start.34 = (bf16[512,768]{1,0:T(8,128)(2,1)}, bf16[512,768]{1,0:T(8,128)(2,1)}, u32[]{:S(2)}, u32[]{:S(2)}) collective-permute-start(bf16[512,768]{1,0:T(8,128)(2,1)} %get-tuple-element.47), channel_id=1, source_target_pairs={{16,0},{1,16},{17,1},{2,17},{18,2},{3,18},{19,3},{4,19},{20,4},{5,... | collective-permute-start | bytes 2359304 | tf_op jit(solution)/shard_map/ppermute | solution.py:326
  342.4 29.4 %collective-permute-start.35 = (bf16[512,768]{1,0:T(8,128)(2,1)}, bf16[512,768]{1,0:T(8,128)(2,1)}, u32[]{:S(2)}, u32[]{:S(2)}) collective-permute-start(bf16[512,768]{1,0:T(8,128)(2,1)} %get-tuple-element.48), channel_id=1, source_target_pairs={{0,16},{16,1},{1,17},{17,2},{2,18},{18,3},{3,19},{19,4},{4,20},{20... | collective-permute-start | bytes 2359304 | tf_op jit(solution)/shard_map/ppermute | solution.py:326
  368.4 62.5 %collective-permute-start.53 = (bf16[2,2,2,2,24,3072]{5,4,2,1,3,0:T(8,128)(2,1)}, bf16[2,2,2,2,24,3072]{5,4,2,1,3,0:T(8,128)(2,1)}, u32[]{:S(2)}, u32[]{:S(2)}) collective-permute-start(bf16[2,2,2,2,24,3072]{5,4,2,1,3,0:T(8,128)(2,1)} %bitcast.371), channel_id=1, source_target_pairs={{0,1},{1,0},{2,3},{3,2},{4,5},{5,4},{6,7},{7,6},{8,9},{9,8},{10,11... | collective-permute-start | bytes 7077896 | tf_op jit(solution)/shard_map/ppermute | solution.py:30
  368.5 21.7 %collective-permute-start.38 = (bf16[2,2,2,2,24,1152]{5,4,3,2,1,0:T(8,128)(2,1)}, bf16[2,2,2,2,24,1152]{5,4,3,2,1,0:T(8,128)(2,1)}, u32[]{:S(2)}, u32[]{:S(2)}) collective-permute-start(bf16[2,2,2,2,24,1152]{5,4,3,2,1,0:T(8,128)(2,1)} %dynamic-slice_bitcast_fusion.2), channel_id=1, source_target_pairs={{0,1},{1,0},{2,3},{3,2},{4,5},{5,4},{6,7},{7,6},{8,9},{9,8},{10,11... | collective-permute-start | bytes 2654216 | tf_op jit(solution)/shard_map/ppermute | solution.py:30
  369.0 25.6 %collective-permute-start.43 = (bf16[2,2,2,2,24,1152]{5,4,2,1,0,3:T(8,128)(2,1)}, bf16[2,2,2,2,24,1152]{5,4,2,1,0,3:T(8,128)(2,1)}, u32[]{:S(2)}, u32[]{:S(2)}) collective-permute-start(bf16[2,2,2,2,24,1152]{5,4,2,1,0,3:T(8,128)(2,1)} %bitcast.372), channel_id=1, source_target_pairs={{0,1},{1,0},{2,3},{3,2},{4,5},{5,4},{6,7},{7,6},{8,9},{9,8},{10,11... | collective-permute-start | bytes 2654216 | tf_op jit(solution)/shard_map/ppermute | solution.py:30
  371.9 16.6 %collective-permute-start.49 = (bf16[2,2,2,24,768]{4,3,2,1,0:T(8,128)(2,1)S(1)}, bf16[2,2,2,24,768]{4,3,2,1,0:T(8,128)(2,1)S(1)}, u32[]{:S(2)}, u32[]{:S(2)}) collective-permute-start(bf16[2,2,2,24,768]{4,3,2,1,0:T(8,128)(2,1)S(1)} %dynamic-slice_bitcast_fusion.9), channel_id=1, source_target_pairs={{0,2},{1,3},{2,0},{3,1},{4,6},{5,7},{6,4},{7,5},{8,10},{9,11},{10,... | collective-permute-start | bytes 884744 | tf_op jit(solution)/shard_map/ppermute | solution.py:30
  391.7 12.9 %collective-permute-start.39 = (bf16[2,2,2,24,1152]{4,3,2,1,0:T(8,128)(2,1)S(1)}, bf16[2,2,2,24,1152]{4,3,2,1,0:T(8,128)(2,1)S(1)}, u32[]{:S(2)}, u32[]{:S(2)}) collective-permute-start(bf16[2,2,2,24,1152]{4,3,2,1,0:T(8,128)(2,1)S(1)} %dynamic-slice_bitcast_fusion.6), channel_id=1, source_target_pairs={{0,16},{1,17},{2,18},{3,19},{4,20},{5,21},{6,22},{7,23},{8,24},{9,... | collective-permute-start | bytes 1327112 | tf_op jit(solution)/shard_map/ppermute | solution.py:30
  400.1 12.7 %collective-permute-start.44 = (bf16[2,2,2,24,1152]{4,3,2,1,0:T(8,128)(2,1)S(1)}, bf16[2,2,2,24,1152]{4,3,2,1,0:T(8,128)(2,1)S(1)}, u32[]{:S(2)}, u32[]{:S(2)}) collective-permute-start(bf16[2,2,2,24,1152]{4,3,2,1,0:T(8,128)(2,1)S(1)} %dynamic-slice_bitcast_fusion.5), channel_id=1, source_target_pairs={{0,2},{1,3},{2,0},{3,1},{4,6},{5,7},{6,4},{7,5},{8,10},{9,11},{10,... | collective-permute-start | bytes 1327112 | tf_op jit(solution)/shard_map/ppermute | solution.py:30
  404.8 10.4 %collective-permute-start.40 = (bf16[2,2,24,1152]{3,2,1,0:T(8,128)(2,1)S(1)}, bf16[2,2,24,1152]{3,2,1,0:T(8,128)(2,1)S(1)}, u32[]{:S(2)}, u32[]{:S(2)}) collective-permute-start(bf16[2,2,24,1152]{3,2,1,0:T(8,128)(2,1)S(1)} %dynamic-slice_bitcast_fusion.11), channel_id=1, source_target_pairs={{0,2},{1,3},{2,0},{3,1},{4,6},{5,7},{6,4},{7,5},{8,10},{9,11},{10,... | collective-permute-start | bytes 663560 | tf_op jit(solution)/shard_map/ppermute | solution.py:30
  415.3 8.1 %collective-permute-start.41 = (bf16[2,24,1152]{2,1,0:T(8,128)(2,1)S(1)}, bf16[2,24,1152]{2,1,0:T(8,128)(2,1)S(1)}, u32[]{:S(2)}, u32[]{:S(2)}) collective-permute-start(bf16[2,24,1152]{2,1,0:T(8,128)(2,1)S(1)} %dynamic-slice_bitcast_fusion.16), channel_id=1, source_target_pairs={{0,8},{1,9},{2,10},{3,11},{4,12},{5,13},{6,14},{7,15},{8,0},{9,1},... | collective-permute-start | bytes 331784 | tf_op jit(solution)/shard_map/ppermute | solution.py:30
  423.4 12.5 %collective-permute-start.42 = (bf16[24,1152]{1,0:T(8,128)(2,1)S(1)}, bf16[24,1152]{1,0:T(8,128)(2,1)S(1)}, u32[]{:S(2)}, u32[]{:S(2)}) collective-permute-start(bf16[24,1152]{1,0:T(8,128)(2,1)S(1)} %dynamic-slice_bitcast_fusion.19), channel_id=1, source_target_pairs={{0,4},{1,5},{2,6},{3,7},{4,0},{5,1},{6,2},{7,3},{8,12},{9,13},{10,... | collective-permute-start | bytes 165896 | tf_op jit(solution)/shard_map/ppermute | solution.py:30
  424.9 11.0 %collective-permute-start.47 = (bf16[24,1152]{1,0:T(8,128)(2,1)S(1)}, bf16[24,1152]{1,0:T(8,128)(2,1)S(1)}, u32[]{:S(2)}, u32[]{:S(2)}) collective-permute-start(bf16[24,1152]{1,0:T(8,128)(2,1)S(1)} %dynamic-slice_bitcast_fusion.18), channel_id=1, source_target_pairs={{0,4},{1,5},{2,6},{3,7},{4,0},{5,1},{6,2},{7,3},{8,12},{9,13},{10,... | collective-permute-start | bytes 165896 | tf_op jit(solution)/shard_map/ppermute | solution.py:30
  429.7 26.4 %collective-permute-start.59 = (bf16[2,2,2,96,768]{4,3,2,1,0:T(8,128)(2,1)S(1)}, bf16[2,2,2,96,768]{4,3,2,1,0:T(8,128)(2,1)S(1)}, u32[]{:S(2)}, u32[]{:S(2)}) collective-permute-start(bf16[2,2,2,96,768]{4,3,2,1,0:T(8,128)(2,1)S(1)} %dynamic-slice_bitcast_fusion), channel_id=1, source_target_pairs={{0,2},{1,3},{2,0},{3,1},{4,6},{5,7},{6,4},{7,5},{8,10},{9,11},{10,... | collective-permute-start | bytes 3538952 | tf_op jit(solution)/shard_map/ppermute | solution.py:30
  433.9 29.0 %collective-permute-start.54 = (bf16[2,2,2,24,3072]{4,3,1,0,2:T(8,128)(2,1)S(1)}, bf16[2,2,2,24,3072]{4,3,1,0,2:T(8,128)(2,1)S(1)}, u32[]{:S(2)}, u32[]{:S(2)}) collective-permute-start(bf16[2,2,2,24,3072]{4,3,1,0,2:T(8,128)(2,1)S(1)} %dynamic-slice_bitcast_fusion.1), channel_id=1, source_target_pairs={{0,16},{1,17},{2,18},{3,19},{4,20},{5,21},{6,22},{7,23},{8,24},{9,... | collective-permute-start | bytes 3538952 | tf_op jit(solution)/shard_map/ppermute | solution.py:30
  456.4 16.5 %collective-permute-start.60 = (bf16[2,2,96,768]{3,2,1,0:T(8,128)(2,1)S(1)}, bf16[2,2,96,768]{3,2,1,0:T(8,128)(2,1)S(1)}, u32[]{:S(2)}, u32[]{:S(2)}) collective-permute-start(bf16[2,2,96,768]{3,2,1,0:T(8,128)(2,1)S(1)} %dynamic-slice_bitcast_fusion.3), channel_id=1, source_target_pairs={{0,16},{1,17},{2,18},{3,19},{4,20},{5,21},{6,22},{7,23},{8,24},{9,... | collective-permute-start | bytes 1769480 | tf_op jit(solution)/shard_map/ppermute | solution.py:30
  463.3 13.2 %collective-permute-start.55 = (bf16[2,2,24,3072]{3,2,1,0:T(8,128)(2,1)S(1)}, bf16[2,2,24,3072]{3,2,1,0:T(8,128)(2,1)S(1)}, u32[]{:S(2)}, u32[]{:S(2)}) collective-permute-start(bf16[2,2,24,3072]{3,2,1,0:T(8,128)(2,1)S(1)} %dynamic-slice_bitcast_fusion.4), channel_id=1, source_target_pairs={{0,2},{1,3},{2,0},{3,1},{4,6},{5,7},{6,4},{7,5},{8,10},{9,11},{10,... | collective-permute-start | bytes 1769480 | tf_op jit(solution)/shard_map/ppermute | solution.py:30
  473.1 21.9 %collective-permute-start.61 = (bf16[2,96,768]{2,1,0:T(8,128)(2,1)S(1)}, bf16[2,96,768]{2,1,0:T(8,128)(2,1)S(1)}, u32[]{:S(2)}, u32[]{:S(2)}) collective-permute-start(bf16[2,96,768]{2,1,0:T(8,128)(2,1)S(1)} %dynamic-slice_bitcast_fusion.7), channel_id=1, source_target_pairs={{0,8},{1,9},{2,10},{3,11},{4,12},{5,13},{6,14},{7,15},{8,0},{9,1},... | collective-permute-start | bytes 884744 | tf_op jit(solution)/shard_map/ppermute | solution.py:30
  476.7 24.5 %collective-permute-start.56 = (bf16[2,24,3072]{2,1,0:T(8,128)(2,1)S(1)}, bf16[2,24,3072]{2,1,0:T(8,128)(2,1)S(1)}, u32[]{:S(2)}, u32[]{:S(2)}) collective-permute-start(bf16[2,24,3072]{2,1,0:T(8,128)(2,1)S(1)} %dynamic-slice_bitcast_fusion.8), channel_id=1, source_target_pairs={{0,8},{1,9},{2,10},{3,11},{4,12},{5,13},{6,14},{7,15},{8,0},{9,1},... | collective-permute-start | bytes 884744 | tf_op jit(solution)/shard_map/ppermute | solution.py:30
  495.1 9.3 %collective-permute-start.62 = (bf16[96,768]{1,0:T(8,128)(2,1)S(1)}, bf16[96,768]{1,0:T(8,128)(2,1)S(1)}, u32[]{:S(2)}, u32[]{:S(2)}) collective-permute-start(bf16[96,768]{1,0:T(8,128)(2,1)S(1)} %dynamic-slice_bitcast_fusion.12), channel_id=1, source_target_pairs={{0,4},{1,5},{2,6},{3,7},{4,0},{5,1},{6,2},{7,3},{8,12},{9,13},{10,... | collective-permute-start | bytes 442376 | tf_op jit(solution)/shard_map/ppermute | solution.py:30
  (66 other events, 1287.5 us)

commit v2 on v1

--- a/solution.py
+++ b/solution.py
@@ -30,19 +30,22 @@
     return lax.ppermute(block, AXES, [(i, i ^ bit) for i in range(count)])
 
 
-def gathered(shard, order, count, me):
-    held, have = shard, []
-    for bit in order:
-        axis = sum(b > bit for b in have)
-        have.append(bit)
-        other = jnp.expand_dims(swap(held, bit, count), axis)
-        own = jnp.expand_dims(held, axis)
-        held = jnp.where(
-            (me & bit) == 0,
-            jnp.concatenate([own, other], axis=axis),
-            jnp.concatenate([other, own], axis=axis),
-        )
-    return held.reshape((count * shard.shape[0],) + shard.shape[1:])
+def after(value, *others):
+    return lax.optimization_barrier((value, *others))[0]
+
+
+def merge(held, have, other, bit, me):
+    axis = sum(b > bit for b in have)
+    other, own = jnp.expand_dims(other, axis), jnp.expand_dims(held, axis)
+    return jnp.where(
+        (me & bit) == 0,
+        jnp.concatenate([own, other], axis=axis),
+        jnp.concatenate([other, own], axis=axis),
+    )
+
+
+def flat(held, rows, count):
+    return held.reshape((count * rows,) + held.shape[-1:])
 
 
 def reduced(blocks, order, count, me):
@@ -57,6 +60,20 @@
         total = keep.astype(f32) + swap(send, bit, count).astype(f32)
         held = total if not have else total.astype(blocks.dtype)
     return held
+
+
+def relative(bits):
+    return [sum(bit for at, bit in enumerate(bits) if j >> at & 1) for j in range(1 << len(bits))]
+
+
+def halved(keep, send, order, count):
+    total = keep.astype(f32)
+    for bit in order:
+        total = total + swap(send, bit, count).astype(f32)
+        half = total.shape[0] // 2
+        send, total = total[half:].astype(bf16), total[: max(half, 1)]
+        send = yield send
+    yield total[0]
 
 
 def segment_at(lengths_ref, sequences, position):
@@ -272,18 +289,203 @@
     )(lengths, first, queries, keys, values, grads, stats)
 
 
+TN = (((0,), (0,)), ((), ()))
+
+
+def row_mean(value):
+    return jnp.mean(value, axis=-1, keepdims=True)
+
+
+def column_sum(value):
+    return jnp.sum(value, axis=0, keepdims=True)
+
+
 def normalize(summed):
-    row_mean = jnp.mean(summed, axis=-1, keepdims=True)
-    centered = summed - row_mean
-    variance = jnp.mean(centered * centered, axis=-1, keepdims=True)
-    inverse_std = lax.rsqrt(variance + norm_eps)
-    return (centered * inverse_std, inverse_std)
-
-
-def normalize_back(grad_normed, normed, inverse_std):
-    grad_mean = jnp.mean(grad_normed, axis=-1, keepdims=True)
-    cross_mean = jnp.mean(grad_normed * normed, axis=-1, keepdims=True)
-    return inverse_std * (grad_normed - grad_mean - normed * cross_mean)
+    centered = summed - row_mean(summed)
+    inverse_std = lax.rsqrt(row_mean(centered * centered) + norm_eps)
+    return centered * inverse_std, inverse_std
+
+
+def normalize_back(grad, normed, inverse_std):
+    return inverse_std * (grad - row_mean(grad) - normed * row_mean(grad * normed))
+
+
+def feed_kernel(plan, *refs):
+    held, in_dest, out_slot, shard, deep, thin_first = plan
+    me_ref, att_ref, states_ref, cot_ref, vec_ref, upb_ref = refs[:6]
+    mixed_in, down_in = refs[6 : 6 + held], refs[6 + held : 6 + 2 * held]
+    at = 6 + 2 * held
+    result_ref, res_ref, gatt_ref, small_ref = refs[at : at + 4]
+    mixed_out, down_out = refs[at + 4 : at + 4 + held], refs[at + 4 + held : at + 4 + 2 * held]
+    at += 4 + 2 * held
+    (wslot, wmix, wdown, act, slope, gmix, gdown, acc, in_sem, out_sem) = refs[at:]
+    me = me_ref[0]
+    width = states_ref.shape[1]
+    hidden = wdown.shape[0]
+    slots = len(in_dest[0][0])
+
+    def copies_in():
+        for a in range(held):
+            for j in range(slots):
+                dest = in_dest[0][a][j] ^ me
+                yield pltpu.make_async_copy(
+                    mixed_in[a].at[j], wslot.at[dest], in_sem.at[0, a * slots + j]
+                )
+
+    def copies_down():
+        for a in range(held):
+            for j in range(slots):
+                dest = pl.multiple_of((in_dest[1][a][j] ^ me) * deep, 16)
+                yield pltpu.make_async_copy(
+                    down_in[a].at[j], wdown.at[pl.ds(dest, deep), :], in_sem.at[1, a * slots + j]
+                )
+
+    for copy in copies_in():
+        copy.start()
+    for copy in copies_down():
+        copy.start()
+    for copy in copies_in():
+        copy.wait()
+    total = held * slots
+    step = min(total, 8)
+    for d in range(0, total, step):
+        block = wslot[d : d + step].astype(f32).reshape(step * shard, wslot.shape[2])
+        wmix[d * shard : (d + step) * shard, :] = block.astype(bf16)
+
+    bias_out, bias_down, gain_one, shift_one, gain_two, shift_two = (
+        vec_ref[i : i + 1, :] for i in range(6)
+    )
+    branch = mul(att_ref[...], wmix[:, :width]) + bias_out
+    normed_one, scale_one = normalize(states_ref[...].astype(f32) + branch)
+    first_norm = normed_one * gain_one + shift_one
+    inner = first_norm.astype(bf16)
+    for copy in copies_down():
+        copy.wait()
+    chunks = range(0, hidden, width)
+    for c in chunks:
+        lifted = mul(inner, wmix[:, width + c : 2 * width + c]) + upb_ref[:, c : c + width]
+        phi_sum = 0.5 * (1.0 + lax.erf(lifted * root_half))
+        active = (lifted * phi_sum).astype(bf16)
+        act[:, c : c + width] = active
+        slope[:, c : c + width] = phi_sum + lifted * (
+            inverse_root_two_pi * jnp.exp(-0.5 * lifted * lifted)
+        )
+        part = mul(active, wdown[c : c + width, :])
+        acc[...] = part if c == 0 else acc[...] + part
+    normed_two, scale_two = normalize(first_norm + (acc[...] + bias_down))
+    result_ref[...] = (normed_two * gain_two + shift_two).astype(bf16)
+
+    cot = cot_ref[...].astype(f32)
+    small_ref[4:5, :] = column_sum(cot * normed_two)
+    small_ref[5:6, :] = column_sum(cot)
+    grad_mid = normalize_back(cot * gain_two, normed_two, scale_two)
+    grad_down = grad_mid.astype(bf16)
+    small_ref[1:2, :] = column_sum(grad_down.astype(f32))
+
+    def put(target, order, value, first, per):
+        for i in range(value.shape[0] // per):
+            rows = value[i * per : (i + 1) * per]
+            yield out_slot(order, (first + i) ^ me if total > 1 else 0), rows
+
+    def copies_out(order, source, targets, sem):
+        for a in range(held):
+            yield pltpu.make_async_copy(
+                source.at[pl.ds(a * slots, slots)], targets[a], out_sem.at[sem, a]
+            )
+
+    inner_t = inner.T
+    for c in chunks:
+        active = act[:, c : c + width]
+        grad_active = mul(grad_down, wdown[c : c + width, :], NT)
+        grad_lift = (grad_active * slope[:, c : c + width]).astype(bf16)
+        small_ref[8 + c // width : 9 + c // width, :] = column_sum(grad_lift.astype(f32))
+        grad_w = mul(active, grad_down, TN).astype(bf16)
+        for slot, rows in put(gdown, 1, grad_w, c // deep, min(deep, width)):
+            if total > 1:
+                gdown[slot] = rows
+            else:
+                gdown[slot, c : c + width, :] = rows
+        grad_w = mul(inner_t, grad_lift)
+        for slot, rows in put(gmix, 0, grad_w, 0, shard):
+            gmix[slot, :, width + c : 2 * width + c] = rows.astype(bf16)
+        part = mul(grad_lift, wmix[:, width + c : 2 * width + c], NT)
+        acc[...] = part if c == 0 else acc[...] + part
+    for copy in copies_out(1, gdown, down_out, 1):
+        copy.start()
+    grad_first = acc[...] + grad_mid
+    small_ref[2:3, :] = column_sum(grad_first * normed_one)
+    small_ref[3:4, :] = column_sum(grad_first)
+    grad_residual = normalize_back(grad_first * gain_one, normed_one, scale_one)
+    res_ref[...] = grad_residual
+    grad_branch = grad_residual.astype(bf16)
+    small_ref[0:1, :] = column_sum(grad_branch.astype(f32))
+    grad_w = mul(att_ref[...], grad_branch, TN)
+    for slot, rows in put(gmix, 0, grad_w, 0, shard):
+        gmix[slot, :, :width] = rows.astype(bf16)
+    for copy in copies_out(0, gmix, mixed_out, 0):
+        copy.start()
+    gatt_ref[...] = mul(grad_branch, wmix[:, :width], NT).astype(bf16)
+    small_ref[6:8, :] = jnp.zeros((2, width), f32)
+    small_ref[12:, :] = jnp.zeros((small_ref.shape[0] - 12, width), f32)
+    for copy in (*copies_out(1, gdown, down_out, 1), *copies_out(0, gmix, mixed_out, 0)):
+        copy.wait()
+
+
+def exchange_slot(bits):
+    def slot(diff):
+        found = jnp.int32(0)
+        for at, bit in enumerate(reversed(bits)):
+            found = found + (((diff & bit) != 0).astype(jnp.int32) << at)
+        return found
+
+    return slot
+
+
+def feed_forward(me, attended, states, cotangent, vectors, up_bias, mixed, down, orders, backs):
+    rows, width = states.shape
+    held, (slots, shard, columns) = len(mixed), mixed[0].shape
+    deep = down[0].shape[1]
+    hidden = held * slots * deep
+    if held > 1:
+        dest = [
+            [relative(order[:-1]), [r + order[-1] for r in relative(order[:-1])]]
+            for order in orders
+        ]
+    else:
+        dest = [[[0]], [[0]]]
+    slot_of = [exchange_slot(back) for back in backs]
+    plan = (held, dest, lambda order, diff: slot_of[order](diff) if held > 1 else 0, shard, deep, 0)
+    whole = pl.BlockSpec(memory_space=pltpu.VMEM)
+    anywhere = pl.BlockSpec(memory_space=pl.ANY)
+    shape = jax.ShapeDtypeStruct
+    total = held * slots
+    return pl.pallas_call(
+        functools.partial(feed_kernel, plan),
+        name="feed_forward",
+        out_shape=(
+            shape((rows, width), bf16),
+            shape((rows, width), f32),
+            shape((rows, width), bf16),
+            shape((16, width), f32),
+            *[shape((slots, shard, columns), bf16)] * held,
+            *[shape((slots, deep, width), bf16)] * held,
+        ),
+        in_specs=[pl.BlockSpec(memory_space=pltpu.SMEM), *[whole] * 5, *[anywhere] * (2 * held)],
+        out_specs=[*[whole] * 4, *[anywhere] * (2 * held)],
+        scratch_shapes=[
+            pltpu.VMEM((total, shard, columns), bf16),
+            pltpu.VMEM((total * shard, columns), bf16),
+            pltpu.VMEM((hidden, width), bf16),
+            pltpu.VMEM((rows, hidden), bf16),
+            pltpu.VMEM((rows, hidden), f32),
+            pltpu.VMEM((total, shard, columns), bf16),
+            pltpu.VMEM((total, deep, width), bf16),
+            pltpu.VMEM((rows, width), f32),
+            pltpu.SemaphoreType.DMA((2, total)),
+            pltpu.SemaphoreType.DMA((2, held)),
+        ],
+        compiler_params=pltpu.CompilerParams(vmem_limit_bytes=60 * 2**20),
+    )(me, attended, states, cotangent, vectors, up_bias, *mixed, *down)
 
 
 def local(
@@ -309,43 +511,48 @@
     heads_axis, blocks_axis = lax.axis_size("head"), lax.axis_size("blk")
     count = heads_axis * blocks_axis
     me = lax.axis_index(AXES)
-    place = lax.axis_index("blk") * heads_axis + lax.axis_index("head")
-    first = (place * rows).astype(jnp.int32).reshape(1)
+    head, blk = lax.axis_index("head"), lax.axis_index("blk")
+    first = ((blk * heads_axis + head) * rows).astype(jnp.int32).reshape(1)
     bits = [1 << b for b in range((count - 1).bit_length())]
-    far = [b for b in bits if b not in (1, 2, blocks_axis)]
-    order_a = tuple(far + [2, blocks_axis, 1])
-    order_b = tuple(far + [blocks_axis, 2, 1])
-    back_a = order_a[::-1]
-    back_b = order_b[::-1]
-
-    def shift(block, by):
-        index_of = lambda q: q % heads_axis * blocks_axis + q // heads_axis
+    far = [b for b in bits if b not in (1, 2, blocks_axis)][::-1]
+    order_a = tuple(far + [blocks_axis, 2, 1])
+    order_b = tuple(far + [2, blocks_axis, 1])
+    back_a, back_b = order_a[::-1], order_b[::-1]
+    shard = attention_weight.shape[0]
+    slotted = shard % 8 == 0
+    half = width // 2
+
+    def along(block, by_first, by_second):
         pairs = [
-            (index_of(q), index_of(q + by)) for q in range(count) if 0 <= q + by < count
+            (h * blocks_axis + b, h * blocks_axis + b + by)
+            for h, by in ((0, by_first), (1, by_second))
+            for b in range(blocks_axis)
+            if 0 <= b + by < blocks_axis
         ]
         return lax.ppermute(block, AXES, pairs)
 
     slot_index = owner_rows % rows
     pick = (slot_index[None, :] == jnp.arange(rows, dtype=jnp.int32)[:, None]).astype(bf16)
     states = jnp.dot(pick, hidden_states, preferred_element_type=f32).astype(bf16)
-    grad_result = jnp.dot(pick, output_cotangent, preferred_element_type=f32)
-
-    thin = -(-max(SEG_ROWS - 1 - rows, 0) // 16) * 16
-    near = min(rows, -(-(SEG_ROWS - 1) // 16) * 16)
-    side = near + thin
-    parts = [
-        shift(states[rows - near :], 1),
-        states,
-        shift(states[:near], -1),
-    ]
-    if thin:
-        parts = [shift(states[rows - thin :], 2), *parts, shift(states[:thin], -2)]
-    reach = jnp.concatenate(parts, axis=0)
-
-    half = 3 * width // 2
-    weight_a = gathered(attention_weight[:, :half], order_a, count, me)
-    weight_b = gathered(attention_weight[:, half:], order_b, count, me)
-    triple_weight = jnp.concatenate([weight_a, weight_b], axis=1)
+    cotangent = jnp.dot(pick, output_cotangent, preferred_element_type=f32).astype(bf16)
+
+    thin = -(-(SEG_ROWS - 1 - rows) // 16) * 16
+    side = rows + thin
+    partner = swap(states, blocks_axis, count)
+    is_first = head == 0
+    sent = jnp.where(
+        is_first,
+        jnp.concatenate([states[rows - thin :], partner], axis=0),
+        jnp.concatenate([partner, states[:thin]], axis=0),
+    )
+    outer = along(sent, 1, -1)
+    edge = along(jnp.where(is_first, states[:thin], states[rows - thin :]), -1, 1)
+    reach = jnp.where(
+        is_first,
+        jnp.concatenate([outer, states, partner, edge], axis=0),
+        jnp.concatenate([edge, partner, states, outer], axis=0),
+    )
+
     small = (
         query_bias,
         value_bias,
@@ -357,11 +564,47 @@
         second_shift,
         upward_bias,
     )
-    small_widths = [s.shape[0] for s in small]
+    small_widths = [v.shape[0] for v in small]
     small_ends = np.cumsum(small_widths)
-    packed = jnp.concatenate(small)
-    packed = jnp.pad(packed, (0, -packed.shape[0] % 128))
-    packed_all = gathered(packed[None], order_a, count, me).astype(f32)
+    packed = jnp.concatenate([v.reshape(shard, -1) for v in small], axis=1)
+    packed = jnp.pad(packed, ((0, 0), (0, -packed.shape[1] % 128)))
+    lead = [
+        jnp.concatenate([attention_weight[:, n * width + o :][:, :half] for n in range(3)], axis=1)
+        for o in (0, half)
+    ]
+    lead[0] = jnp.concatenate([lead[0], packed], axis=1)
+    lead_orders = (order_a, order_b)
+    follow = [jnp.concatenate([output_weight, upward_weight], axis=1), downward_weight]
+    follow_orders = (order_a, order_b)
+    if slotted:
+        follow = [block[None] for block in follow]
+    follow_parts = [[block] for block in follow]
+    for step in range(len(bits)):
+        lead_recv = [swap(b, o[step], count) for b, o in zip(lead, lead_orders)]
+        if slotted and step == len(bits) - 1:
+            lead = [
+                merge(b, o[:step], r, o[step], me)
+                for b, o, r in zip(lead, lead_orders, lead_recv)
+            ]
+            break
+        follow = [after(b, *lead_recv) for b in follow]
+        follow_recv = [swap(b, o[step], count) for b, o in zip(follow, follow_orders)]
+        lead = [
+            merge(b, o[:step], r, o[step], me) for b, o, r in zip(lead, lead_orders, lead_recv)
+        ]
+        if not slotted:
+            follow = [
+                merge(b, o[:step], r, o[step], me)
+                for b, o, r in zip(follow, follow_orders, follow_recv)
+            ]
+            follow_parts = [
+                [flat(b, rest.shape[0], 2 << step)[None]]
+                for b, rest in zip(follow, (output_weight, downward_weight))
+            ]
+        elif step < len(bits) - 1:
+            follow = [jnp.concatenate(pair, axis=0) for pair in zip(follow, follow_recv)]
+    weight_a, weight_b = (flat(b, shard, count) for b in lead[:2])
+    packed_all = weight_a[:, 3 * half :].astype(f32)
     (
         bias_query,
         bias_value,
@@ -373,127 +616,114 @@
         shift_two,
         bias_upward,
     ) = [
-        packed_all[:, end - n : end].reshape(count * n)
+        packed_all[:, (end - n) // shard : end // shard].reshape(count * n)
         for end, n in zip(small_ends, small_widths)
     ]
-    mixer_weight = gathered(output_weight, order_a, count, me)
-    upward_full = gathered(upward_weight, order_a, count, me)
-    downward_full = gathered(downward_weight, order_b, count, me)
+    columns = lambda n: jnp.concatenate(
+        [w[:, n * half : (n + 1) * half] for w in (weight_a, weight_b)], axis=1
+    )
+    weight_query, weight_key, weight_value = (columns(n) for n in range(3))
 
     queries = (
-        (jnp.dot(states, triple_weight[:, :width], preferred_element_type=f32) + bias_query)
-        .astype(bf16) * jnp.asarray(score_scale, bf16)
-    )
-    keys = jnp.dot(reach, triple_weight[:, width : 2 * width], preferred_element_type=f32).astype(bf16)
-    values = (
-        jnp.dot(reach, triple_weight[:, 2 * width :], preferred_element_type=f32) + bias_value
-    ).astype(bf16)
+        (jnp.dot(states, weight_query, preferred_element_type=f32) + bias_query).astype(bf16)
+        * jnp.asarray(score_scale, bf16)
+    )
+    keys = jnp.dot(reach, weight_key, preferred_element_type=f32).astype(bf16)
+    values = (jnp.dot(reach, weight_value, preferred_element_type=f32) + bias_value).astype(bf16)
     attended, stats = attention_forward(lengths, first, queries, keys, values, side)
-
-    branch = jnp.dot(attended, mixer_weight, preferred_element_type=f32) + bias_output
-    normed_one, scale_one = normalize(states.astype(f32) + branch)
-    first_norm = normed_one * gain_one + shift_one
-    inner_rows = first_norm.astype(bf16)
-    lifted = jnp.dot(inner_rows, upward_full, preferred_element_type=f32) + bias_upward
-    activated = jax.nn.gelu(lifted, approximate=False).astype(bf16)
-    branch_two = jnp.dot(activated, downward_full, preferred_element_type=f32) + bias_downward
-    normed_two, scale_two = normalize(first_norm + branch_two)
-    result = normed_two * gain_two + shift_two
-    layer_output = jnp.take(result.astype(bf16), slot_index, axis=0)
-
-    grad_second_gain = jnp.sum(grad_result * normed_two, axis=0)
-    grad_second_shift = jnp.sum(grad_result, axis=0)
-    grad_mid = normalize_back(grad_result * gain_two, normed_two, scale_two)
-    grad_down_rows = grad_mid.astype(bf16)
-    grad_downward_bias = jnp.sum(grad_down_rows.astype(f32), axis=0)
-    grad_downward_weight = jnp.einsum(
-        "rf,rd->fd", activated, grad_down_rows, preferred_element_type=f32
-    ).astype(bf16)
-    grad_activated = jnp.einsum(
-        "rd,fd->rf", grad_down_rows, downward_full, preferred_element_type=f32
-    )
-    gelu_slope = 0.5 * (1.0 + lax.erf(lifted * root_half)) + lifted * inverse_root_two_pi * jnp.exp(
-        -0.5 * lifted * lifted
-    )
-    grad_lifted = (grad_activated * gelu_slope).astype(bf16)
-    grad_upward_bias = jnp.sum(grad_lifted.astype(f32), axis=0)
-    grad_upward_weight = jnp.einsum(
-        "rd,rf->df", inner_rows, grad_lifted, preferred_element_type=f32
-    ).astype(bf16)
-    grad_first = (
-        jnp.einsum("rf,df->rd", grad_lifted, upward_full, preferred_element_type=f32) + grad_mid
-    )
-    grad_first_gain = jnp.sum(grad_first * normed_one, axis=0)
-    grad_first_shift = jnp.sum(grad_first, axis=0)
-    grad_residual = normalize_back(grad_first * gain_one, normed_one, scale_one)
-    grad_branch = grad_residual.astype(bf16)
-    grad_output_bias = jnp.sum(grad_branch.astype(f32), axis=0)
-    grad_output_weight = jnp.einsum(
-        "rd,re->de", attended, grad_branch, preferred_element_type=f32
-    ).astype(bf16)
-    grad_attended = jnp.einsum(
-        "re,de->rd", grad_branch, mixer_weight, preferred_element_type=f32
-    ).astype(bf16)
-    by_device = lambda grad: grad.reshape((count, grad.shape[0] // count) + grad.shape[1:])
-    out_downward = reduced(by_device(grad_downward_weight), back_b, count, me)
-    out_upward = reduced(by_device(grad_upward_weight), back_a, count, me)
-    out_mixer = reduced(by_device(grad_output_weight), back_b, count, me)
+    if slotted:
+        follow_parts = [
+            [b, swap(after(b, attended), o[-1], count)] for b, o in zip(follow, follow_orders)
+        ]
+
+    vectors = jnp.stack(
+        [bias_output, bias_downward, gain_one, shift_one, gain_two, shift_two]
+        + [jnp.zeros((width,), f32)] * 2
+    )
+    me_of = me.astype(jnp.int32).reshape(1)
+    outs = feed_forward(
+        me_of,
+        attended,
+        states,
+        cotangent,
+        vectors,
+        bias_upward[None],
+        *follow_parts,
+        follow_orders,
+        (back_a, back_b),
+    )
+    result, grad_residual, grad_attended, small_sums = outs[:4]
+    layer_output = jnp.take(result, slot_index, axis=0)
+    if slotted:
+        (mixed_keep, mixed_send, down_keep, down_send) = outs[4:]
+        reductions = [
+            halved(mixed_keep, mixed_send, back_a, count),
+            halved(down_keep, down_send, back_b, count),
+        ]
+        sends = [next(r) for r in reductions]
+        grad_attended = after(grad_attended, *sends)
+        for _ in range(len(bits) - 1):
+            sends = [r.send(s) for r, s in zip(reductions, sends)]
+        out_mixed, out_downward = [r.send(s) for r, s in zip(reductions, sends)]
+    else:
+        out_mixed = reduced(outs[4].reshape(count, shard, -1), back_a, count, me)
+        out_downward = reduced(outs[5].reshape((count,) + downward_weight.shape), back_b, count, me)
 
     grad_query, grad_key, grad_value = attention_backward(
         lengths, first, queries, keys, values, grad_attended, stats, side
     )
-    grad_triple = jnp.concatenate(
-        [
-            jnp.einsum("rd,rc->dc", states, grad_query, preferred_element_type=f32),
-            jnp.einsum("rd,rc->dc", reach, grad_key, preferred_element_type=f32),
-            jnp.einsum("rd,rc->dc", reach, grad_value, preferred_element_type=f32),
-        ],
-        axis=1,
-    ).astype(bf16)
+    grad_columns = [
+        jnp.einsum("rd,rc->dc", rows_of, grad, preferred_element_type=f32).astype(bf16)
+        for rows_of, grad in ((states, grad_query), (reach, grad_key), (reach, grad_value))
+    ]
+    grad_a, grad_b = (
+        jnp.concatenate([g[:, o : o + half] for g in grad_columns], axis=1).reshape(
+            count, shard, 3 * half
+        )
+        for o in (0, half)
+    )
     grad_query_bias = jnp.sum(grad_query.astype(f32), axis=0)
     grad_value_bias = jnp.sum(grad_value.astype(f32), axis=0)
     grad_reach = jnp.einsum(
-        "rc,dc->rd", grad_key, triple_weight[:, width : 2 * width], preferred_element_type=f32
-    ) + jnp.einsum(
-        "rc,dc->rd", grad_value, triple_weight[:, 2 * width :], preferred_element_type=f32
-    )
-    from_right = shift(grad_reach[thin : side].astype(bf16), -1).astype(f32)
-    from_left = shift(grad_reach[side + rows : side + rows + near].astype(bf16), 1).astype(f32)
+        "rc,dc->rd", grad_key, weight_key, preferred_element_type=f32
+    ) + jnp.einsum("rc,dc->rd", grad_value, weight_value, preferred_element_type=f32)
+    low_part, middle, high_part = (
+        grad_reach[:side],
+        grad_reach[side : side + rows],
+        grad_reach[side + rows :],
+    )
+    grad_outer = jnp.where(is_first, low_part, high_part)
+    grad_near = jnp.where(is_first, high_part[:rows], low_part[thin:])
+    grad_edge = jnp.where(is_first, high_part[rows:], low_part[:thin])
+    back = along(grad_outer.astype(bf16), -1, 1).astype(f32)
+    back_edge = along(grad_edge.astype(bf16), 1, -1).astype(f32)
+    back_own = jnp.where(is_first, back[:thin], back[rows:])
+    back_partner = jnp.where(is_first, back[thin:], back[:rows])
+    back_near = swap((grad_near + back_partner).astype(bf16), blocks_axis, count).astype(f32)
+    pad_low = lambda v: jnp.pad(v, ((0, rows - thin), (0, 0)))
+    pad_high = lambda v: jnp.pad(v, ((rows - thin, 0), (0, 0)))
     grad_input = (
-        grad_reach[side : side + rows]
-        + jnp.einsum("rc,dc->rd", grad_query, triple_weight[:, :width], preferred_element_type=f32)
+        middle
+        + jnp.einsum("rc,dc->rd", grad_query, weight_query, preferred_element_type=f32)
         + grad_residual
-    )
-    grad_input = (
-        grad_input
-        + jnp.pad(from_right, ((rows - near, 0), (0, 0)))
-        + jnp.pad(from_left, ((0, rows - near), (0, 0)))
-    )
-    if thin:
-        far_right = shift(grad_reach[:thin].astype(bf16), -2).astype(f32)
-        far_left = shift(grad_reach[side + rows + near :].astype(bf16), 2).astype(f32)
-        grad_input = (
-            grad_input
-            + jnp.pad(far_right, ((rows - thin, 0), (0, 0)))
-            + jnp.pad(far_left, ((0, rows - thin), (0, 0)))
+        + back_near
+        + jnp.where(
+            is_first, pad_high(back_own) + pad_low(back_edge), pad_low(back_own) + pad_high(back_edge)
         )
+    )
     grad_hidden = jnp.take(grad_input, slot_index, axis=0)
 
-    out_a = reduced(by_device(grad_triple[:, :half]), back_a, count, me)
-    out_b = reduced(by_device(grad_triple[:, half:]), back_b, count, me)
-    out_triple = jnp.concatenate([out_a, out_b], axis=1)
-    grads_small = (
-        grad_query_bias,
-        grad_value_bias,
-        grad_output_bias,
-        grad_downward_bias,
-        grad_first_gain,
-        grad_first_shift,
-        grad_second_gain,
-        grad_second_shift,
-        grad_upward_bias,
-    )
-    packed_grads = jnp.concatenate([by_device(g) for g in grads_small], axis=1)
+    out_a = reduced(grad_a, back_a, count, me)
+    out_b = reduced(grad_b, back_b, count, me)
+    out_triple = jnp.concatenate(
+        [o[:, n * half : (n + 1) * half] for n in range(3) for o in (out_a, out_b)], axis=1
+    )
+    by_device = lambda grad: grad.reshape((count, grad.shape[0] // count))
+    packed_grads = jnp.concatenate(
+        [by_device(g) for g in (grad_query_bias, grad_value_bias, *small_sums[:6])]
+        + [by_device(small_sums[8 : 8 + upward_weight.shape[1] // width].reshape(-1))],
+        axis=1,
+    )
     packed_grads = jnp.pad(packed_grads, ((0, 0), (0, -packed_grads.shape[1] % 128)))
     summed = reduced(packed_grads, back_a, count, me)
     (
@@ -511,8 +741,8 @@
         layer_output,
         grad_hidden,
         out_triple,
-        out_mixer,
-        out_upward,
+        out_mixed[:, :width],
+        out_mixed[:, width:],
         out_downward,
         out_query,
         out_value,

time: 511 us -> 366 us (0.72)
  waiting for transfers between devices: 174 us -> 92.3 us
  matrix products: 75.5 us -> 29 us
  Pallas kernels: 45.9 us -> 76.5 us
  starting transfers between devices: 111 us -> 84.1 us
  other arithmetic: 45.2 us -> 28.6 us
    ppermute x60 -> x47, waiting for transfers between devices: 172 us -> 92 us  [swap(): return lax.ppermute(block, AXES, [(i, i ^ bit) for i in range(count)])]
    dot_general x19 -> x10, matrix products: 73.7 us -> 28.4 us  [the longest x3 9.35 us: local(): jnp.einsum('rd,rc->dc', rows_of, grad, preferred_element_type=f32)]
    pallas_call x0 -> x1, Pallas kernels: none -> 30.6 us  [feed_forward(): pl.pallas_call(functools.partial(feed_kernel, plan), name='feed_forward',...]
    ppermute x8 -> x4, starting transfers between devices: 21.6 us -> 7.64 us  [along(): return lax.ppermute(block, AXES, pairs)]
    select_n x53 -> x23, other arithmetic: 17 us -> 3.41 us  [the longest x18 1.69 us: merge(): jnp.where(me & bit == 0, jnp.concatenate([own, other], axis=axis), jnp.co...]
    ppermute x60 -> x47, starting transfers between devices: 89.8 us -> 76.4 us  [swap(): return lax.ppermute(block, AXES, [(i, i ^ bit) for i in range(count)])]
    dynamic_slice x6 -> x4, local copies, waits for them, and re-layouts: 13.4 us -> 2.75 us  [reduced(): keep = lax.dynamic_index_in_dim(held, mine, axis, keepdims=False)]
    add x0 -> x9, other arithmetic: none -> 10.6 us  [the longest x8 10.3 us: halved(): total = total + swap(send, bit, count).astype(f32)]
  transfers between devices with their start and end apart: 68 -> 51, of which waited for: 34 -> 23; matrix products, arithmetic and copies ran while one was open for 21% -> 26% of each run, Pallas kernels for 4% -> 13%
where the time goes in v2:
time: 366 us; the launch traced here: 362 us
  waiting for transfers between devices  92.3 us (25%)
  starting transfers between devices  84.1 us (23%)
  Pallas kernels  76.5 us (21%)
  local copies, waits for them, and re-layouts  49.2 us (13%)
  matrix products  29 us (8%)
  other arithmetic  28.6 us (8%)
    ppermute x47, waiting for transfers between devices, swap(): return lax.ppermute(block, AXES, [(i, i ^ bit) for i in range(count)])  92 us
    ppermute x47, starting transfers between devices, swap(): return lax.ppermute(block, AXES, [(i, i ^ bit) for i in range(count)])  76.4 us
    pallas_call x1, Pallas kernels, feed_forward(): pl.pallas_call(functools.partial(feed_kernel, plan), name='feed_forward',...  30.6 us
    pallas_call x1, Pallas kernels, attention_backward(): pl.pallas_call(functools.partial(backward_kernel, lengths.shape[0], side)...  24.4 us
    pallas_call x1, Pallas kernels, attention_forward(): pl.pallas_call(functools.partial(forward_kernel, lengths.shape[0], side),...  21.6 us
    add x8, other arithmetic, halved(): total = total + swap(send, bit, count).astype(f32)  10.3 us
    dot_general x3, matrix products, local(): jnp.einsum('rd,rc->dc', rows_of, grad, preferred_element_type=f32)  9.35 us
    ppermute x4, starting transfers between devices, along(): return lax.ppermute(block, AXES, pairs)  7.64 us
  transfers between devices with their start and end apart: 51, of which 23 were waited for; matrix products, arithmetic and copies ran while one was open for 26% of the time, Pallas kernels for 13%

profile of v2, /device:TPU:0, one launch (start us, length us, event | category | flops | bytes accessed | tf_op | source)
XLA Modules:
  0.0 362.0 jit_solution(9641466240918868238)
XLA Ops:
  8.4 4.1 %collective-permute-start = (bf16[24,1280]{1,0:T(8,128)(2,1)S(1)}, bf16[24,1280]{1,0:T(8,128)(2,1)S(1)}, u32[]{:S(2)}, u32[]{:S(2)}) collective-permute-start(bf16[24,1280]{1,0:T(8,128)(2,1)S(1)} %fusion.28), channel_id=1, source_target_pairs={{0,8},{1,9},{2,10},{3,11},{4,12},{5,13},{6,14},{7,15},{8,0},{9,1},... | collective-permute-start | bytes 184328 | tf_op jit(solution)/shard_map/ppermute | solution.py:30
  19.7 2.9 collective-permute-start.18
  23.5 3.5 collective-permute-start.13
  27.1 2.4 collective-permute-done.1
  32.9 4.8 %collective-permute-done.13 = bf16[1,24,3840]{2,1,0:T(8,128)(2,1)S(1)} collective-permute-done((bf16[1,24,3840]{2,1,0:T(8,128)(2,1)S(1)}, bf16[1,24,3840]{2,1,0:T(8,128)(2,1)S(1)}, u32[]{:S(2)}, u32[]{:S(2)}) %collective-permute-start.13) | collective-permute-done | bytes 184352 | tf_op jit(solution)/shard_map/ppermute | solution.py:30
  37.7 2.1 collective-permute-start.14
  42.1 5.6 %collective-permute-done.19 = bf16[2,96,768]{2,1,0:T(8,128)(2,1)S(1)} collective-permute-done((bf16[2,96,768]{2,1,0:T(8,128)(2,1)S(1)}, bf16[2,96,768]{2,1,0:T(8,128)(2,1)S(1)}, u32[]{:S(2)}, u32[]{:S(2)}) %collective-permute-start.19) | collective-permute-done | bytes 294944 | tf_op jit(solution)/shard_map/ppermute | solution.py:30
  49.2 4.7 %collective-permute-done.14 = bf16[2,24,3840]{2,1,0:T(8,128)(2,1)S(1)} collective-permute-done((bf16[2,24,3840]{2,1,0:T(8,128)(2,1)S(1)}, bf16[2,24,3840]{2,1,0:T(8,128)(2,1)S(1)}, u32[]{:S(2)}, u32[]{:S(2)}) %collective-permute-start.14) | collective-permute-done | bytes 368672 | tf_op jit(solution)/shard_map/ppermute | solution.py:30
  55.5 2.0 collective-permute-start.15
  57.6 1.9 collective-permute-start.11
  61.5 10.3 %collective-permute-done.20 = bf16[4,96,768]{2,1,0:T(8,128)(2,1)S(1)} collective-permute-done((bf16[4,96,768]{2,1,0:T(8,128)(2,1)S(1)}, bf16[4,96,768]{2,1,0:T(8,128)(2,1)S(1)}, u32[]{:S(2)}, u32[]{:S(2)}) %collective-permute-start.20) | collective-permute-done | bytes 589856 | tf_op jit(solution)/shard_map/ppermute | solution.py:30
  72.6 7.7 %collective-permute-start.21 = (bf16[8,96,768]{2,1,0:T(8,128)(2,1)S(1)}, bf16[8,96,768]{2,1,0:T(8,128)(2,1)S(1)}, u32[]{:S(2)}, u32[]{:S(2)}) collective-permute-start(bf16[8,96,768]{2,1,0:T(8,128)(2,1)S(1)} %pad_maximum_fusion.8), channel_id=1, source_target_pairs={{0,16},{1,17},{2,18},{3,19},{4,20},{5,21},{6,22},{7,23},{8,24},{9,... | collective-permute-start | bytes 3538952 | tf_op jit(solution)/shard_map/ppermute | solution.py:30
  81.7 2.5 collective-permute-start.16
  87.5 2.1 convolution_convert_fusion.k_ref
  89.6 3.6 add_convert_fusion.v_ref
  94.0 21.6 %attention_forward.1 = (bf16[512,768]{1,0:T(8,128)(2,1)S(1)}, f32[6,8,1024]{2,1,0:T(8,128)S(1)}) custom-call(s32[4]{0:T(128)S(1)} %copy-done.5, s32[1]{0:T(128)} %bitcast.1.first_ref, bf16[512,768]{1,0:T(8,128)(2,1)S(1)} %fusion.12.q_ref, bf16[1568,768]{1,0:T(8,128)(2,1)S(1)} %convolution_convert_fusion.k_ref, bf16[1568,768]{1,0:T(8,128)(2,1)} %add_convert_fusion.v_ref), custom_call_target="tpu_custom_call" | custom-call | tf_op jit(solution)/shard_map/attention_forward/pallas_call | solution.py:235
  118.1 9.5 %collective-permute-start.17 = (bf16[16,24,3840]{2,1,0:T(8,128)(2,1)}, bf16[16,24,3840]{2,1,0:T(8,128)(2,1)}, u32[]{:S(2)}, u32[]{:S(2)}) collective-permute-start(bf16[16,24,3840]{2,1,0:T(8,128)(2,1)} %constant_dynamic-update-slice_fusion.refs_6_), channel_id=1, source_target_pairs={{0,1},{1,0},{2,3},{3,2},{4,5},{5,4},{6,7},{7,6},{8,9},{9,8},{10,11... | collective-permute-start | bytes 8847368 | tf_op jit(solution)/shard_map/ppermute | solution.py:30
  132.9 3.2 collective-permute-done.22.refs_9_
  136.1 30.6 %feed_forward.1 = (bf16[512,768]{1,0:T(8,128)(2,1)}, f32[512,768]{1,0:T(8,128)}, bf16[512,768]{1,0:T(8,128)(2,1)}, f32[16,768]{1,0:T(8,128)}, bf16[16,24,3840]{2...) custom-call(s32[1]{0:T(128)} %bitcast.refs_0_, ...), custom_call_target="tpu_custom_call" | custom-call | tf_op jit(solution)/shard_map/feed_forward/pallas_call | solution.py:462
  169.6 3.6 %gather_fusion = bf16[512,768]{1,0:T(8,128)(2,1)S(1)} fusion(bf16[512,768]{1,0:T(8,128)(2,1)} %get-tuple-element.50, s32[1024]{0:T(1024)S(1)} %pad_clamp_fusion), kind=kCustom, calls=%fused_computation | custom fusion | bytes 1574912 | tf_op jit(solution)/shard_map/jit(_take)/gather | solution.py:656
  175.8 3.1 convert_add_fusion.1
  181.4 2.6 convert_add_fusion
  187.0 24.4 %attention_backward.1 = (bf16[512,768]{1,0:T(8,128)(2,1)S(1)}, bf16[1568,768]{1,0:T(8,128)(2,1)S(1)}, bf16[1568,768]{1,0:T(8,128)(2,1)}) custom-call(s32[4]{0:T(128)S(1)} %copy-done.5, s32[1]{0:T(128)} %bitcast.1.first_ref, bf16[512,768]{1,0:T(8,128)(2,1)S(1)} %fusion.12.q_ref, bf16[1568,768]{1,0:T(8,128)(2,1)} %copy-done.2, ...), custom_call_target="tpu_custom_call" | custom-call | tf_op jit(solution)/shard_map/attention_backward/pallas_call | solution.py:261
  211.5 2.2 convert_reduce_fusion
  213.9 5.2 %convolution_convert_fusion.2 = bf16[768,768]{0,1:T(8,128)(2,1)} fusion(bf16[1568,768]{1,0:T(8,128)(2,1)S(1)} %copy-done.17, bf16[1568,768]{1,0:T(8,128)(2,1)} %get-tuple-element.59), kind=kOutput, calls=%fused_computation.39 | convolution fusion | flops 1850277888 | bytes 5996544 | tf_op jit(solution)/shard_map/rd,rc->dc/dot_general | solution.py:676
  220.0 3.4 convolution_convert_fusion.3
  223.4 4.3 %fusion.16 = f32[1568,768]{1,0:T(8,128)} fusion(bf16[1568,768]{1,0:T(8,128)(2,1)S(1)} %get-tuple-element.58, bf16[768,384]{1,0:T(8,128)(2,1)S(1)} %copy-done.33, bf16[768,384]{1,0:T(8,128)(2,1)S(1)} %copy-done.31), kind=kOutput, calls=%fused_computation.72 | convolution fusion | flops 1852047360 | bytes 8404992 | tf_op jit(solution)/shard_map/rc,dc->rd/dot_general | solution.py:687
  228.1 11.4 %collective-permute-start.46 = (f32[2,2,2,2,384]{4,3,2,1,0:T(2,128)S(1)}, f32[2,2,2,2,384]{4,3,2,1,0:T(2,128)S(1)}, u32[]{:S(2)}, u32[]{:S(2)}) collective-permute-start(f32[2,2,2,2,384]{4,3,2,1,0:T(2,128)S(1)} %bitcast.202), channel_id=1, source_target_pairs={{0,1},{1,0},{2,3},{3,2},{4,5},{5,4},{6,7},{7,6},{8,9},{9,8},{10,11... | collective-permute-start | bytes 73736 | tf_op jit(solution)/shard_map/ppermute | solution.py:30
  240.9 2.1 fusion.48
  244.0 2.3 copy.65
  246.3 2.7 constant_dynamic-slice_fusion.11
  249.0 4.7 %convolution_add_fusion = f32[1568,768]{1,0:T(8,128)S(1)} fusion(f32[1568,768]{1,0:T(8,128)} %fusion.16, bf16[1568,768]{1,0:T(8,128)(2,1)S(1)} %copy-done.18, bf16[768,384]{1,0:T(8,128)(2,1)} %copy-done.29, bf16[768,384]{1,0:T(8,128)(2,1)S(1)} %copy-done.28), kind=kOutput, calls=%fused_computation.6 | convolution fusion | flops 1853251584 | bytes 13221888 | tf_op jit(solution)/shard_map/rc,dc->rd/dot_general | solution.py:689
  256.4 2.7 collective-permute-done.47
  259.2 2.0 fusion.17
  263.7 2.7 copy.64
  267.7 3.2 collective-permute-start.27
  272.4 6.1 %collective-permute-done.50 = f32[384]{0:T(512)S(1)} collective-permute-done((f32[384]{0:T(512)S(1)}, f32[384]{0:T(512)S(1)}, u32[]{:S(2)}, u32[]{:S(2)}) %collective-permute-start.50) | collective-permute-done | bytes 1568 | tf_op jit(solution)/shard_map/ppermute | solution.py:30
  279.7 2.5 slice_add_fusion.1
  282.3 3.9 %collective-permute-start.43 = (bf16[4,96,768]{2,1,0:T(8,128)(2,1)S(1)}, bf16[4,96,768]{2,1,0:T(8,128)(2,1)S(1)}, u32[]{:S(2)}, u32[]{:S(2)}) collective-permute-start(bf16[4,96,768]{2,1,0:T(8,128)(2,1)S(1)} %slice.459), channel_id=1, source_target_pairs={{0,2},{1,3},{2,0},{3,1},{4,6},{5,7},{6,4},{7,5},{8,10},{9,11},{10,... | collective-permute-start | bytes 1769480 | tf_op jit(solution)/shard_map/ppermute | solution.py:30
  289.8 10.6 %collective-permute-done.43 = bf16[4,96,768]{2,1,0:T(8,128)(2,1)S(1)} collective-permute-done((bf16[4,96,768]{2,1,0:T(8,128)(2,1)S(1)}, bf16[4,96,768]{2,1,0:T(8,128)(2,1)S(1)}, u32[]{:S(2)}, u32[]{:S(2)}) %collective-permute-start.43) | collective-permute-done | bytes 589856 | tf_op jit(solution)/shard_map/ppermute | solution.py:30
  300.6 15.0 %collective-permute-done.34 = bf16[2,2,2,24,1152]{4,3,0,1,2:T(8,128)(2,1)S(1)} collective-permute-done((bf16[2,2,2,24,1152]{4,3,0,1,2:T(8,128)(2,1)S(1)}, bf16[2,2,2,24,1152]{4,3,0,1,2:T(8,128)(2,1)S(1)}, u32[]{:S(2)}, u32[]{:S(2)}) %collective-permute-start.34) | collective-permute-done | bytes 442400 | tf_op jit(solution)/shard_map/ppermute | solution.py:30
  325.9 2.6 gather_fusion.1
  328.5 2.9 broadcast_select_fusion
  334.0 2.9 collective-permute-start.37
  338.0 2.8 collective-permute-done.37
  340.8 2.1 collective-permute-done.32
  344.8 7.0 %collective-permute-done.40 = bf16[2,24,3840]{2,1,0:T(8,128)(2,1)S(1)} collective-permute-done((bf16[2,24,3840]{2,1,0:T(8,128)(2,1)S(1)}, bf16[2,24,3840]{2,1,0:T(8,128)(2,1)S(1)}, u32[]{:S(2)}, u32[]{:S(2)}) %collective-permute-start.40) | collective-permute-done | bytes 368672 | tf_op jit(solution)/shard_map/ppermute | solution.py:30
  352.4 8.0 %collective-permute-done.41 = bf16[1,24,3840]{2,1,0:T(8,128)(2,1)S(1)} collective-permute-done((bf16[1,24,3840]{2,1,0:T(8,128)(2,1)S(1)}, bf16[1,24,3840]{2,1,0:T(8,128)(2,1)S(1)}, u32[]{:S(2)}, u32[]{:S(2)}) %collective-permute-start.41) | collective-permute-done | bytes 184352 | tf_op jit(solution)/shard_map/ppermute | solution.py:30
  (322 shorter events, 85.9 us)
Async XLA Ops:
  8.4 11.2 %collective-permute-start = (bf16[24,1280]{1,0:T(8,128)(2,1)S(1)}, bf16[24,1280]{1,0:T(8,128)(2,1)S(1)}, u32[]{:S(2)}, u32[]{:S(2)}) collective-permute-start(bf16[24,1280]{1,0:T(8,128)(2,1)S(1)} %fusion.28), channel_id=1, source_target_pairs={{0,8},{1,9},{2,10},{3,11},{4,12},{5,13},{6,14},{7,15},{8,0},{9,1},... | collective-permute-start | bytes 184328 | tf_op jit(solution)/shard_map/ppermute | solution.py:30
  12.6 5.3 %collective-permute-start.5 = (bf16[24,1152]{1,0:T(8,128)(2,1)S(1)}, bf16[24,1152]{1,0:T(8,128)(2,1)S(1)}, u32[]{:S(2)}, u32[]{:S(2)}) collective-permute-start(bf16[24,1152]{1,0:T(8,128)(2,1)S(1)} %get-tuple-element.114), channel_id=1, source_target_pairs={{0,8},{1,9},{2,10},{3,11},{4,12},{5,13},{6,14},{7,15},{8,0},{9,1},... | collective-permute-start | bytes 165896 | tf_op jit(solution)/shard_map/ppermute | solution.py:30
  14.0 41.5 %collective-permute-start.10 = (bf16[512,768]{1,0:T(8,128)(2,1)S(1)}, bf16[512,768]{1,0:T(8,128)(2,1)S(1)}, u32[]{:S(2)}, u32[]{:S(2)}) collective-permute-start(bf16[512,768]{1,0:T(8,128)(2,1)S(1)} %convolution_convert_fusion.5.refs_2_), channel_id=1, source_target_pairs={{0,16},{1,17},{2,18},{3,19},{4,20},{5,21},{6,22},{7,23},{8,24},{9,... | collective-permute-start | bytes 2359304 | tf_op jit(solution)/shard_map/ppermute | solution.py:30
  15.9 65.9 %collective-permute-start.12 = (bf16[16,768]{1,0:T(8,128)(2,1)S(1)}, bf16[16,768]{1,0:T(8,128)(2,1)S(1)}, u32[]{:S(2)}, u32[]{:S(2)}) collective-permute-start(bf16[16,768]{1,0:T(8,128)(2,1)S(1)} %get-tuple-element.98), channel_id=1, source_target_pairs={{1,0},{2,1},{3,2},{4,3},{5,4},{6,5},{7,6},{8,7},{9,8},{10,9},{11,1... | collective-permute-start | bytes 73736 | tf_op jit(solution)/shard_map/ppermute | solution.py:532
  18.0 5.5 %collective-permute-start.6 = (bf16[2,24,1152]{2,1,0:T(8,128)(2,1)S(1)}, bf16[2,24,1152]{2,1,0:T(8,128)(2,1)S(1)}, u32[]{:S(2)}, u32[]{:S(2)}) collective-permute-start(bf16[2,24,1152]{2,1,0:T(8,128)(2,1)S(1)} %maximum_select_fusion.12), channel_id=1, source_target_pairs={{0,4},{1,5},{2,6},{3,7},{4,0},{5,1},{6,2},{7,3},{8,12},{9,13},{10,... | collective-permute-start | bytes 331784 | tf_op jit(solution)/shard_map/ppermute | solution.py:30
  19.7 11.5 %collective-permute-start.18 = (bf16[1,96,768]{2,1,0:T(8,128)(2,1)S(1)}, bf16[1,96,768]{2,1,0:T(8,128)(2,1)S(1)}, u32[]{:S(2)}, u32[]{:S(2)}) collective-permute-start(bf16[1,96,768]{2,1,0:T(8,128)(2,1)S(1)} %bitcast.200), channel_id=1, source_target_pairs={{0,8},{1,9},{2,10},{3,11},{4,12},{5,13},{6,14},{7,15},{8,0},{9,1},... | collective-permute-start | bytes 442376 | tf_op jit(solution)/shard_map/ppermute | solution.py:30
  22.7 6.9 %collective-permute-start.1 = (bf16[2,24,1280]{2,1,0:T(8,128)(2,1)S(1)}, bf16[2,24,1280]{2,1,0:T(8,128)(2,1)S(1)}, u32[]{:S(2)}, u32[]{:S(2)}) collective-permute-start(bf16[2,24,1280]{2,1,0:T(8,128)(2,1)S(1)} %maximum_select_fusion.10), channel_id=1, source_target_pairs={{0,4},{1,5},{2,6},{3,7},{4,0},{5,1},{6,2},{7,3},{8,12},{9,13},{10,... | collective-permute-start | bytes 368648 | tf_op jit(solution)/shard_map/ppermute | solution.py:30
  23.5 14.2 %collective-permute-start.13 = (bf16[1,24,3840]{2,1,0:T(8,128)(2,1)S(1)}, bf16[1,24,3840]{2,1,0:T(8,128)(2,1)S(1)}, u32[]{:S(2)}, u32[]{:S(2)}) collective-permute-start(bf16[1,24,3840]{2,1,0:T(8,128)(2,1)S(1)} %maximum_bitcast_fusion.4), channel_id=1, source_target_pairs={{0,8},{1,9},{2,10},{3,11},{4,12},{5,13},{6,14},{7,15},{8,0},{9,1},... | collective-permute-start | bytes 552968 | tf_op jit(solution)/shard_map/ppermute | solution.py:30
  29.5 8.2 %collective-permute-start.7 = (bf16[2,2,24,1152]{3,2,1,0:T(8,128)(2,1)S(1)}, bf16[2,2,24,1152]{3,2,1,0:T(8,128)(2,1)S(1)}, u32[]{:S(2)}, u32[]{:S(2)}) collective-permute-start(bf16[2,2,24,1152]{3,2,1,0:T(8,128)(2,1)S(1)} %maximum_select_fusion.8), channel_id=1, source_target_pairs={{0,2},{1,3},{2,0},{3,1},{4,6},{5,7},{6,4},{7,5},{8,10},{9,11},{10,... | collective-permute-start | bytes 663560 | tf_op jit(solution)/shard_map/ppermute | solution.py:30
  31.2 9.0 %collective-permute-start.2 = (bf16[2,2,24,1280]{3,2,1,0:T(8,128)(2,1)S(1)}, bf16[2,2,24,1280]{3,2,1,0:T(8,128)(2,1)S(1)}, u32[]{:S(2)}, u32[]{:S(2)}) collective-permute-start(bf16[2,2,24,1280]{3,2,1,0:T(8,128)(2,1)S(1)} %maximum_select_fusion.7), channel_id=1, source_target_pairs={{0,16},{1,17},{2,18},{3,19},{4,20},{5,21},{6,22},{7,23},{8,24},{9,... | collective-permute-start | bytes 737288 | tf_op jit(solution)/shard_map/ppermute | solution.py:30
  37.7 9.9 %collective-permute-start.19 = (bf16[2,96,768]{2,1,0:T(8,128)(2,1)S(1)}, bf16[2,96,768]{2,1,0:T(8,128)(2,1)S(1)}, u32[]{:S(2)}, u32[]{:S(2)}) collective-permute-start(bf16[2,96,768]{2,1,0:T(8,128)(2,1)S(1)} %pad_maximum_fusion.22), channel_id=1, source_target_pairs={{0,4},{1,5},{2,6},{3,7},{4,0},{5,1},{6,2},{7,3},{8,12},{9,13},{10,... | collective-permute-start | bytes 884744 | tf_op jit(solution)/shard_map/ppermute | solution.py:30
  37.7 16.2 %collective-permute-start.14 = (bf16[2,24,3840]{2,1,0:T(8,128)(2,1)S(1)}, bf16[2,24,3840]{2,1,0:T(8,128)(2,1)S(1)}, u32[]{:S(2)}, u32[]{:S(2)}) collective-permute-start(bf16[2,24,3840]{2,1,0:T(8,128)(2,1)S(1)} %pad_maximum_fusion.21), channel_id=1, source_target_pairs={{0,4},{1,5},{2,6},{3,7},{4,0},{5,1},{6,2},{7,3},{8,12},{9,13},{10,... | collective-permute-start | bytes 1105928 | tf_op jit(solution)/shard_map/ppermute | solution.py:30
  40.1 17.5 %collective-permute-start.8 = (bf16[2,2,2,24,1152]{4,3,2,1,0:T(8,128)(2,1)S(1)}, bf16[2,2,2,24,1152]{4,3,2,1,0:T(8,128)(2,1)S(1)}, u32[]{:S(2)}, u32[]{:S(2)}) collective-permute-start(bf16[2,2,2,24,1152]{4,3,2,1,0:T(8,128)(2,1)S(1)} %maximum_select_fusion.6), channel_id=1, source_target_pairs={{0,16},{1,17},{2,18},{3,19},{4,20},{5,21},{6,22},{7,23},{8,24},{9,... | collective-permute-start | bytes 1327112 | tf_op jit(solution)/shard_map/ppermute | solution.py:30
  47.6 12.5 %collective-permute-start.3 = (bf16[2,2,2,24,1280]{4,3,2,1,0:T(8,128)(2,1)S(1)}, bf16[2,2,2,24,1280]{4,3,2,1,0:T(8,128)(2,1)S(1)}, u32[]{:S(2)}, u32[]{:S(2)}) collective-permute-start(bf16[2,2,2,24,1280]{4,3,2,1,0:T(8,128)(2,1)S(1)} %maximum_select_fusion.5), channel_id=1, source_target_pairs={{0,2},{1,3},{2,0},{3,1},{4,6},{5,7},{6,4},{7,5},{8,10},{9,11},{10,... | collective-permute-start | bytes 1474568 | tf_op jit(solution)/shard_map/ppermute | solution.py:30
  53.9 18.0 %collective-permute-start.20 = (bf16[4,96,768]{2,1,0:T(8,128)(2,1)S(1)}, bf16[4,96,768]{2,1,0:T(8,128)(2,1)S(1)}, u32[]{:S(2)}, u32[]{:S(2)}) collective-permute-start(bf16[4,96,768]{2,1,0:T(8,128)(2,1)S(1)} %pad_maximum_fusion.18), channel_id=1, source_target_pairs={{0,2},{1,3},{2,0},{3,1},{4,6},{5,7},{6,4},{7,5},{8,10},{9,11},{10,... | collective-permute-start | bytes 1769480 | tf_op jit(solution)/shard_map/ppermute | solution.py:30
  55.5 17.1 %collective-permute-start.15 = (bf16[4,24,3840]{2,1,0:T(8,128)(2,1)S(1)}, bf16[4,24,3840]{2,1,0:T(8,128)(2,1)S(1)}, u32[]{:S(2)}, u32[]{:S(2)}) collective-permute-start(bf16[4,24,3840]{2,1,0:T(8,128)(2,1)S(1)} %pad_maximum_fusion.17), channel_id=1, source_target_pairs={{0,16},{1,17},{2,18},{3,19},{4,20},{5,21},{6,22},{7,23},{8,24},{9,... | collective-permute-start | bytes 2211848 | tf_op jit(solution)/shard_map/ppermute | solution.py:30
  57.6 26.6 %collective-permute-start.11 = (bf16[528,768]{1,0:T(8,128)(2,1)S(1)}, bf16[528,768]{1,0:T(8,128)(2,1)S(1)}, u32[]{:S(2)}, u32[]{:S(2)}) collective-permute-start(bf16[528,768]{1,0:T(8,128)(2,1)S(1)} %maximum_select_fusion.4), channel_id=1, source_target_pairs={{0,1},{1,2},{2,3},{3,4},{4,5},{5,6},{6,7},{7,8},{8,9},{9,10},{10,1... | collective-permute-start | bytes 2433032 | tf_op jit(solution)/shard_map/ppermute | solution.py:532
  60.2 24.6 %collective-permute-start.9 = (bf16[2,2,2,2,24,1152]{5,4,3,2,1,0:T(8,128)(2,1)S(1)}, bf16[2,2,2,2,24,1152]{5,4,3,2,1,0:T(8,128)(2,1)S(1)}, u32[]{:S(2)}, u32[]{:S(2)}) collective-permute-start(bf16[2,2,2,2,24,1152]{5,4,3,2,1,0:T(8,128)(2,1)S(1)} %maximum_select_fusion.3), channel_id=1, source_target_pairs={{0,1},{1,0},{2,3},{3,2},{4,5},{5,4},{6,7},{7,6},{8,9},{9,8},{10,11... | collective-permute-start | bytes 2654216 | tf_op jit(solution)/shard_map/ppermute | solution.py:30
  71.9 13.4 %collective-permute-start.4 = (bf16[2,2,2,2,24,1280]{5,4,3,2,1,0:T(8,128)(2,1)S(1)}, bf16[2,2,2,2,24,1280]{5,4,3,2,1,0:T(8,128)(2,1)S(1)}, u32[]{:S(2)}, u32[]{:S(2)}) collective-permute-start(bf16[2,2,2,2,24,1280]{5,4,3,2,1,0:T(8,128)(2,1)S(1)} %maximum_select_fusion.2), channel_id=1, source_target_pairs={{0,1},{1,0},{2,3},{3,2},{4,5},{5,4},{6,7},{7,6},{8,9},{9,8},{10,11... | collective-permute-start | bytes 2949128 | tf_op jit(solution)/shard_map/ppermute | solution.py:30
  72.6 55.1 %collective-permute-start.21 = (bf16[8,96,768]{2,1,0:T(8,128)(2,1)S(1)}, bf16[8,96,768]{2,1,0:T(8,128)(2,1)S(1)}, u32[]{:S(2)}, u32[]{:S(2)}) collective-permute-start(bf16[8,96,768]{2,1,0:T(8,128)(2,1)S(1)} %pad_maximum_fusion.8), channel_id=1, source_target_pairs={{0,16},{1,17},{2,18},{3,19},{4,20},{5,21},{6,22},{7,23},{8,24},{9,... | collective-permute-start | bytes 3538952 | tf_op jit(solution)/shard_map/ppermute | solution.py:30
  81.7 35.2 %collective-permute-start.16 = (bf16[8,24,3840]{2,1,0:T(8,128)(2,1)S(1)}, bf16[8,24,3840]{2,1,0:T(8,128)(2,1)S(1)}, u32[]{:S(2)}, u32[]{:S(2)}) collective-permute-start(bf16[8,24,3840]{2,1,0:T(8,128)(2,1)S(1)} %pad_maximum_fusion.4), channel_id=1, source_target_pairs={{0,2},{1,3},{2,0},{3,1},{4,6},{5,7},{6,4},{7,5},{8,10},{9,11},{10,... | collective-permute-start | bytes 4423688 | tf_op jit(solution)/shard_map/ppermute | solution.py:30
  118.1 18.0 %collective-permute-start.17 = (bf16[16,24,3840]{2,1,0:T(8,128)(2,1)}, bf16[16,24,3840]{2,1,0:T(8,128)(2,1)}, u32[]{:S(2)}, u32[]{:S(2)}) collective-permute-start(bf16[16,24,3840]{2,1,0:T(8,128)(2,1)} %constant_dynamic-update-slice_fusion.refs_6_), channel_id=1, source_target_pairs={{0,1},{1,0},{2,3},{3,2},{4,5},{5,4},{6,7},{7,6},{8,9},{9,8},{10,11... | collective-permute-start | bytes 8847368 | tf_op jit(solution)/shard_map/ppermute | solution.py:30
  127.8 8.3 %collective-permute-start.22 = (bf16[16,96,768]{2,1,0:T(8,128)(2,1)S(1)}, bf16[16,96,768]{2,1,0:T(8,128)(2,1)}, u32[]{:S(2)}, u32[]{:S(2)}) collective-permute-start(bf16[16,96,768]{2,1,0:T(8,128)(2,1)S(1)} %constant_dynamic-update-slice_fusion.2.refs_8_), channel_id=1, source_target_pairs={{0,1},{1,0},{2,3},{3,2},{4,5},{5,4},{6,7},{7,6},{8,9},{9,8},{10,11... | collective-permute-start | bytes 7077896 | tf_op jit(solution)/shard_map/ppermute | solution.py:30
  166.7 13.6 %collective-permute-start.23 = (bf16[16,24,3840]{2,1,0:T(8,128)(2,1)}, bf16[16,24,3840]{2,1,0:T(8,128)(2,1)}, u32[]{:S(2)}, u32[]{:S(2)}) collective-permute-start(bf16[16,24,3840]{2,1,0:T(8,128)(2,1)} %get-tuple-element.53), channel_id=1, source_target_pairs={{0,1},{1,0},{2,3},{3,2},{4,5},{5,4},{6,7},{7,6},{8,9},{9,8},{10,11... | collective-permute-start | bytes 8847368 | tf_op jit(solution)/shard_map/ppermute | solution.py:30
  167.1 8.7 %collective-permute-start.24 = (bf16[16,96,768]{2,1,0:T(8,128)(2,1)}, bf16[16,96,768]{2,1,0:T(8,128)(2,1)}, u32[]{:S(2)}, u32[]{:S(2)}) collective-permute-start(bf16[16,96,768]{2,1,0:T(8,128)(2,1)} %get-tuple-element.55), channel_id=1, source_target_pairs={{0,1},{1,0},{2,3},{3,2},{4,5},{5,4},{6,7},{7,6},{8,9},{9,8},{10,11... | collective-permute-start | bytes 7077896 | tf_op jit(solution)/shard_map/ppermute | solution.py:30
  180.2 99.4 %collective-permute-start.42 = (bf16[8,96,768]{2,1,0:T(8,128)(2,1)}, bf16[8,96,768]{2,1,0:T(8,128)(2,1)}, u32[]{:S(2)}, u32[]{:S(2)}) collective-permute-start(bf16[8,96,768]{2,1,0:T(8,128)(2,1)} %slice.457), channel_id=1, source_target_pairs={{0,16},{1,17},{2,18},{3,19},{4,20},{5,21},{6,22},{7,23},{8,24},{9,... | collective-permute-start | bytes 3538952 | tf_op jit(solution)/shard_map/ppermute | solution.py:30
  185.3 133.7 %collective-permute-start.38 = (bf16[8,24,3840]{2,1,0:T(8,128)(2,1)}, bf16[8,24,3840]{2,1,0:T(8,128)(2,1)}, u32[]{:S(2)}, u32[]{:S(2)}) collective-permute-start(bf16[8,24,3840]{2,1,0:T(8,128)(2,1)} %slice.456), channel_id=1, source_target_pairs={{0,2},{1,3},{2,0},{3,1},{4,6},{5,7},{6,4},{7,5},{8,10},{9,11},{10,... | collective-permute-start | bytes 4423688 | tf_op jit(solution)/shard_map/ppermute | solution.py:30
  228.1 27.1 %collective-permute-start.46 = (f32[2,2,2,2,384]{4,3,2,1,0:T(2,128)S(1)}, f32[2,2,2,2,384]{4,3,2,1,0:T(2,128)S(1)}, u32[]{:S(2)}, u32[]{:S(2)}) collective-permute-start(f32[2,2,2,2,384]{4,3,2,1,0:T(2,128)S(1)} %bitcast.202), channel_id=1, source_target_pairs={{0,1},{1,0},{2,3},{3,2},{4,5},{5,4},{6,7},{7,6},{8,9},{9,8},{10,11... | collective-permute-start | bytes 73736 | tf_op jit(solution)/shard_map/ppermute | solution.py:30
  262.8 8.1 %collective-permute-start.49 = (f32[2,384]{1,0:T(2,128)S(1)}, f32[2,384]{1,0:T(2,128)S(1)}, u32[]{:S(2)}, u32[]{:S(2)}) collective-permute-start(f32[2,384]{1,0:T(2,128)S(1)} %bitcast.204), channel_id=1, source_target_pairs={{0,4},{1,5},{2,6},{3,7},{4,0},{5,1},{6,2},{7,3},{8,12},{9,13},{10,... | collective-permute-start | bytes 9224 | tf_op jit(solution)/shard_map/ppermute | solution.py:30
  266.4 19.8 %collective-permute-start.25 = (bf16[528,768]{1,0:T(8,128)(2,1)}, bf16[528,768]{1,0:T(8,128)(2,1)S(1)}, u32[]{:S(2)}, u32[]{:S(2)}) collective-permute-start(bf16[528,768]{1,0:T(8,128)(2,1)} %fusion.6), channel_id=1, source_target_pairs={{1,0},{2,1},{3,2},{4,3},{5,4},{6,5},{7,6},{8,7},{9,8},{10,9},{11,1... | collective-permute-start | bytes 2433032 | tf_op jit(solution)/shard_map/ppermute | solution.py:532
  271.0 7.5 %collective-permute-start.50 = (f32[384]{0:T(512)S(1)}, f32[384]{0:T(512)S(1)}, u32[]{:S(2)}, u32[]{:S(2)}) collective-permute-start(f32[384]{0:T(512)S(1)} %get-tuple-element.77), channel_id=1, source_target_pairs={{0,8},{1,9},{2,10},{3,11},{4,12},{5,13},{6,14},{7,15},{8,0},{9,1},... | collective-permute-start | bytes 4616 | tf_op jit(solution)/shard_map/ppermute | solution.py:30
  271.6 15.3 %collective-permute-start.33 = (bf16[2,2,2,2,24,1152]{5,4,1,2,3,0:T(8,128)(2,1)S(1)}, bf16[2,2,2,2,24,1152]{5,4,1,2,3,0:T(8,128)(2,1)S(1)}, u32[]{:S(2)}, u32[]{:S(2)}) collective-permute-start(bf16[2,2,2,2,24,1152]{5,4,1,2,3,0:T(8,128)(2,1)S(1)} %bitcast.186), channel_id=1, source_target_pairs={{0,1},{1,0},{2,3},{3,2},{4,5},{5,4},{6,7},{7,6},{8,9},{9,8},{10,11... | collective-permute-start | bytes 2654216 | tf_op jit(solution)/shard_map/ppermute | solution.py:30
  278.5 10.8 %collective-permute-start.28 = (bf16[2,2,2,2,24,1152]{5,4,3,2,1,0:T(8,128)(2,1)S(1)}, bf16[2,2,2,2,24,1152]{5,4,3,2,1,0:T(8,128)(2,1)S(1)}, u32[]{:S(2)}, u32[]{:S(2)}) collective-permute-start(bf16[2,2,2,2,24,1152]{5,4,3,2,1,0:T(8,128)(2,1)S(1)} %dynamic-slice_bitcast_fusion), channel_id=1, source_target_pairs={{0,1},{1,0},{2,3},{3,2},{4,5},{5,4},{6,7},{7,6},{8,9},{9,8},{10,11... | collective-permute-start | bytes 2654216 | tf_op jit(solution)/shard_map/ppermute | solution.py:30
  282.3 18.1 %collective-permute-start.43 = (bf16[4,96,768]{2,1,0:T(8,128)(2,1)S(1)}, bf16[4,96,768]{2,1,0:T(8,128)(2,1)S(1)}, u32[]{:S(2)}, u32[]{:S(2)}) collective-permute-start(bf16[4,96,768]{2,1,0:T(8,128)(2,1)S(1)} %slice.459), channel_id=1, source_target_pairs={{0,2},{1,3},{2,0},{3,1},{4,6},{5,7},{6,4},{7,5},{8,10},{9,11},{10,... | collective-permute-start | bytes 1769480 | tf_op jit(solution)/shard_map/ppermute | solution.py:30
  286.8 38.6 %collective-permute-start.26 = (bf16[512,768]{1,0:T(8,128)(2,1)S(1)}, bf16[512,768]{1,0:T(8,128)(2,1)S(1)}, u32[]{:S(2)}, u32[]{:S(2)}) collective-permute-start(bf16[512,768]{1,0:T(8,128)(2,1)S(1)} %fusion.8), channel_id=1, source_target_pairs={{0,16},{1,17},{2,18},{3,19},{4,20},{5,21},{6,22},{7,23},{8,24},{9,... | collective-permute-start | bytes 2359304 | tf_op jit(solution)/shard_map/ppermute | solution.py:30
  287.8 27.8 %collective-permute-start.34 = (bf16[2,2,2,24,1152]{4,3,0,1,2:T(8,128)(2,1)S(1)}, bf16[2,2,2,24,1152]{4,3,0,1,2:T(8,128)(2,1)S(1)}, u32[]{:S(2)}, u32[]{:S(2)}) collective-permute-start(bf16[2,2,2,24,1152]{4,3,0,1,2:T(8,128)(2,1)S(1)} %dynamic-slice_bitcast_fusion.1), channel_id=1, source_target_pairs={{0,16},{1,17},{2,18},{3,19},{4,20},{5,21},{6,22},{7,23},{8,24},{9,... | collective-permute-start | bytes 1327112 | tf_op jit(solution)/shard_map/ppermute | solution.py:30
  289.6 26.6 %collective-permute-start.29 = (bf16[2,2,2,24,1152]{4,3,2,1,0:T(8,128)(2,1)S(1)}, bf16[2,2,2,24,1152]{4,3,2,1,0:T(8,128)(2,1)S(1)}, u32[]{:S(2)}, u32[]{:S(2)}) collective-permute-start(bf16[2,2,2,24,1152]{4,3,2,1,0:T(8,128)(2,1)S(1)} %dynamic-slice_bitcast_fusion.2), channel_id=1, source_target_pairs={{0,2},{1,3},{2,0},{3,1},{4,6},{5,7},{6,4},{7,5},{8,10},{9,11},{10,... | collective-permute-start | bytes 1327112 | tf_op jit(solution)/shard_map/ppermute | solution.py:30
  300.5 16.2 %collective-permute-start.44 = (bf16[2,96,768]{2,1,0:T(8,128)(2,1)S(1)}, bf16[2,96,768]{2,1,0:T(8,128)(2,1)S(1)}, u32[]{:S(2)}, u32[]{:S(2)}) collective-permute-start(bf16[2,96,768]{2,1,0:T(8,128)(2,1)S(1)} %slice.461), channel_id=1, source_target_pairs={{0,4},{1,5},{2,6},{3,7},{4,0},{5,1},{6,2},{7,3},{8,12},{9,13},{10,... | collective-permute-start | bytes 884744 | tf_op jit(solution)/shard_map/ppermute | solution.py:30
  315.7 6.3 %collective-permute-start.35 = (bf16[2,2,24,1152]{3,2,0,1:T(8,128)(2,1)S(1)}, bf16[2,2,24,1152]{3,2,0,1:T(8,128)(2,1)S(1)}, u32[]{:S(2)}, u32[]{:S(2)}) collective-permute-start(bf16[2,2,24,1152]{3,2,0,1:T(8,128)(2,1)S(1)} %dynamic-slice_bitcast_fusion.3), channel_id=1, source_target_pairs={{0,2},{1,3},{2,0},{3,1},{4,6},{5,7},{6,4},{7,5},{8,10},{9,11},{10,... | collective-permute-start | bytes 663560 | tf_op jit(solution)/shard_map/ppermute | solution.py:30
  316.4 7.3 %collective-permute-start.30 = (bf16[2,2,24,1152]{3,2,1,0:T(8,128)(2,1)S(1)}, bf16[2,2,24,1152]{3,2,1,0:T(8,128)(2,1)S(1)}, u32[]{:S(2)}, u32[]{:S(2)}) collective-permute-start(bf16[2,2,24,1152]{3,2,1,0:T(8,128)(2,1)S(1)} %dynamic-slice_bitcast_fusion.4), channel_id=1, source_target_pairs={{0,16},{1,17},{2,18},{3,19},{4,20},{5,21},{6,22},{7,23},{8,24},{9,... | collective-permute-start | bytes 663560 | tf_op jit(solution)/shard_map/ppermute | solution.py:30
  317.5 13.9 %collective-permute-start.45 = (bf16[1,96,768]{2,1,0:T(8,128)(2,1)}, bf16[1,96,768]{2,1,0:T(8,128)(2,1)}, u32[]{:S(2)}, u32[]{:S(2)}) collective-permute-start(bf16[1,96,768]{2,1,0:T(8,128)(2,1)} %slice.463), channel_id=1, source_target_pairs={{0,8},{1,9},{2,10},{3,11},{4,12},{5,13},{6,14},{7,15},{8,0},{9,1},... | collective-permute-start | bytes 442376 | tf_op jit(solution)/shard_map/ppermute | solution.py:30
  321.6 21.3 %collective-permute-start.39 = (bf16[4,24,3840]{2,1,0:T(8,128)(2,1)}, bf16[4,24,3840]{2,1,0:T(8,128)(2,1)S(1)}, u32[]{:S(2)}, u32[]{:S(2)}) collective-permute-start(bf16[4,24,3840]{2,1,0:T(8,128)(2,1)} %slice.458), channel_id=1, source_target_pairs={{0,16},{1,17},{2,18},{3,19},{4,20},{5,21},{6,22},{7,23},{8,24},{9,... | collective-permute-start | bytes 2211848 | tf_op jit(solution)/shard_map/ppermute | solution.py:30
  322.7 10.3 %collective-permute-start.36 = (bf16[2,24,1152]{2,1,0:T(8,128)(2,1)}, bf16[2,24,1152]{2,1,0:T(8,128)(2,1)}, u32[]{:S(2)}, u32[]{:S(2)}) collective-permute-start(bf16[2,24,1152]{2,1,0:T(8,128)(2,1)} %dynamic-slice_bitcast_fusion.5), channel_id=1, source_target_pairs={{0,4},{1,5},{2,6},{3,7},{4,0},{5,1},{6,2},{7,3},{8,12},{9,13},{10,... | collective-permute-start | bytes 331784 | tf_op jit(solution)/shard_map/ppermute | solution.py:30
  324.4 12.4 %collective-permute-start.31 = (bf16[2,24,1152]{2,1,0:T(8,128)(2,1)}, bf16[2,24,1152]{2,1,0:T(8,128)(2,1)}, u32[]{:S(2)}, u32[]{:S(2)}) collective-permute-start(bf16[2,24,1152]{2,1,0:T(8,128)(2,1)} %dynamic-slice_bitcast_fusion.6), channel_id=1, source_target_pairs={{0,4},{1,5},{2,6},{3,7},{4,0},{5,1},{6,2},{7,3},{8,12},{9,13},{10,... | collective-permute-start | bytes 331784 | tf_op jit(solution)/shard_map/ppermute | solution.py:30
  334.0 6.8 %collective-permute-start.37 = (bf16[24,1152]{1,0:T(8,128)(2,1)S(1)}, bf16[24,1152]{1,0:T(8,128)(2,1)S(1)}, u32[]{:S(2)}, u32[]{:S(2)}) collective-permute-start(bf16[24,1152]{1,0:T(8,128)(2,1)S(1)} %dynamic-slice_bitcast_fusion.7), channel_id=1, source_target_pairs={{0,8},{1,9},{2,10},{3,11},{4,12},{5,13},{6,14},{7,15},{8,0},{9,1},... | collective-permute-start | bytes 165896 | tf_op jit(solution)/shard_map/ppermute | solution.py:30
  337.8 5.1 %collective-permute-start.32 = (bf16[24,1152]{1,0:T(8,128)(2,1)S(1)}, bf16[24,1152]{1,0:T(8,128)(2,1)S(1)}, u32[]{:S(2)}, u32[]{:S(2)}) collective-permute-start(bf16[24,1152]{1,0:T(8,128)(2,1)S(1)} %dynamic-slice_bitcast_fusion.8), channel_id=1, source_target_pairs={{0,8},{1,9},{2,10},{3,11},{4,12},{5,13},{6,14},{7,15},{8,0},{9,1},... | collective-permute-start | bytes 165896 | tf_op jit(solution)/shard_map/ppermute | solution.py:30
  343.2 8.6 %collective-permute-start.40 = (bf16[2,24,3840]{2,1,0:T(8,128)(2,1)S(1)}, bf16[2,24,3840]{2,1,0:T(8,128)(2,1)S(1)}, u32[]{:S(2)}, u32[]{:S(2)}) collective-permute-start(bf16[2,24,3840]{2,1,0:T(8,128)(2,1)S(1)} %slice.460), channel_id=1, source_target_pairs={{0,4},{1,5},{2,6},{3,7},{4,0},{5,1},{6,2},{7,3},{8,12},{9,13},{10,... | collective-permute-start | bytes 1105928 | tf_op jit(solution)/shard_map/ppermute | solution.py:30
  351.9 8.5 %collective-permute-start.41 = (bf16[1,24,3840]{2,1,0:T(8,128)(2,1)S(1)}, bf16[1,24,3840]{2,1,0:T(8,128)(2,1)S(1)}, u32[]{:S(2)}, u32[]{:S(2)}) collective-permute-start(bf16[1,24,3840]{2,1,0:T(8,128)(2,1)S(1)} %slice.462), channel_id=1, source_target_pairs={{0,8},{1,9},{2,10},{3,11},{4,12},{5,13},{6,14},{7,15},{8,0},{9,1},... | collective-permute-start | bytes 552968 | tf_op jit(solution)/shard_map/ppermute | solution.py:30
  (46 other events, 403.5 us)

commit v3 on v2

v3 whole, which is shorter than its diff:
```python
import functools

import jax
import jax.numpy as jnp
import numpy as np
from jax import lax
from jax.experimental import pallas as pl
from jax.experimental.pallas import tpu as pltpu
from jax.sharding import PartitionSpec as P

DH = 64
SEG_TOK = 502
MEMR = 10
SEG_ROWS = SEG_TOK + 2 * MEMR
AXES = ("head", "blk")
TILE = 128
PAIR = 2 * DH
WINDOW = 544

norm_eps = 1e-12
masked_score = -1e30
score_scale = 0.125
root_half = 0.7071067811865476
inverse_root_two_pi = 0.3989422804014327
f32 = jnp.float32
bf16 = jnp.bfloat16


def swap(block, bit, count):
    return lax.ppermute(block, AXES, [(i, i ^ bit) for i in range(count)])


def tied(values, others):
    values = tuple(values)
    return list(lax.optimization_barrier((*values, *others))[: len(values)])


def after(value, *others):
    return tied([value], others)[0]


def relative(bits):
    return [sum(bit for at, bit in enumerate(bits) if j >> at & 1) for j in range(1 << len(bits))]


def gathered(shard, order, count, me):
    held, have = shard, []
    for bit in order:
        axis = sum(b > bit for b in have)
        have.append(bit)
        other = jnp.expand_dims(swap(held, bit, count), axis)
        own = jnp.expand_dims(held, axis)
        held = jnp.where(
            (me & bit) == 0,
            jnp.concatenate([own, other], axis=axis),
            jnp.concatenate([other, own], axis=axis),
        )
    return held.reshape((count * shard.shape[0],) + shard.shape[1:])


def reduced(blocks, order, count, me):
    have = sorted(order, reverse=True)
    held = blocks.reshape((2,) * len(have) + blocks.shape[1:])
    for step, bit in enumerate(order):
        axis = have.index(bit)
        have.remove(bit)
        mine = ((me & bit) != 0).astype(jnp.int32)
        keep = lax.dynamic_index_in_dim(held, mine, axis, keepdims=False)
        send = lax.dynamic_index_in_dim(held, 1 - mine, axis, keepdims=False)
        total = keep.astype(f32) + swap(send, bit, count).astype(f32)
        held = total if not have else total.astype(blocks.dtype)
    return held


class Spread:
    def __init__(self, held, rounds, count):
        self.held, self.rounds, self.count = held, list(rounds), count
        self.parts = None

    def start(self):
        self.recvs = [swap(self.held, c, self.count) for c in relative(self.rounds[0])[1:]]

    def finish(self, token=()):
        recvs = tied(self.recvs, token) if token else self.recvs
        self.held = jnp.concatenate([self.held, *recvs], axis=0)
        self.rounds.pop(0)
        return self.held

    def start_two(self):
        self.start()
        (self.last,) = self.rounds[1]
        self.own = swap(self.held, self.last, self.count)

    def finish_two(self, token=()):
        recvs = tied(self.recvs, token) if token else self.recvs
        self.parts = [self.held, *recvs, self.own, *[swap(r, self.last, self.count) for r in recvs]]
        return recvs


def piece_places(rounds):
    base = relative([b for r in rounds[:-2] for b in r])
    pieces = [[j + c for j in base] for c in relative(rounds[-2])]
    return [[j + c for j in piece] for c in relative(rounds[-1]) for piece in pieces]


class Gathering:
    def __init__(self, keep, send, rounds, count):
        self.terms, self.sends, self.rounds, self.count = [keep], [send], list(rounds), count
        self.total = None
        self.start()

    def start(self):
        combos = relative(self.rounds[0][::-1])[1:]
        self.recvs = [swap(s, c, self.count) for s, c in zip(self.sends, combos)]

    def arrive(self, token=()):
        self.recvs = tied(self.recvs, token) if token else self.recvs
        return self.recvs

    def advance(self, token=()):
        recvs = self.arrive(token)
        self.terms += recvs
        self.rounds.pop(0)
        add = lambda at: sum(t[at].astype(f32) for t in self.terms)
        if not self.rounds:
            self.total = add(0)
            return [self.total]
        parts = 1 << len(self.rounds[0])
        each = self.terms[0].shape[0] // parts
        self.sends = [add(slice(j * each, (j + 1) * each)).astype(bf16) for j in range(1, parts)]
        self.terms = [t[:each] for t in self.terms]
        self.start()
        return self.sends


def segment_at(lengths_ref, sequences, position):
    start = jnp.int32(0)
    low = jnp.int32(0)
    high = jnp.int32(0)
    for i in range(sequences):
        tokens = lengths_ref[i]
        end = start + tokens + 2 * MEMR * lax.div(tokens + (SEG_TOK - 1), jnp.int32(SEG_TOK))
        inside = (position >= start) & (position < end)
        first = start + lax.div(position - start, jnp.int32(SEG_ROWS)) * SEG_ROWS
        low = jnp.where(inside, first, low)
        high = jnp.where(inside, jnp.minimum(first + SEG_ROWS, end), high)
        start = end
    return low, high


def over_segments(lengths_ref, sequences, first_row, rows, side, body):
    def step(position):
        low, high = segment_at(lengths_ref, sequences, position)
        high = jnp.maximum(high, position + 1)
        low_at = low - first_row + side
        high_at = high - first_row + side
        window = jnp.minimum(lax.div(low_at, jnp.int32(16)) * 16, rows + 2 * side - WINDOW)
        window = pl.multiple_of(jnp.maximum(window, 0), 16)
        tile_from = lax.div(jnp.maximum(low - first_row, 0), jnp.int32(TILE))
        tile_to = lax.div(jnp.minimum(high - first_row, rows) + TILE - 1, jnp.int32(TILE))
        body(low_at, high_at, window, tile_from, tile_to)
        return high

    lax.while_loop(lambda position: position < first_row + rows, step, first_row)


def two_heads(block):
    lane = lax.broadcasted_iota(jnp.int32, block.shape, 1)
    zero = jnp.zeros_like(block)
    return jnp.concatenate(
        [jnp.where(lane < DH, block, zero), jnp.where(lane < DH, zero, block)], axis=0
    )


def own_blocks(product):
    return jnp.concatenate([product[:DH, :TILE], product[DH:, TILE:]], axis=0).T


def key_bias(low_at, high_at, window):
    row = lax.broadcasted_iota(jnp.int32, (WINDOW, 2 * TILE), 0) + window
    return jnp.where((row >= low_at) & (row < high_at), 0.0, masked_score)


def rows_inside(tile, low_at, high_at, side, shape, dim):
    at = lax.broadcasted_iota(jnp.int32, shape, dim)
    if dim == 1:
        at = at & (TILE - 1)
    at = at + (tile * TILE + side)
    return (at >= low_at) & (at < high_at)


NT = (((1,), (1,)), ((), ()))
NN = (((1,), (0,)), ((), ()))


def mul(left, right, dims=NN):
    return lax.dot_general(left, right, dims, preferred_element_type=f32)


def slots_to_rows(slots, shard, store):
    total, _, columns = slots.shape
    step = min(total, 8)
    for d in range(0, total, step):
        block = slots[d : d + step].astype(f32).reshape(step * shard, columns)
        store(slice(d * shard, (d + step) * shard), block.astype(bf16))


def forward_kernel(plan, lengths_ref, first_ref, me_ref, *refs):
    sequences, side, taken, dests, shard = plan
    outer_ref, states_ref, partner_ref, edge_ref = refs[:4]
    pieces, refs = (refs[4 : 4 + taken], refs[4 + taken : 4 + 2 * taken]), refs[4 + 2 * taken :]
    (q_ref, k_ref, v_ref, o_ref, stat_ref, weight_ref, reach_ref, vec_ref) = refs[:8]
    bias_ref, vt_ref, slots_a, slots_b, small_ref, in_sem = refs[8:]
    rows, width = states_ref.shape
    half, thin = width // 2, edge_ref.shape[0]
    pair = pl.program_id(0)
    me, head = me_ref[0], me_ref[1]

    @pl.when(pair == 0)
    def _():
        slots = len(dests[0][0])
        copies = [
            pltpu.make_async_copy(
                pieces[n][a].at[j], target.at[dests[n][a][j] ^ me], in_sem.at[n, a * slots + j]
            )
            for n, target in enumerate((slots_a, slots_b))
            for a in range(taken)
            for j in range(slots)
        ]
        for copy in copies:
            copy.start()

        @pl.when(head == 0)
        def _():
            reach_ref[:side, :] = outer_ref[...]
            reach_ref[side + rows : side + 2 * rows, :] = partner_ref[...]
            reach_ref[side + 2 * rows :, :] = edge_ref[...]

        @pl.when(head != 0)
        def _():
            reach_ref[:thin, :] = edge_ref[...]
            reach_ref[thin:side, :] = partner_ref[...]
            reach_ref[side + rows :, :] = outer_ref[...]

        reach_ref[side : side + rows, :] = states_ref[...]
        for copy in copies:
            copy.wait()

        def store(offset):
            def put(at, block):
                for n in range(3):
                    to = n * width + offset
                    weight_ref[at, to : to + half] = block[:, n * half : (n + 1) * half]
                if block.shape[1] > 3 * half:
                    small_ref[at, :] = block[:, 3 * half :]

            return put

        slots_to_rows(slots_a, shard, store(0))
        slots_to_rows(slots_b, shard, store(half))
        vec_ref[...] = small_ref[...].astype(f32).T[: vec_ref.shape[0]]

    stat_ref[...] = jnp.zeros_like(stat_ref)
    o_ref[...] = jnp.zeros_like(o_ref)
    lanes = [pl.ds(pl.multiple_of(pair * PAIR + n * width, PAIR), PAIR) for n in range(3)]
    queries = mul(states_ref[...], weight_ref[:, lanes[0]]) + vec_ref[0:1, lanes[0]]
    q_ref[...] = queries.astype(bf16) * jnp.asarray(score_scale, bf16)
    both_weight = jnp.concatenate([weight_ref[:, lanes[1]], weight_ref[:, lanes[2]]], axis=1)
    both = mul(reach_ref[...], both_weight)
    k_ref[...] = both[:, :PAIR].astype(bf16)
    v_ref[...] = (both[:, PAIR:] + vec_ref[1:2, lanes[0]]).astype(bf16)

    def segment(low_at, high_at, window, tile_from, tile_to):
        bias_ref[...] = key_bias(low_at, high_at, window)
        keys_at = pl.ds(window, WINDOW)
        vt_ref[...] = v_ref[keys_at, :].T

        def one(tile, carry):
            at = pl.ds(pl.multiple_of(tile * TILE, TILE), TILE)
            wide = pl.ds(pl.multiple_of(tile * 2 * TILE, 2 * TILE), 2 * TILE)
            queries = two_heads(q_ref[at, :])
            scores = mul(k_ref[keys_at, :], queries, NT) + bias_ref[...]
            top = jnp.max(scores, axis=0, keepdims=True)
            raised = jnp.exp(scores - top)
            inverse = 1.0 / jnp.sum(raised, axis=0, keepdims=True)
            weights = (raised * inverse).astype(bf16)
            mixed = own_blocks(mul(vt_ref[...], weights)).astype(bf16)
            inside = rows_inside(tile, low_at, high_at, side, (TILE, PAIR), 0)
            o_ref[at, :] = jnp.where(inside, mixed, o_ref[at, :])
            there = rows_inside(tile, low_at, high_at, side, (1, 2 * TILE), 1)
            stat_ref[0, 0:1, wide] = jnp.where(there, top, stat_ref[0, 0:1, wide])
            stat_ref[0, 1:2, wide] = jnp.where(there, inverse, stat_ref[0, 1:2, wide])
            return carry

        lax.fori_loop(tile_from, tile_to, one, 0)

    over_segments(lengths_ref, sequences, first_ref[0], rows, side, segment)


def backward_kernel(
    plan,
    lengths_ref,
    first_ref,
    me_ref,
    q_ref,
    k_ref,
    v_ref,
    g_ref,
    stat_ref,
    reach_ref,
    *refs,
):
    sequences, side, held, slot_of, shard = plan
    sums_in, dq_ref, dk_ref, dv_ref = refs[:4]
    outs = (refs[4 : 4 + held], refs[4 + held : 4 + 2 * held])
    (bias_ref, kt_ref, dq_acc, dk_acc, dv_acc, reach_t, slots_ref, small_ref, sem) = refs[4 + 2 * held :]
    rows = q_ref.shape[0]
    pair, pairs = pl.program_id(0), pl.num_programs(0)
    me = me_ref[0]
    total, width = slots_ref.shape[1], reach_ref.shape[1]
    half = width // 2

    @pl.when(pair == 0)
    def _():
        reach_t[...] = reach_ref[...].T
        small_ref[...] = jnp.zeros_like(small_ref)

    dq_acc[...] = jnp.zeros_like(dq_acc)
    dk_acc[...] = jnp.zeros_like(dk_acc)
    dv_acc[...] = jnp.zeros_like(dv_acc)

    def segment(low_at, high_at, window, tile_from, tile_to):
        bias_ref[...] = key_bias(low_at, high_at, window)
        keys_at = pl.ds(window, WINDOW)
        kt_ref[...] = k_ref[keys_at, :].T

        def one(tile, carry):
            at = pl.ds(pl.multiple_of(tile * TILE, TILE), TILE)
            wide = pl.ds(pl.multiple_of(tile * 2 * TILE, 2 * TILE), 2 * TILE)
            queries = two_heads(q_ref[at, :])
            grads = two_heads(g_ref[at, :])
            there = rows_inside(tile, low_at, high_at, side, (1, 2 * TILE), 1)
            top = jnp.where(there, stat_ref[0, 0:1, wide], -masked_score)
            inverse = jnp.where(there, stat_ref[0, 1:2, wide], 0.0)
            scores = mul(k_ref[keys_at, :], queries, NT) + bias_ref[...]
            probs = jnp.exp(scores - top) * inverse
            grad_probs = mul(v_ref[keys_at, :], grads, NT)
            shared = jnp.sum(probs * grad_probs, axis=0, keepdims=True)
            grad_scores = (probs * (grad_probs - shared)).astype(bf16)
            dv_acc[keys_at, :] += mul(probs.astype(bf16), grads)
            dk_acc[keys_at, :] += mul(grad_scores, queries)
            dq_acc[at, :] += own_blocks(mul(kt_ref[...], grad_scores))
            return carry

        lax.fori_loop(tile_from, tile_to, one, 0)

    over_segments(lengths_ref, sequences, first_ref[0], rows, side, segment)
    dq = (dq_acc[...] * score_scale).astype(bf16)
    dkv = jnp.concatenate([dk_acc[...].astype(bf16), dv_acc[...].astype(bf16)], axis=1)
    dq_ref[...] = dq
    dk_ref[...] = dkv[:, :PAIR]
    dv_ref[...] = dkv[:, PAIR:]
    here = pl.ds(pl.multiple_of(pair * PAIR, PAIR), PAIR)
    small_ref[0:1, here] = jnp.sum(dq.astype(f32), axis=0, keepdims=True)
    small_ref[1:2, here] = jnp.sum(dkv[:, PAIR:].astype(f32), axis=0, keepdims=True)
    which = lax.div(pair, lax.div(pairs, 2))
    inner = lax.rem(pair, lax.div(pairs, 2)) * PAIR
    lanes = [pl.ds(pl.multiple_of(inner + n * half, PAIR), PAIR) for n in range(3)]

    def put(to, value, columns):
        for i in range(total):
            slot = slot_of(to, i ^ me) if total > 1 else 0
            slots_ref[to, slot, :, columns] = value[i * shard : (i + 1) * shard].astype(bf16)

    own_t = reach_ref[side : side + rows, :]
    grad_q = mul(own_t, dq, (((0,), (0,)), ((), ())))
    grad_w = mul(reach_t[...], dkv)
    for to in range(2):

        @pl.when(which == to)
        def _():
            put(to, grad_q, lanes[0])
            put(to, grad_w[:, :PAIR], lanes[1])
            put(to, grad_w[:, PAIR:], lanes[2])

    each = total // held
    copies = lambda to: [
        pltpu.make_async_copy(
            slots_ref.at[to, pl.ds(a * each, each), :, pl.ds(0, 3 * half + to * TILE)],
            outs[to][a],
            sem.at[to, a],
        )
        for a in range(held)
    ]

    @pl.when(pair == lax.div(pairs, 2))
    def _():
        for copy in copies(0):
            copy.start()

    @pl.when(pair == pairs - 1)
    def _():
        count = sums_in.shape[0]
        small_ref[2 : 2 + count, :] = sums_in[...]
        put(1, small_ref[...].T, pl.ds(3 * half, TILE))
        for copy in copies(1):
            copy.start()
        for copy in (*copies(0), *copies(1)):
            copy.wait()


def pack_kernel(shard, weight_ref, output_ref, upward_ref, *refs):
    *vector_refs, lead_ref, mixed_ref, rows_ref = refs
    rows_ref[...] = jnp.zeros_like(rows_ref)
    row = 0
    for ref in vector_refs:
        values = ref[...].astype(f32).reshape(1, ref.shape[0])
        for at in range(0, ref.shape[0], shard):
            rows_ref[row : row + 1, :shard] = values[:, at : at + shard]
            row += 1
    width = output_ref.shape[1]
    half = width // 2
    for n in range(3):
        for to in range(2):
            at = (3 * to + n) * half
            lead_ref[:, at : at + half] = weight_ref[:, n * width + to * half :][:, :half]
    lead_ref[:, 3 * width :] = rows_ref[...].T[:shard].astype(bf16)
    mixed_ref[:, :width] = output_ref[...]
    mixed_ref[:, width:] = upward_ref[...]


def pack(weight, output, upward, vectors):
    shard = weight.shape[0]
    shape = jax.ShapeDtypeStruct
    return pl.pallas_call(
        functools.partial(pack_kernel, shard),
        name="pack",
        out_shape=(
            shape((shard, weight.shape[1] + 128), bf16),
            shape((shard, output.shape[1] + upward.shape[1]), bf16),
        ),
        in_specs=[pl.BlockSpec(memory_space=pltpu.VMEM)] * (3 + len(vectors)),
        out_specs=[pl.BlockSpec(memory_space=pltpu.VMEM)] * 2,
        scratch_shapes=[pltpu.VMEM((128, 128), f32)],
    )(weight, output, upward, *vectors)


def attention_forward(lengths, first, me_head, rows_of, pieces, side, dests):
    outer, states, partner, edge = rows_of
    rows, features = states.shape
    wide = rows + 2 * side
    taken, (slots, shard, columns) = len(pieces[0]), pieces[0][0].shape
    pairs = features // PAIR
    whole = lambda *shape: pl.BlockSpec(shape, lambda h, *_: (0,) * len(shape))
    column = lambda n: pl.BlockSpec((n, PAIR), lambda h, *_: (0, h))
    anywhere = pl.BlockSpec(memory_space=pl.ANY)
    shape = jax.ShapeDtypeStruct
    plan = (lengths.shape[0], side, taken, dests, shard)
    return pl.pallas_call(
        functools.partial(forward_kernel, plan),
        name="attention_forward",
        out_shape=(
            shape((rows, features), bf16),
            shape((wide, features), bf16),
            shape((wide, features), bf16),
            shape((rows, features), bf16),
            shape((pairs, 8, 2 * rows), f32),
            shape((features, 3 * features), bf16),
            shape((wide, features), bf16),
            shape((16, features), f32),
        ),
        grid_spec=pltpu.PrefetchScalarGridSpec(
            num_scalar_prefetch=3,
            grid=(pairs,),
            in_specs=[*[whole(*r.shape) for r in rows_of], *[anywhere] * (2 * taken)],
            out_specs=[
                column(rows),
                column(wide),
                column(wide),
                column(rows),
                pl.BlockSpec((1, 8, 2 * rows), lambda h, *_: (h, 0, 0)),
                whole(features, 3 * features),
                whole(wide, features),
                whole(16, features),
            ],
            scratch_shapes=[
                pltpu.VMEM((WINDOW, 2 * TILE), f32),
                pltpu.VMEM((PAIR, WINDOW), bf16),
                *[pltpu.VMEM((taken * slots,) + half[0].shape[1:], bf16) for half in pieces],
                pltpu.VMEM((features, columns - 3 * features // 2), bf16),
                pltpu.SemaphoreType.DMA((2, taken * slots)),
            ],
        ),
        compiler_params=pltpu.CompilerParams(vmem_limit_bytes=48 * 2**20),
    )(lengths, first, me_head, *rows_of, *pieces[0], *pieces[1])


def attention_backward(
    lengths, first, me, queries, keys, values, grads, stats, reach, side, shard, held, backs, sums
):
    rows, features = queries.shape
    wide = keys.shape[0]
    pairs = features // PAIR
    total = features // shard if held > 1 else 1
    per = shard if held > 1 else features
    columns = 3 * features // 2
    column = lambda n: pl.BlockSpec((n, PAIR), lambda h, *_: (0, h))
    whole = lambda *shape: pl.BlockSpec(shape, lambda h, *_: (0,) * len(shape))
    anywhere = pl.BlockSpec(memory_space=pl.ANY)
    shape = jax.ShapeDtypeStruct
    slot_of = [exchange_slot(back) for back in backs]
    place = lambda to, diff: slot_of[to](diff)
    return pl.pallas_call(
        functools.partial(backward_kernel, (lengths.shape[0], side, held, place, per)),
        name="attention_backward",
        out_shape=(
            shape((rows, features), bf16),
            shape((wide, features), bf16),
            shape((wide, features), bf16),
            *[shape((total // held, per, columns), bf16)] * held,
            *[shape((total // held, per, columns + TILE), bf16)] * held,
        ),
        grid_spec=pltpu.PrefetchScalarGridSpec(
            num_scalar_prefetch=3,
            grid=(pairs,),
            in_specs=[
                column(rows),
                column(wide),
                column(wide),
                column(rows),
                pl.BlockSpec((1, 8, 2 * rows), lambda h, *_: (h, 0, 0)),
                whole(wide, features),
                whole(*sums.shape),
            ],
            out_specs=[column(rows), column(wide), column(wide), *[anywhere] * (2 * held)],
            scratch_shapes=[
                pltpu.VMEM((WINDOW, 2 * TILE), f32),
                pltpu.VMEM((PAIR, WINDOW), bf16),
                pltpu.VMEM((rows, PAIR), f32),
                pltpu.VMEM((wide, PAIR), f32),
                pltpu.VMEM((wide, PAIR), f32),
                pltpu.VMEM((features, wide), bf16),
                pltpu.VMEM((2, total, per, columns + TILE), bf16),
                pltpu.VMEM((TILE, features), f32),
                pltpu.SemaphoreType.DMA((2, held)),
            ],
        ),
        compiler_params=pltpu.CompilerParams(vmem_limit_bytes=56 * 2**20),
    )(lengths, first, me, queries, keys, values, grads, stats, reach, sums)


TN = (((0,), (0,)), ((), ()))


def row_mean(value):
    return jnp.mean(value, axis=-1, keepdims=True)


def column_sum(value):
    return jnp.sum(value, axis=0, keepdims=True)


def normalize(summed):
    centered = summed - row_mean(summed)
    inverse_std = lax.rsqrt(row_mean(centered * centered) + norm_eps)
    return centered * inverse_std, inverse_std


def normalize_back(grad, normed, inverse_std):
    return inverse_std * (grad - row_mean(grad) - normed * row_mean(grad * normed))


def feed_kernel(plan, *refs):
    taken, held, in_dest, out_slot, shard, deep = plan
    me_ref, att_ref, states_ref, cot_ref, vec_ref, upb_ref = refs[:6]
    mixed_in, down_in = refs[6 : 6 + taken], refs[6 + taken : 6 + 2 * taken]
    at = 6 + 2 * taken
    result_ref, res_ref, gatt_ref, small_ref = refs[at : at + 4]
    mixed_out, down_out = refs[at + 4 : at + 4 + held], refs[at + 4 + held : at + 4 + 2 * held]
    at += 4 + 2 * held
    (wslot, wmix, wdown, act, slope, gmix, gdown, acc, in_sem, out_sem) = refs[at:]
    me = me_ref[0]
    width = states_ref.shape[1]
    hidden = wdown.shape[0]
    slots = len(in_dest[0][0])

    def copies_in():
        for a in range(taken):
            for j in range(slots):
                dest = in_dest[0][a][j] ^ me
                yield pltpu.make_async_copy(
                    mixed_in[a].at[j], wslot.at[dest], in_sem.at[0, a * slots + j]
                )

    def copies_down():
        for a in range(taken):
            for j in range(slots):
                dest = pl.multiple_of((in_dest[1][a][j] ^ me) * deep, 16)
                yield pltpu.make_async_copy(
                    down_in[a].at[j], wdown.at[pl.ds(dest, deep), :], in_sem.at[1, a * slots + j]
                )

    for copy in copies_in():
        copy.start()
    for copy in copies_down():
        copy.start()
    for copy in copies_in():
        copy.wait()
    total = taken * slots

    def store(at, block):
        wmix[at, :] = block

    slots_to_rows(wslot, shard, store)

    bias_out, bias_down, gain_one, shift_one, gain_two, shift_two = (
        vec_ref[i : i + 1, :] for i in range(2, 8)
    )
    branch = mul(att_ref[...], wmix[:, :width]) + bias_out
    normed_one, scale_one = normalize(states_ref[...].astype(f32) + branch)
    first_norm = normed_one * gain_one + shift_one
    inner = first_norm.astype(bf16)
    for copy in copies_down():
        copy.wait()
    chunks = range(0, hidden, width)
    for c in chunks:
        lifted = mul(inner, wmix[:, width + c : 2 * width + c]) + upb_ref[:, c : c + width]
        phi_sum = 0.5 * (1.0 + lax.erf(lifted * root_half))
        active = (lifted * phi_sum).astype(bf16)
        act[:, c : c + width] = active
        slope[:, c : c + width] = phi_sum + lifted * (
            inverse_root_two_pi * jnp.exp(-0.5 * lifted * lifted)
        )
        part = mul(active, wdown[c : c + width, :])
        acc[...] = part if c == 0 else acc[...] + part
    normed_two, scale_two = normalize(first_norm + (acc[...] + bias_down))
    result_ref[...] = (normed_two * gain_two + shift_two).astype(bf16)

    cot = cot_ref[...].astype(f32)
    small_ref[4:5, :] = column_sum(cot * normed_two)
    small_ref[5:6, :] = column_sum(cot)
    grad_mid = normalize_back(cot * gain_two, normed_two, scale_two)
    grad_down = grad_mid.astype(bf16)
    small_ref[1:2, :] = column_sum(grad_down.astype(f32))

    def put(target, order, value, first, per):
        for i in range(value.shape[0] // per):
            rows = value[i * per : (i + 1) * per]
            yield out_slot(order, (first + i) ^ me if total > 1 else 0), rows

    def copies_out(order, source, targets, sem):
        for a in range(held):
            yield pltpu.make_async_copy(
                source.at[pl.ds(a * (total // held), total // held)], targets[a], out_sem.at[sem, a]
            )

    inner_t = inner.T
    for c in chunks:
        active = act[:, c : c + width]
        grad_active = mul(grad_down, wdown[c : c + width, :], NT)
        grad_lift = (grad_active * slope[:, c : c + width]).astype(bf16)
        small_ref[8 + c // width : 9 + c // width, :] = column_sum(grad_lift.astype(f32))
        grad_w = mul(active, grad_down, TN).astype(bf16)
        for slot, rows in put(gdown, 1, grad_w, c // deep, min(deep, width)):
            if total > 1:
                gdown[slot] = rows
            else:
                gdown[slot, c : c + width, :] = rows
        grad_w = mul(inner_t, grad_lift)
        for slot, rows in put(gmix, 0, grad_w, 0, shard):
            gmix[slot, :, width + c : 2 * width + c] = rows.astype(bf16)
        part = mul(grad_lift, wmix[:, width + c : 2 * width + c], NT)
        acc[...] = part if c == 0 else acc[...] + part
    for copy in copies_out(1, gdown, down_out, 1):
        copy.start()
    grad_first = acc[...] + grad_mid
    small_ref[2:3, :] = column_sum(grad_first * normed_one)
    small_ref[3:4, :] = column_sum(grad_first)
    grad_residual = normalize_back(grad_first * gain_one, normed_one, scale_one)
    res_ref[...] = grad_residual
    grad_branch = grad_residual.astype(bf16)
    small_ref[0:1, :] = column_sum(grad_branch.astype(f32))
    grad_w = mul(att_ref[...], grad_branch, TN)
    for slot, rows in put(gmix, 0, grad_w, 0, shard):
        gmix[slot, :, :width] = rows.astype(bf16)
    for copy in copies_out(0, gmix, mixed_out, 0):
        copy.start()
    gatt_ref[...] = mul(grad_branch, wmix[:, :width], NT).astype(bf16)
    small_ref[6:8, :] = jnp.zeros((2, width), f32)
    small_ref[12:, :] = jnp.zeros((small_ref.shape[0] - 12, width), f32)
    for copy in (*copies_out(1, gdown, down_out, 1), *copies_out(0, gmix, mixed_out, 0)):
        copy.wait()


def exchange_slot(bits):
    def slot(diff):
        found = jnp.int32(0)
        for at, bit in enumerate(reversed(bits)):
            found = found + (((diff & bit) != 0).astype(jnp.int32) << at)
        return found

    return slot


def feed_forward(me, attended, states, cotangent, vectors, up_bias, mixed, down, dests, backs):
    rows, width = states.shape
    taken, (slots, shard, columns) = len(mixed), mixed[0].shape
    held = min(taken, 2)
    deep = down[0].shape[1]
    total = taken * slots
    hidden = total * deep
    slot_of = [exchange_slot(back) for back in backs]
    place = lambda order, diff: slot_of[order](diff) if held > 1 else 0
    plan = (taken, held, dests, place, shard, deep)
    whole = pl.BlockSpec(memory_space=pltpu.VMEM)
    anywhere = pl.BlockSpec(memory_space=pl.ANY)
    shape = jax.ShapeDtypeStruct
    return pl.pallas_call(
        functools.partial(feed_kernel, plan),
        name="feed_forward",
        out_shape=(
            shape((rows, width), bf16),
            shape((rows, width), f32),
            shape((rows, width), bf16),
            shape((16, width), f32),
            *[shape((total // held, shard, columns), bf16)] * held,
            *[shape((total // held, deep, width), bf16)] * held,
        ),
        in_specs=[pl.BlockSpec(memory_space=pltpu.SMEM), *[whole] * 5, *[anywhere] * (2 * taken)],
        out_specs=[*[whole] * 4, *[anywhere] * (2 * held)],
        scratch_shapes=[
            pltpu.VMEM((total, shard, columns), bf16),
            pltpu.VMEM((total * shard, columns), bf16),
            pltpu.VMEM((hidden, width), bf16),
            pltpu.VMEM((rows, hidden), bf16),
            pltpu.VMEM((rows, hidden), f32),
            pltpu.VMEM((total, shard, columns), bf16),
            pltpu.VMEM((total, deep, width), bf16),
            pltpu.VMEM((rows, width), f32),
            pltpu.SemaphoreType.DMA((2, total)),
            pltpu.SemaphoreType.DMA((2, held)),
        ],
        compiler_params=pltpu.CompilerParams(vmem_limit_bytes=60 * 2**20),
    )(me, attended, states, cotangent, vectors, up_bias, *mixed, *down)


def local(
    hidden_states,
    owner_rows,
    lengths,
    attention_weight,
    output_weight,
    upward_weight,
    downward_weight,
    query_bias,
    value_bias,
    output_bias,
    upward_bias,
    downward_bias,
    first_gain,
    first_shift,
    second_gain,
    second_shift,
    output_cotangent,
):
    rows, width = hidden_states.shape
    heads_axis, blocks_axis = lax.axis_size("head"), lax.axis_size("blk")
    count = heads_axis * blocks_axis
    me = lax.axis_index(AXES)
    head, blk = lax.axis_index("head"), lax.axis_index("blk")
    first = ((blk * heads_axis + head) * rows).astype(jnp.int32).reshape(1)
    bits = [1 << b for b in range((count - 1).bit_length())]
    far = tuple(b for b in bits if b not in (1, 2, blocks_axis))[::-1]
    near_y, near_x, core = (2,), (blocks_axis,), (1,)
    apart = [(b,) for b in far]
    lead_rounds = ([far, near_x, near_y, core], [far, near_y, near_x, core])
    follow_rounds = (
        [far, near_x, near_y, core],
        [near_y, *apart, near_x, core],
    )
    back_rounds = (
        [core, near_y, near_x, far[::-1]],
        [core, near_x, far[::-1], near_y],
        [core, near_x, near_y, far[::-1]],
        [core, near_y, near_x, far[::-1]],
    )
    back_bits = [[b for r in rounds for b in r] for rounds in back_rounds]
    order = bits[::-1]
    shard = attention_weight.shape[0]
    slotted = shard % 8 == 0
    half = width // 2
    def along(block, by_first, by_second):
        pairs = [
            (h * blocks_axis + b, h * blocks_axis + b + by)
            for h, by in ((0, by_first), (1, by_second))
            for b in range(blocks_axis)
            if 0 <= b + by < blocks_axis
        ]
        return lax.ppermute(block, AXES, pairs)

    slot_index = owner_rows % rows
    pick = (slot_index[None, :] == jnp.arange(rows, dtype=jnp.int32)[:, None]).astype(bf16)
    states = jnp.dot(pick, hidden_states, preferred_element_type=f32).astype(bf16)
    cotangent = jnp.dot(pick, output_cotangent, preferred_element_type=f32).astype(bf16)

    thin = -(-(SEG_ROWS - 1 - rows) // 16) * 16
    side = rows + thin
    partner = swap(states, blocks_axis, count)
    is_first = head == 0
    sent = jnp.where(
        is_first,
        jnp.concatenate([states[rows - thin :], partner], axis=0),
        jnp.concatenate([partner, states[:thin]], axis=0),
    )
    outer = along(sent, 1, -1)
    edge = along(jnp.where(is_first, states[:thin], states[rows - thin :]), -1, 1)
    rows_of = (outer, states, partner, edge)

    small = (
        query_bias,
        value_bias,
        output_bias,
        downward_bias,
        first_gain,
        first_shift,
        second_gain,
        second_shift,
        upward_bias,
    )
    extra = upward_bias.shape[0] // shard
    lead, mixed = pack(attention_weight, output_weight, upward_weight, small)
    cut = 6 * half
    me_of = me.astype(jnp.int32).reshape(1)
    me_head = jnp.stack([me, head]).astype(jnp.int32)
    if slotted:
        lead_all = Spread(lead[None], lead_rounds[0], count)
        lead_all.start()
        follow = [
            Spread(block[None], rounds, count)
            for block, rounds in zip((mixed, downward_weight), follow_rounds)
        ]
        follow[1].start()
        held = lead_all.finish()
        lead_a = Spread(
            jnp.concatenate([held[..., : cut // 2], held[..., cut:]], axis=-1),
            lead_rounds[0][1:],
            count,
        )
        lead_b = Spread(held[..., cut // 2 : cut], lead_rounds[1][1:], count)
        leads = (lead_a, lead_b)
        [chain.start() for chain in leads]
        follow[0].held = after(follow[0].held, held)
        follow[0].start()
        token = [follow[1].finish([held])]
        follow[1].start()
        token = [*[chain.finish(token) for chain in leads], sent]
        [chain.start_two() for chain in leads]
        token = [chain.finish(token) for chain in follow]
        [chain.start() for chain in follow]
        token = [x for chain in leads for x in chain.finish_two(token)]
        token = [chain.finish([*token, outer, edge]) for chain in follow]
        [chain.start_two() for chain in follow]
        pieces = [chain.parts for chain in leads]
        pieces[0][0] = after(pieces[0][0], *token)
        lead_places = [piece_places(rounds) for rounds in lead_rounds]
    else:
        full = gathered(lead, order, count, me)
        pieces = [
            [jnp.concatenate([full[:, : cut // 2], full[:, cut:]], axis=1)[None]],
            [full[None, :, cut // 2 : cut]],
        ]
        lead_places = [[[0]], [[0]]]
    queries, keys, values, attended, stats, weight_full, reach, vectors = attention_forward(
        lengths, first, me_head, rows_of, pieces, side, lead_places
    )
    if slotted:
        [chain.finish_two([attended]) for chain in follow]
        follow_parts = [chain.parts for chain in follow]
        follow_places = [piece_places(rounds) for rounds in follow_rounds]
    else:
        follow_parts = [
            [gathered(mixed, order, count, me)[None]],
            [gathered(downward_weight, order, count, me)[None]],
        ]
        follow_places = [[[0]], [[0]]]
    bias_upward = (
        vectors[8 : 8 + extra].reshape(extra, count, shard).transpose(1, 0, 2).reshape(1, -1)
    )

    outs = feed_forward(
        me_of,
        attended,
        states,
        cotangent,
        vectors,
        bias_upward,
        *follow_parts,
        follow_places,
        back_bits[:2],
    )
    result, grad_residual, grad_attended, small_sums = outs[:4]
    gradients = outs[4:]
    sums = jnp.concatenate(
        [
            small_sums[:6],
            small_sums[8 : 8 + extra].reshape(count, extra, shard).transpose(1, 0, 2).reshape(extra, width),
        ]
    )
    if slotted:
        group = [
            Gathering(*pair, rounds, count)
            for pair, rounds in zip((gradients[:2], gradients[2:]), back_rounds)
        ]
        token = [x for chain in group for x in chain.advance()]
        grad_attended = after(grad_attended, *token)

    grad_query, grad_key, grad_value, *slots = attention_backward(
        lengths,
        first,
        me_of,
        queries,
        keys,
        values,
        grad_attended,
        stats,
        reach,
        side,
        shard,
        2 if slotted else 1,
        back_bits[2:],
        sums,
    )

    step = lambda chains, token: [x for chain in chains for x in chain.advance(token)]
    if slotted:
        arrived = [x for chain in group for x in chain.arrive()]
        grad_query, grad_key, grad_value, *slots = tied(
            (grad_query, grad_key, grad_value, *slots), arrived
        )
        token = step(group, [grad_query])
        halves = [
            Gathering(*pair, rounds, count)
            for pair, rounds in zip((slots[:2], slots[2:]), back_rounds[2:])
        ]
        (grad_key,) = tied([grad_key], token)

    def input_rows(select):
        return sum(
            jnp.einsum(
                "rc,dc->rd",
                select(grad),
                weight_full[:, n * width : (n + 1) * width],
                preferred_element_type=f32,
            )
            for n, grad in ((1, grad_key), (2, grad_value))
        )

    grad_outer = input_rows(lambda g: jnp.where(is_first, g[:side], g[side + rows :]))
    grad_outer = grad_outer.astype(bf16)
    back = along(grad_outer, -1, 1)
    if slotted:
        token = step(halves, [grad_outer])
        (grad_key,) = tied([grad_key], token)
    grad_rest = input_rows(
        lambda g: jnp.where(
            is_first, g[side + rows :], jnp.concatenate([g[thin:side], g[:thin]], axis=0)
        )
    )
    back_edge = along(grad_rest[rows:].astype(bf16), 1, -1)
    if slotted:
        token = step(group, [grad_rest])
        (back,) = tied([back], token)
    back_own = jnp.where(is_first, back[:thin], back[rows:]).astype(f32)
    back_partner = jnp.where(is_first, back[thin:], back[:rows])
    grad_near = (grad_rest[:rows] + back_partner.astype(f32)).astype(bf16)
    back_near = swap(grad_near, blocks_axis, count)
    if slotted:
        (grad_key, grad_query, result) = tied([grad_key, grad_query, result], [grad_near])
    middle = (
        input_rows(lambda g: g[side : side + rows])
        + jnp.einsum("rc,dc->rd", grad_query, weight_full[:, :width], preferred_element_type=f32)
        + grad_residual
    )
    if slotted:
        token = step(halves, [middle])
        (result,) = tied([result], token)
    layer_output = jnp.take(result, slot_index, axis=0)
    if slotted:
        token = step(group, [layer_output])
        token = step(halves, token)
        (back_near,) = tied([back_near], token)
    pad_low = lambda v: jnp.pad(v, ((0, rows - thin), (0, 0)))
    pad_high = lambda v: jnp.pad(v, ((rows - thin, 0), (0, 0)))
    back_edge = back_edge.astype(f32)
    grad_input = (
        middle
        + back_near.astype(f32)
        + jnp.where(
            is_first, pad_high(back_own) + pad_low(back_edge), pad_low(back_own) + pad_high(back_edge)
        )
    )
    grad_hidden = jnp.take(grad_input, slot_index, axis=0)

    if slotted:
        step(halves, [grad_hidden])
        out_mixed, out_downward, out_a, out_b = (c.total for c in (*group, *halves))
    else:
        by_device = lambda grad: grad.reshape((count, grad.size // grad.shape[-1] // count, -1))
        out_mixed = reduced(by_device(gradients[0]), order, count, me)
        out_downward = reduced(by_device(gradients[1]), order, count, me)
        out_a = reduced(by_device(slots[0]), order, count, me)
        out_b = reduced(by_device(slots[1]), order, count, me)
    out_triple = jnp.concatenate(
        [o[:, n * half : (n + 1) * half] for n in range(3) for o in (out_a, out_b)], axis=1
    )
    summed = out_b[:, 3 * half :].T
    (
        out_query,
        out_value,
        out_output,
        out_down_bias,
        out_gain_one,
        out_shift_one,
        out_gain_two,
        out_shift_two,
    ) = [summed[i] for i in range(8)]
    out_up_bias = summed[8 : 8 + extra].reshape(-1)
    return (
        layer_output,
        grad_hidden,
        out_triple,
        out_mixed[:, :width],
        out_mixed[:, width:],
        out_downward,
        out_query,
        out_value,
        out_output,
        out_up_bias,
        out_down_bias,
        out_gain_one,
        out_shift_one,
        out_gain_two,
        out_shift_two,
    )


def solution(mesh):
    matrix, vector = P(AXES, None), P(AXES)
    return jax.shard_map(
        local,
        mesh=mesh,
        in_specs=(matrix, vector, P(), *[matrix] * 4, *[vector] * 9, matrix),
        out_specs=(*[matrix] * 6, *[vector] * 9),
        check_vma=False,
    )
```

time: 366 us -> 340 us (0.929)
  Pallas kernels: 76.5 us -> 105 us
  local copies, waits for them, and re-layouts: 49.2 us -> 21.9 us
  matrix products: 29 us -> 9.49 us
  waiting for transfers between devices: 92.3 us -> 79.9 us
  other arithmetic: 28.6 us -> 32.3 us
    pallas_call x2 -> x3, Pallas kernels: 46 us -> 74.7 us  [the longest x1 36.9 us: attention_forward(): pl.pallas_call(functools.partial(forward_kernel, plan), name='attention_f...]
    dot_general x9 -> x7, matrix products: 26.8 us -> 7.42 us  [the longest x6 6.61 us: input_rows(): jnp.einsum('rc,dc->rd', select(grad), weight_full[:, n * width:(n + 1) *...]
    convert_element_type x14 -> x15, other arithmetic: 4.31 us -> 19.7 us  [the longest x12 18.6 us: advance(): add(slice(j * each, (j + 1) * each)).astype(bf16)]
    ppermute x47 -> x50, waiting for transfers between devices: 92 us -> 79.5 us  [swap(): return lax.ppermute(block, AXES, [(i, i ^ bit) for i in range(count)])]
    slice x18 -> x13, local copies, waits for them, and re-layouts: 14.4 us -> 3.01 us  [the longest x2 1.24 us: local(): g[thin:side]]
    reshape x12 -> x5, local copies, waits for them, and re-layouts: 6.91 us -> 1.65 us  [the longest x2 0.82 us: local(): vectors[8:8 + extra].reshape(extra, count, shard).transpose(1, 0, 2)]
    unnamed x96 -> x98, local copies, waits for them, and re-layouts: 5.22 us -> 10.2 us
    concatenate x6 -> x2, local copies, waits for them, and re-layouts: 6.5 us -> 1.69 us  [finish(): self.held = jnp.concatenate([self.held, *recvs], axis=0)]
  transfers between devices with their start and end apart: 51 -> 54, of which waited for: 23 -> 18; matrix products, arithmetic and copies ran while one was open for 26% -> 15% of each run, Pallas kernels for 13% -> 22%
where the time goes in v3:
time: 340 us; the launch traced here: 335 us
  Pallas kernels  105 us (31%)
  starting transfers between devices  83.9 us (25%)
  waiting for transfers between devices  79.9 us (24%)
  other arithmetic  32.3 us (9%)
  local copies, waits for them, and re-layouts  21.9 us (6%)
  matrix products  9.49 us (3%)
    ppermute x50, waiting for transfers between devices, swap(): return lax.ppermute(block, AXES, [(i, i ^ bit) for i in range(count)])  79.5 us
    ppermute x50, starting transfers between devices, swap(): return lax.ppermute(block, AXES, [(i, i ^ bit) for i in range(count)])  78.6 us
    pallas_call x1, Pallas kernels, attention_forward(): pl.pallas_call(functools.partial(forward_kernel, plan), name='attention_f...  36.9 us
    pallas_call x1, Pallas kernels, attention_backward(): pl.pallas_call(functools.partial(backward_kernel, (lengths.shape[0], side...  35.9 us
    pallas_call x1, Pallas kernels, feed_forward(): pl.pallas_call(functools.partial(feed_kernel, plan), name='feed_forward',...  30.6 us
    convert_element_type x12, other arithmetic, advance(): add(slice(j * each, (j + 1) * each)).astype(bf16)  18.6 us
    unnamed x98, local copies, waits for them, and re-layouts  10.2 us
  transfers between devices with their start and end apart: 54, of which 18 were waited for; matrix products, arithmetic and copies ran while one was open for 15% of the time, Pallas kernels for 22%

profile of v3, /device:TPU:0, one launch (start us, length us, event | category | flops | bytes accessed | tf_op | source)
XLA Modules:
  0.0 334.6 jit_solution(10554755781707436639)
XLA Ops:
  0.7 1.9 pack.1
  2.6 4.0 %collective-permute-start.3 = (bf16[1,24,2432]{2,1,0:T(8,128)(2,1)}, bf16[1,24,2432]{2,1,0:T(8,128)(2,1)S(1)}, u32[]{:S(2)}, u32[]{:S(2)}) collective-permute-start(bf16[1,24,2432]{2,1,0:T(8,128)(2,1)} %bitcast.27), channel_id=1, source_target_pairs={{0,8},{1,9},{2,10},{3,11},{4,12},{5,13},{6,14},{7,15},{8,0},{9,1},... | collective-permute-start | bytes 350216 | tf_op jit(solution)/shard_map/ppermute | solution.py:30
  6.6 1.6 collective-permute-start.4
  8.2 1.7 collective-permute-start.7
  11.3 1.6 collective-permute-start
  14.3 1.9 collective-permute-done.5
  16.4 2.5 collective-permute-start.10
  18.9 1.6 collective-permute-start.8
  20.5 1.6 constant_dynamic-update-slice_fusion.3
  23.7 1.6 collective-permute-start.6
  25.3 3.9 %collective-permute-done.11 = bf16[4,24,1152]{2,1,0:T(8,128)(2,1)S(1)} collective-permute-done((bf16[4,24,1152]{2,1,0:T(8,128)(2,1)S(1)}, bf16[4,24,1152]{2,1,0:T(8,128)(2,1)S(1)}, u32[]{:S(2)}, u32[]{:S(2)}) %collective-permute-start.11) | collective-permute-done | bytes 221216 | tf_op jit(solution)/shard_map/ppermute | solution.py:30
  29.8 5.1 %collective-permute-done.6 = bf16[4,24,1280]{2,1,0:T(8,128)(2,1)S(1)} collective-permute-done((bf16[4,24,1280]{2,1,0:T(8,128)(2,1)S(1)}, bf16[4,24,1280]{2,1,0:T(8,128)(2,1)S(1)}, u32[]{:S(2)}, u32[]{:S(2)}) %collective-permute-start.6) | collective-permute-done | bytes 245792 | tf_op jit(solution)/shard_map/ppermute | solution.py:30
  36.4 2.3 collective-permute-done.9
  44.8 14.6 %collective-permute-done.14 = bf16[2,96,768]{2,1,0:T(8,128)(2,1)S(1)} collective-permute-done((bf16[2,96,768]{2,1,0:T(8,128)(2,1)S(1)}, bf16[2,96,768]{2,1,0:T(8,128)(2,1)S(1)}, u32[]{:S(2)}, u32[]{:S(2)}) %collective-permute-start.14) | collective-permute-done | bytes 294944 | tf_op jit(solution)/shard_map/ppermute | solution.py:30
  60.8 6.8 %collective-permute-done.15.refs_9_ = bf16[8,24,1152]{2,1,0:T(8,128)(2,1)S(1)} collective-permute-done((bf16[8,24,1152]{2,1,0:T(8,128)(2,1)S(1)}, bf16[8,24,1152]{2,1,0:T(8,128)(2,1)S(1)}, u32[]{:S(2)}, u32[]{:S(2)}) %collective-permute-start.15) | collective-permute-done | bytes 442400 | tf_op jit(solution)/shard_map/ppermute | solution.py:30
  69.4 2.5 collective-permute-start.21
  71.9 9.0 %collective-permute-done.16 = bf16[4,96,768]{2,1,0:T(8,128)(2,1)S(1)} collective-permute-done((bf16[4,96,768]{2,1,0:T(8,128)(2,1)S(1)}, bf16[4,96,768]{2,1,0:T(8,128)(2,1)S(1)}, u32[]{:S(2)}, u32[]{:S(2)}) %collective-permute-start.16) | collective-permute-done | bytes 589856 | tf_op jit(solution)/shard_map/ppermute | solution.py:30
  86.8 36.9 %attention_forward.1 = (bf16[512,768]{1,0:T(8,128)(2,1)S(1)}, bf16[1568,768]{1,0:T(8,128)(2,1)}, bf16[1568,768]{1,0:T(8,128)(2,1)}, bf16[512,768]{1,0:T(8,128)(2...) custom-call(s32[4]{0:T(128)S(1)} %copy-done.6, ...), custom_call_target="tpu_custom_call" | custom-call | tf_op jit(solution)/shard_map/attention_forward/pallas_call | solution.py:459
  126.2 10.9 %collective-permute-start.23 = (bf16[8,24,3840]{2,1,0:T(8,128)(2,1)}, bf16[8,24,3840]{2,1,0:T(8,128)(2,1)S(1)}, u32[]{:S(2)}, u32[]{:S(2)}) collective-permute-start(bf16[8,24,3840]{2,1,0:T(8,128)(2,1)} %collective-permute-done.21.refs_7_), channel_id=1, source_target_pairs={{0,1},{1,0},{2,3},{3,2},{4,5},{5,4},{6,7},{7,6},{8,9},{9,8},{10,11... | collective-permute-start | bytes 4423688 | tf_op jit(solution)/shard_map/ppermute | solution.py:30
  140.0 3.6 %collective-permute-done.25.refs_12_ = bf16[8,96,768]{2,1,0:T(8,128)(2,1)S(1)} collective-permute-done((bf16[8,96,768]{2,1,0:T(8,128)(2,1)}, bf16[8,96,768]{2,1,0:T(8,128)(2,1)S(1)}, u32[]{:S(2)}, u32[]{:S(2)}) %collective-permute-start.25) | collective-permute-done | bytes 1179680 | tf_op jit(solution)/shard_map/ppermute | solution.py:30
  145.7 30.6 %feed_forward.1 = (bf16[512,768]{1,0:T(8,128)(2,1)}, f32[512,768]{1,0:T(8,128)}, bf16[512,768]{1,0:T(8,128)(2,1)}, f32[16,768]{1,0:T(8,128)}, bf16[16,24,3840]{2...) custom-call(s32[1]{0:T(128)} %bitcast.1.refs_0_.me_ref, ...), custom_call_target="tpu_custom_call" | custom-call | tf_op jit(solution)/shard_map/feed_forward/pallas_call | solution.py:718
  177.0 5.1 %collective-permute-done.27 = bf16[16,24,3840]{2,1,0:T(8,128)(2,1)S(1)} collective-permute-done((bf16[16,24,3840]{2,1,0:T(8,128)(2,1)}, bf16[16,24,3840]{2,1,0:T(8,128)(2,1)S(1)}, u32[]{:S(2)}, u32[]{:S(2)}) %collective-permute-start.27) | collective-permute-done | bytes 2949152 | tf_op jit(solution)/shard_map/ppermute | solution.py:30
  182.0 4.0 %add_convert_fusion = bf16[8,24,3840]{2,1,0:T(8,128)(2,1)} fusion(bf16[16,24,3840]{2,1,0:T(8,128)(2,1)S(1)} %collective-permute-done.27, bf16[16,24,3840]{2,1,0:T(8,128)(2,1)} %get-tuple-element.116), kind=kLoop, calls=%fused_computation.2 | loop fusion | flops 2949120 | bytes 4423680 | tf_op jit(solution)/shard_map/convert_element_type | solution.py:130
  186.1 1.6 add_convert_fusion.1
  187.9 3.9 %collective-permute-start.30 = (bf16[8,96,768]{2,1,0:T(8,128)(2,1)}, bf16[8,96,768]{2,1,0:T(8,128)(2,1)}, u32[]{:S(2)}, u32[]{:S(2)}) collective-permute-start(bf16[8,96,768]{2,1,0:T(8,128)(2,1)} %add_convert_fusion.1), channel_id=1, source_target_pairs={{0,16},{1,17},{2,18},{3,19},{4,20},{5,21},{6,22},{7,23},{8,24},{9,... | collective-permute-start | bytes 3538952 | tf_op jit(solution)/shard_map/ppermute | solution.py:30
  192.7 35.9 %attention_backward.1 = (bf16[512,768]{1,0:T(8,128)(2,1)}, bf16[1568,768]{1,0:T(8,128)(2,1)}, bf16[1568,768]{1,0:T(8,128)(2,1)}, bf16[16,24,1152]{2,1,0:T(8,128)...) custom-call(s32[4]{0:T(128)} %lengths_ref.3, ...), custom_call_target="tpu_custom_call" | custom-call | tf_op jit(solution)/shard_map/attention_backward/pallas_call | solution.py:513
  230.5 2.4 fusion.7
  232.9 10.8 %collective-permute-start.32 = (bf16[16,24,1280]{2,1,0:T(8,128)(2,1)S(1)}, bf16[16,24,1280]{2,1,0:T(8,128)(2,1)S(1)}, u32[]{:S(2)}, u32[]{:S(2)}) collective-permute-start(bf16[16,24,1280]{2,1,0:T(8,128)(2,1)S(1)} %copy-done.41), channel_id=1, source_target_pairs={{0,1},{1,0},{2,3},{3,2},{4,5},{5,4},{6,7},{7,6},{8,9},{9,8},{10,11... | collective-permute-start | bytes 2949128 | tf_op jit(solution)/shard_map/ppermute | solution.py:30
  243.9 2.0 add_convert_fusion.6
  246.0 4.3 %collective-permute-start.37 = (bf16[2,96,768]{2,1,0:T(8,128)(2,1)S(1)}, bf16[2,96,768]{2,1,0:T(8,128)(2,1)S(1)}, u32[]{:S(2)}, u32[]{:S(2)}) collective-permute-start(bf16[2,96,768]{2,1,0:T(8,128)(2,1)S(1)} %get-tuple-element.184), channel_id=1, source_target_pairs={{0,12},{1,13},{2,14},{3,15},{4,8},{5,9},{6,10},{7,11},{8,4},{9,5},... | collective-permute-start | bytes 884744 | tf_op jit(solution)/shard_map/ppermute | solution.py:30
  250.3 1.6 add_convert_fusion.3
  258.3 1.8 collective-permute-start.38
  260.1 7.9 %collective-permute-done.36 = bf16[2,96,768]{2,1,0:T(8,128)(2,1)S(1)} collective-permute-done((bf16[2,96,768]{2,1,0:T(8,128)(2,1)S(1)}, bf16[2,96,768]{2,1,0:T(8,128)(2,1)S(1)}, u32[]{:S(2)}, u32[]{:S(2)}) %collective-permute-start.36) | collective-permute-done | bytes 294944 | tf_op jit(solution)/shard_map/ppermute | solution.py:30
  268.0 6.8 %collective-permute-done.34 = bf16[4,24,3840]{2,1,0:T(8,128)(2,1)S(1)} collective-permute-done((bf16[4,24,3840]{2,1,0:T(8,128)(2,1)S(1)}, bf16[4,24,3840]{2,1,0:T(8,128)(2,1)S(1)}, u32[]{:S(2)}, u32[]{:S(2)}) %collective-permute-start.34) | collective-permute-done | bytes 737312 | tf_op jit(solution)/shard_map/ppermute | solution.py:30
  274.8 2.1 add_convert_fusion.14
  276.9 2.4 add_convert_fusion.11
  284.6 4.4 %collective-permute-start.43 = (bf16[1,24,3840]{2,1,0:T(8,128)(2,1)}, bf16[1,24,3840]{2,1,0:T(8,128)(2,1)}, u32[]{:S(2)}, u32[]{:S(2)}) collective-permute-start(bf16[1,24,3840]{2,1,0:T(8,128)(2,1)} %get-tuple-element.182), channel_id=1, source_target_pairs={{0,4},{1,5},{2,6},{3,7},{4,0},{5,1},{6,2},{7,3},{8,12},{9,13},{10,... | collective-permute-start | bytes 552968 | tf_op jit(solution)/shard_map/ppermute | solution.py:30
  289.0 3.9 %collective-permute-start.44 = (bf16[1,24,3840]{2,1,0:T(8,128)(2,1)}, bf16[1,24,3840]{2,1,0:T(8,128)(2,1)}, u32[]{:S(2)}, u32[]{:S(2)}) collective-permute-start(bf16[1,24,3840]{2,1,0:T(8,128)(2,1)} %get-tuple-element.181), channel_id=1, source_target_pairs={{0,12},{1,13},{2,14},{3,15},{4,8},{5,9},{6,10},{7,11},{8,4},{9,5},... | collective-permute-start | bytes 552968 | tf_op jit(solution)/shard_map/ppermute | solution.py:30
  295.3 2.0 gather_fusion
  303.7 2.0 add_bitcast_fusion.1
  305.7 1.8 add_convert_fusion.18
  307.6 1.6 collective-permute-start.48
  310.1 1.9 collective-permute-start.50
  312.0 5.1 %collective-permute-done.46 = bf16[4,24,1280]{2,1,0:T(8,128)(2,1)S(1)} collective-permute-done((bf16[4,24,1280]{2,1,0:T(8,128)(2,1)S(1)}, bf16[4,24,1280]{2,1,0:T(8,128)(2,1)S(1)}, u32[]{:S(2)}, u32[]{:S(2)}) %collective-permute-start.46) | collective-permute-done | bytes 245792 | tf_op jit(solution)/shard_map/ppermute | solution.py:30
  319.2 1.8 collective-permute-start.52
  322.3 1.9 gather_fusion.1
  325.5 1.7 collective-permute-start.53
  328.3 3.2 collective-permute-done.53
  (236 shorter events, 62.6 us)
Async XLA Ops:
  2.6 11.7 %collective-permute-start.3 = (bf16[1,24,2432]{2,1,0:T(8,128)(2,1)}, bf16[1,24,2432]{2,1,0:T(8,128)(2,1)S(1)}, u32[]{:S(2)}, u32[]{:S(2)}) collective-permute-start(bf16[1,24,2432]{2,1,0:T(8,128)(2,1)} %bitcast.27), channel_id=1, source_target_pairs={{0,8},{1,9},{2,10},{3,11},{4,12},{5,13},{6,14},{7,15},{8,0},{9,1},... | collective-permute-start | bytes 350216 | tf_op jit(solution)/shard_map/ppermute | solution.py:30
  6.6 7.7 %collective-permute-start.4 = (bf16[1,24,2432]{2,1,0:T(8,128)(2,1)}, bf16[1,24,2432]{2,1,0:T(8,128)(2,1)S(1)}, u32[]{:S(2)}, u32[]{:S(2)}) collective-permute-start(bf16[1,24,2432]{2,1,0:T(8,128)(2,1)} %bitcast.28), channel_id=1, source_target_pairs={{0,4},{1,5},{2,6},{3,7},{4,0},{5,1},{6,2},{7,3},{8,12},{9,13},{10,... | collective-permute-start | bytes 350216 | tf_op jit(solution)/shard_map/ppermute | solution.py:30
  8.2 8.0 %collective-permute-start.5 = (bf16[1,24,2432]{2,1,0:T(8,128)(2,1)}, bf16[1,24,2432]{2,1,0:T(8,128)(2,1)S(1)}, u32[]{:S(2)}, u32[]{:S(2)}) collective-permute-start(bf16[1,24,2432]{2,1,0:T(8,128)(2,1)} %bitcast.29), channel_id=1, source_target_pairs={{0,12},{1,13},{2,14},{3,15},{4,8},{5,9},{6,10},{7,11},{8,4},{9,5},... | collective-permute-start | bytes 350216 | tf_op jit(solution)/shard_map/ppermute | solution.py:30
  8.2 15.4 %collective-permute-start.7 = (bf16[1,96,768]{2,1,0:T(8,128)(2,1)}, bf16[1,96,768]{2,1,0:T(8,128)(2,1)S(1)}, u32[]{:S(2)}, u32[]{:S(2)}) collective-permute-start(bf16[1,96,768]{2,1,0:T(8,128)(2,1)} %bitcast.21), channel_id=1, source_target_pairs={{0,2},{1,3},{2,0},{3,1},{4,6},{5,7},{6,4},{7,5},{8,10},{9,11},{10,... | collective-permute-start | bytes 442376 | tf_op jit(solution)/shard_map/ppermute | solution.py:30
  11.3 23.6 %collective-permute-start = (bf16[512,768]{1,0:T(8,128)(2,1)S(1)}, bf16[512,768]{1,0:T(8,128)(2,1)S(1)}, u32[]{:S(2)}, u32[]{:S(2)}) collective-permute-start(bf16[512,768]{1,0:T(8,128)(2,1)S(1)} %convolution_convert_fusion.1.refs_1_.refs_2_), channel_id=1, source_target_pairs={{0,16},{1,17},{2,18},{3,19},{4,20},{5,21},{6,22},{7,23},{8,24},{9,... | collective-permute-start | bytes 2359304 | tf_op jit(solution)/shard_map/ppermute | solution.py:30
  16.4 20.0 %collective-permute-start.10 = (bf16[1,24,3840]{2,1,0:T(8,128)(2,1)}, bf16[1,24,3840]{2,1,0:T(8,128)(2,1)S(1)}, u32[]{:S(2)}, u32[]{:S(2)}) collective-permute-start(bf16[1,24,3840]{2,1,0:T(8,128)(2,1)} %bitcast.5), channel_id=1, source_target_pairs={{0,12},{1,13},{2,14},{3,15},{4,8},{5,9},{6,10},{7,11},{8,4},{9,5},... | collective-permute-start | bytes 552968 | tf_op jit(solution)/shard_map/ppermute | solution.py:30
  18.9 17.5 %collective-permute-start.8 = (bf16[1,24,3840]{2,1,0:T(8,128)(2,1)}, bf16[1,24,3840]{2,1,0:T(8,128)(2,1)S(1)}, u32[]{:S(2)}, u32[]{:S(2)}) collective-permute-start(bf16[1,24,3840]{2,1,0:T(8,128)(2,1)} %bitcast.5), channel_id=1, source_target_pairs={{0,8},{1,9},{2,10},{3,11},{4,12},{5,13},{6,14},{7,15},{8,0},{9,1},... | collective-permute-start | bytes 552968 | tf_op jit(solution)/shard_map/ppermute | solution.py:30
  22.1 7.1 %collective-permute-start.11 = (bf16[4,24,1152]{2,1,0:T(8,128)(2,1)S(1)}, bf16[4,24,1152]{2,1,0:T(8,128)(2,1)S(1)}, u32[]{:S(2)}, u32[]{:S(2)}) collective-permute-start(bf16[4,24,1152]{2,1,0:T(8,128)(2,1)S(1)} %get-tuple-element.196), channel_id=1, source_target_pairs={{0,2},{1,3},{2,0},{3,1},{4,6},{5,7},{6,4},{7,5},{8,10},{9,11},{10,... | collective-permute-start | bytes 663560 | tf_op jit(solution)/shard_map/ppermute | solution.py:30
  23.7 11.2 %collective-permute-start.6 = (bf16[4,24,1280]{2,1,0:T(8,128)(2,1)S(1)}, bf16[4,24,1280]{2,1,0:T(8,128)(2,1)S(1)}, u32[]{:S(2)}, u32[]{:S(2)}) collective-permute-start(bf16[4,24,1280]{2,1,0:T(8,128)(2,1)S(1)} %pad_maximum_fusion.6), channel_id=1, source_target_pairs={{0,16},{1,17},{2,18},{3,19},{4,20},{5,21},{6,22},{7,23},{8,24},{9,... | collective-permute-start | bytes 737288 | tf_op jit(solution)/shard_map/ppermute | solution.py:30
  29.2 9.6 %collective-permute-start.9 = (bf16[1,24,3840]{2,1,0:T(8,128)(2,1)}, bf16[1,24,3840]{2,1,0:T(8,128)(2,1)S(1)}, u32[]{:S(2)}, u32[]{:S(2)}) collective-permute-start(bf16[1,24,3840]{2,1,0:T(8,128)(2,1)} %bitcast.5), channel_id=1, source_target_pairs={{0,4},{1,5},{2,6},{3,7},{4,0},{5,1},{6,2},{7,3},{8,12},{9,13},{10,... | collective-permute-start | bytes 552968 | tf_op jit(solution)/shard_map/ppermute | solution.py:30
  35.0 33.2 %collective-permute-start.1 = (bf16[528,768]{1,0:T(8,128)(2,1)S(1)}, bf16[528,768]{1,0:T(8,128)(2,1)S(1)}, u32[]{:S(2)}, u32[]{:S(2)}) collective-permute-start(bf16[528,768]{1,0:T(8,128)(2,1)S(1)} %maximum_select_fusion), channel_id=1, source_target_pairs={{0,1},{1,2},{2,3},{3,4},{4,5},{5,6},{6,7},{7,8},{8,9},{9,10},{10,1... | collective-permute-start | bytes 2433032 | tf_op jit(solution)/shard_map/ppermute | solution.py:799
  40.8 27.4 %collective-permute-start.12 = (bf16[4,24,3840]{2,1,0:T(8,128)(2,1)S(1)}, bf16[4,24,3840]{2,1,0:T(8,128)(2,1)S(1)}, u32[]{:S(2)}, u32[]{:S(2)}) collective-permute-start(bf16[4,24,3840]{2,1,0:T(8,128)(2,1)S(1)} %get-tuple-element.198), channel_id=1, source_target_pairs={{0,16},{1,17},{2,18},{3,19},{4,20},{5,21},{6,22},{7,23},{8,24},{9,... | collective-permute-start | bytes 2211848 | tf_op jit(solution)/shard_map/ppermute | solution.py:30
  42.3 25.9 %collective-permute-start.13 = (bf16[8,24,1280]{2,1,0:T(8,128)(2,1)S(1)}, bf16[8,24,1280]{2,1,0:T(8,128)(2,1)S(1)}, u32[]{:S(2)}, u32[]{:S(2)}) collective-permute-start(bf16[8,24,1280]{2,1,0:T(8,128)(2,1)S(1)} %pad_maximum_fusion.2.refs_4_), channel_id=1, source_target_pairs={{0,2},{1,3},{2,0},{3,1},{4,6},{5,7},{6,4},{7,5},{8,10},{9,11},{10,... | collective-permute-start | bytes 1474568 | tf_op jit(solution)/shard_map/ppermute | solution.py:30
  43.8 23.8 %collective-permute-start.15 = (bf16[8,24,1152]{2,1,0:T(8,128)(2,1)S(1)}, bf16[8,24,1152]{2,1,0:T(8,128)(2,1)S(1)}, u32[]{:S(2)}, u32[]{:S(2)}) collective-permute-start(bf16[8,24,1152]{2,1,0:T(8,128)(2,1)S(1)} %pad_maximum_fusion.4.refs_8_), channel_id=1, source_target_pairs={{0,16},{1,17},{2,18},{3,19},{4,20},{5,21},{6,22},{7,23},{8,24},{9,... | collective-permute-start | bytes 1327112 | tf_op jit(solution)/shard_map/ppermute | solution.py:30
  44.4 15.1 %collective-permute-start.14 = (bf16[2,96,768]{2,1,0:T(8,128)(2,1)S(1)}, bf16[2,96,768]{2,1,0:T(8,128)(2,1)S(1)}, u32[]{:S(2)}, u32[]{:S(2)}) collective-permute-start(bf16[2,96,768]{2,1,0:T(8,128)(2,1)S(1)} %pad_maximum_fusion.5), channel_id=1, source_target_pairs={{0,8},{1,9},{2,10},{3,11},{4,12},{5,13},{6,14},{7,15},{8,0},{9,1},... | collective-permute-start | bytes 884744 | tf_op jit(solution)/shard_map/ppermute | solution.py:30
  59.4 8.8 %collective-permute-start.2 = (bf16[16,768]{1,0:T(8,128)(2,1)S(1)}, bf16[16,768]{1,0:T(8,128)(2,1)S(1)}, u32[]{:S(2)}, u32[]{:S(2)}) collective-permute-start(bf16[16,768]{1,0:T(8,128)(2,1)S(1)} %get-tuple-element.193), channel_id=1, source_target_pairs={{1,0},{2,1},{3,2},{4,3},{5,4},{6,5},{7,6},{8,7},{9,8},{10,9},{11,1... | collective-permute-start | bytes 73736 | tf_op jit(solution)/shard_map/ppermute | solution.py:799
  67.6 13.2 %collective-permute-start.16 = (bf16[4,96,768]{2,1,0:T(8,128)(2,1)S(1)}, bf16[4,96,768]{2,1,0:T(8,128)(2,1)S(1)}, u32[]{:S(2)}, u32[]{:S(2)}) collective-permute-start(bf16[4,96,768]{2,1,0:T(8,128)(2,1)S(1)} %pad_maximum_fusion.1), channel_id=1, source_target_pairs={{0,4},{1,5},{2,6},{3,7},{4,0},{5,1},{6,2},{7,3},{8,12},{9,13},{10,... | collective-permute-start | bytes 1769480 | tf_op jit(solution)/shard_map/ppermute | solution.py:30
  69.4 56.8 %collective-permute-start.21 = (bf16[8,24,3840]{2,1,0:T(8,128)(2,1)}, bf16[8,24,3840]{2,1,0:T(8,128)(2,1)}, u32[]{:S(2)}, u32[]{:S(2)}) collective-permute-start(bf16[8,24,3840]{2,1,0:T(8,128)(2,1)} %constant_dynamic-update-slice_fusion.4.refs_6_), channel_id=1, source_target_pairs={{0,2},{1,3},{2,0},{3,1},{4,6},{5,7},{6,4},{7,5},{8,10},{9,11},{10,... | collective-permute-start | bytes 4423688 | tf_op jit(solution)/shard_map/ppermute | solution.py:30
  71.9 12.2 %collective-permute-start.19 = (bf16[8,24,1152]{2,1,0:T(8,128)(2,1)S(1)}, bf16[8,24,1152]{2,1,0:T(8,128)(2,1)S(1)}, u32[]{:S(2)}, u32[]{:S(2)}) collective-permute-start(bf16[8,24,1152]{2,1,0:T(8,128)(2,1)S(1)} %pad_maximum_fusion.4.refs_8_), channel_id=1, source_target_pairs={{0,1},{1,0},{2,3},{3,2},{4,5},{5,4},{6,7},{7,6},{8,9},{9,8},{10,11... | collective-permute-start | bytes 1327112 | tf_op jit(solution)/shard_map/ppermute | solution.py:30
  82.1 55.1 %collective-permute-start.24 = (bf16[8,96,768]{2,1,0:T(8,128)(2,1)}, bf16[8,96,768]{2,1,0:T(8,128)(2,1)}, u32[]{:S(2)}, u32[]{:S(2)}) collective-permute-start(bf16[8,96,768]{2,1,0:T(8,128)(2,1)} %pad_maximum_fusion.refs_10_), channel_id=1, source_target_pairs={{0,16},{1,17},{2,18},{3,19},{4,20},{5,21},{6,22},{7,23},{8,24},{9,... | collective-permute-start | bytes 3538952 | tf_op jit(solution)/shard_map/ppermute | solution.py:30
  85.4 58.2 %collective-permute-start.22 = (bf16[8,24,3840]{2,1,0:T(8,128)(2,1)}, bf16[8,24,3840]{2,1,0:T(8,128)(2,1)}, u32[]{:S(2)}, u32[]{:S(2)}) collective-permute-start(bf16[8,24,3840]{2,1,0:T(8,128)(2,1)} %constant_dynamic-update-slice_fusion.4.refs_6_), channel_id=1, source_target_pairs={{0,1},{1,0},{2,3},{3,2},{4,5},{5,4},{6,7},{7,6},{8,9},{9,8},{10,11... | collective-permute-start | bytes 4423688 | tf_op jit(solution)/shard_map/ppermute | solution.py:30
  126.2 17.5 %collective-permute-start.23 = (bf16[8,24,3840]{2,1,0:T(8,128)(2,1)}, bf16[8,24,3840]{2,1,0:T(8,128)(2,1)S(1)}, u32[]{:S(2)}, u32[]{:S(2)}) collective-permute-start(bf16[8,24,3840]{2,1,0:T(8,128)(2,1)} %collective-permute-done.21.refs_7_), channel_id=1, source_target_pairs={{0,1},{1,0},{2,3},{3,2},{4,5},{5,4},{6,7},{7,6},{8,9},{9,8},{10,11... | collective-permute-start | bytes 4423688 | tf_op jit(solution)/shard_map/ppermute | solution.py:30
  137.1 6.5 %collective-permute-start.25 = (bf16[8,96,768]{2,1,0:T(8,128)(2,1)}, bf16[8,96,768]{2,1,0:T(8,128)(2,1)S(1)}, u32[]{:S(2)}, u32[]{:S(2)}) collective-permute-start(bf16[8,96,768]{2,1,0:T(8,128)(2,1)} %pad_maximum_fusion.refs_10_), channel_id=1, source_target_pairs={{0,1},{1,0},{2,3},{3,2},{4,5},{5,4},{6,7},{7,6},{8,9},{9,8},{10,11... | collective-permute-start | bytes 3538952 | tf_op jit(solution)/shard_map/ppermute | solution.py:30
  137.2 6.5 %collective-permute-start.26 = (bf16[8,96,768]{2,1,0:T(8,128)(2,1)}, bf16[8,96,768]{2,1,0:T(8,128)(2,1)}, u32[]{:S(2)}, u32[]{:S(2)}) collective-permute-start(bf16[8,96,768]{2,1,0:T(8,128)(2,1)} %collective-permute-done.24.refs_11_), channel_id=1, source_target_pairs={{0,1},{1,0},{2,3},{3,2},{4,5},{5,4},{6,7},{7,6},{8,9},{9,8},{10,11... | collective-permute-start | bytes 3538952 | tf_op jit(solution)/shard_map/ppermute | solution.py:30
  176.8 9.3 %collective-permute-start.28 = (bf16[16,96,768]{2,1,0:T(8,128)(2,1)}, bf16[16,96,768]{2,1,0:T(8,128)(2,1)S(1)}, u32[]{:S(2)}, u32[]{:S(2)}) collective-permute-start(bf16[16,96,768]{2,1,0:T(8,128)(2,1)} %get-tuple-element.119), channel_id=1, source_target_pairs={{0,1},{1,0},{2,3},{3,2},{4,5},{5,4},{6,7},{7,6},{8,9},{9,8},{10,11... | collective-permute-start | bytes 7077896 | tf_op jit(solution)/shard_map/ppermute | solution.py:30
  186.1 42.5 %collective-permute-start.29 = (bf16[8,24,3840]{2,1,0:T(8,128)(2,1)}, bf16[8,24,3840]{2,1,0:T(8,128)(2,1)}, u32[]{:S(2)}, u32[]{:S(2)}) collective-permute-start(bf16[8,24,3840]{2,1,0:T(8,128)(2,1)} %add_convert_fusion), channel_id=1, source_target_pairs={{0,2},{1,3},{2,0},{3,1},{4,6},{5,7},{6,4},{7,5},{8,10},{9,11},{10,... | collective-permute-start | bytes 4423688 | tf_op jit(solution)/shard_map/ppermute | solution.py:30
  187.9 40.7 %collective-permute-start.30 = (bf16[8,96,768]{2,1,0:T(8,128)(2,1)}, bf16[8,96,768]{2,1,0:T(8,128)(2,1)}, u32[]{:S(2)}, u32[]{:S(2)}) collective-permute-start(bf16[8,96,768]{2,1,0:T(8,128)(2,1)} %add_convert_fusion.1), channel_id=1, source_target_pairs={{0,16},{1,17},{2,18},{3,19},{4,20},{5,21},{6,22},{7,23},{8,24},{9,... | collective-permute-start | bytes 3538952 | tf_op jit(solution)/shard_map/ppermute | solution.py:30
  232.9 22.8 %collective-permute-start.32 = (bf16[16,24,1280]{2,1,0:T(8,128)(2,1)S(1)}, bf16[16,24,1280]{2,1,0:T(8,128)(2,1)S(1)}, u32[]{:S(2)}, u32[]{:S(2)}) collective-permute-start(bf16[16,24,1280]{2,1,0:T(8,128)(2,1)S(1)} %copy-done.41), channel_id=1, source_target_pairs={{0,1},{1,0},{2,3},{3,2},{4,5},{5,4},{6,7},{7,6},{8,9},{9,8},{10,11... | collective-permute-start | bytes 2949128 | tf_op jit(solution)/shard_map/ppermute | solution.py:30
  243.8 11.6 %collective-permute-start.31 = (bf16[16,24,1152]{2,1,0:T(8,128)(2,1)S(1)}, bf16[16,24,1152]{2,1,0:T(8,128)(2,1)S(1)}, u32[]{:S(2)}, u32[]{:S(2)}) collective-permute-start(bf16[16,24,1152]{2,1,0:T(8,128)(2,1)S(1)} %copy-done.42), channel_id=1, source_target_pairs={{0,1},{1,0},{2,3},{3,2},{4,5},{5,4},{6,7},{7,6},{8,9},{9,8},{10,11... | collective-permute-start | bytes 2654216 | tf_op jit(solution)/shard_map/ppermute | solution.py:30
  245.9 12.5 %collective-permute-start.35 = (bf16[2,96,768]{2,1,0:T(8,128)(2,1)S(1)}, bf16[2,96,768]{2,1,0:T(8,128)(2,1)S(1)}, u32[]{:S(2)}, u32[]{:S(2)}) collective-permute-start(bf16[2,96,768]{2,1,0:T(8,128)(2,1)S(1)} %get-tuple-element.186), channel_id=1, source_target_pairs={{0,8},{1,9},{2,10},{3,11},{4,12},{5,13},{6,14},{7,15},{8,0},{9,1},... | collective-permute-start | bytes 884744 | tf_op jit(solution)/shard_map/ppermute | solution.py:30
  245.9 22.1 %collective-permute-start.36 = (bf16[2,96,768]{2,1,0:T(8,128)(2,1)S(1)}, bf16[2,96,768]{2,1,0:T(8,128)(2,1)S(1)}, u32[]{:S(2)}, u32[]{:S(2)}) collective-permute-start(bf16[2,96,768]{2,1,0:T(8,128)(2,1)S(1)} %get-tuple-element.185), channel_id=1, source_target_pairs={{0,4},{1,5},{2,6},{3,7},{4,0},{5,1},{6,2},{7,3},{8,12},{9,13},{10,... | collective-permute-start | bytes 884744 | tf_op jit(solution)/shard_map/ppermute | solution.py:30
  246.0 22.0 %collective-permute-start.37 = (bf16[2,96,768]{2,1,0:T(8,128)(2,1)S(1)}, bf16[2,96,768]{2,1,0:T(8,128)(2,1)S(1)}, u32[]{:S(2)}, u32[]{:S(2)}) collective-permute-start(bf16[2,96,768]{2,1,0:T(8,128)(2,1)S(1)} %get-tuple-element.184), channel_id=1, source_target_pairs={{0,12},{1,13},{2,14},{3,15},{4,8},{5,9},{6,10},{7,11},{8,4},{9,5},... | collective-permute-start | bytes 884744 | tf_op jit(solution)/shard_map/ppermute | solution.py:30
  255.4 19.5 %collective-permute-start.34 = (bf16[4,24,3840]{2,1,0:T(8,128)(2,1)S(1)}, bf16[4,24,3840]{2,1,0:T(8,128)(2,1)S(1)}, u32[]{:S(2)}, u32[]{:S(2)}) collective-permute-start(bf16[4,24,3840]{2,1,0:T(8,128)(2,1)S(1)} %add_convert_fusion.3), channel_id=1, source_target_pairs={{0,16},{1,17},{2,18},{3,19},{4,20},{5,21},{6,22},{7,23},{8,24},{9,... | collective-permute-start | bytes 2211848 | tf_op jit(solution)/shard_map/ppermute | solution.py:30
  255.8 23.6 %collective-permute-start.33 = (bf16[528,768]{1,0:T(8,128)(2,1)S(1)}, bf16[528,768]{1,0:T(8,128)(2,1)S(1)}, u32[]{:S(2)}, u32[]{:S(2)}) collective-permute-start(bf16[528,768]{1,0:T(8,128)(2,1)S(1)} %add_convert_fusion.2), channel_id=1, source_target_pairs={{1,0},{2,1},{3,2},{4,3},{5,4},{6,5},{7,6},{8,7},{9,8},{10,9},{11,1... | collective-permute-start | bytes 2433032 | tf_op jit(solution)/shard_map/ppermute | solution.py:799
  258.3 30.7 %collective-permute-start.38 = (bf16[8,24,1152]{2,1,0:T(8,128)(2,1)S(1)}, bf16[8,24,1152]{2,1,0:T(8,128)(2,1)S(1)}, u32[]{:S(2)}, u32[]{:S(2)}) collective-permute-start(bf16[8,24,1152]{2,1,0:T(8,128)(2,1)S(1)} %add_convert_fusion.5), channel_id=1, source_target_pairs={{0,16},{1,17},{2,18},{3,19},{4,20},{5,21},{6,22},{7,23},{8,24},{9,... | collective-permute-start | bytes 1327112 | tf_op jit(solution)/shard_map/ppermute | solution.py:30
  268.0 25.7 %collective-permute-start.39 = (bf16[8,24,1280]{2,1,0:T(8,128)(2,1)S(1)}, bf16[8,24,1280]{2,1,0:T(8,128)(2,1)S(1)}, u32[]{:S(2)}, u32[]{:S(2)}) collective-permute-start(bf16[8,24,1280]{2,1,0:T(8,128)(2,1)S(1)} %add_convert_fusion.4), channel_id=1, source_target_pairs={{0,2},{1,3},{2,0},{3,1},{4,6},{5,7},{6,4},{7,5},{8,10},{9,11},{10,... | collective-permute-start | bytes 1474568 | tf_op jit(solution)/shard_map/ppermute | solution.py:30
  276.9 26.8 %collective-permute-start.45 = (bf16[1,96,768]{2,1,0:T(8,128)(2,1)}, bf16[1,96,768]{2,1,0:T(8,128)(2,1)}, u32[]{:S(2)}, u32[]{:S(2)}) collective-permute-start(bf16[1,96,768]{2,1,0:T(8,128)(2,1)} %add_convert_fusion.14), channel_id=1, source_target_pairs={{0,2},{1,3},{2,0},{3,1},{4,6},{5,7},{6,4},{7,5},{8,10},{9,11},{10,... | collective-permute-start | bytes 442376 | tf_op jit(solution)/shard_map/ppermute | solution.py:30
  279.3 19.1 %collective-permute-start.42 = (bf16[1,24,3840]{2,1,0:T(8,128)(2,1)}, bf16[1,24,3840]{2,1,0:T(8,128)(2,1)}, u32[]{:S(2)}, u32[]{:S(2)}) collective-permute-start(bf16[1,24,3840]{2,1,0:T(8,128)(2,1)} %get-tuple-element.183), channel_id=1, source_target_pairs={{0,8},{1,9},{2,10},{3,11},{4,12},{5,13},{6,14},{7,15},{8,0},{9,1},... | collective-permute-start | bytes 552968 | tf_op jit(solution)/shard_map/ppermute | solution.py:30
  284.6 15.0 %collective-permute-start.43 = (bf16[1,24,3840]{2,1,0:T(8,128)(2,1)}, bf16[1,24,3840]{2,1,0:T(8,128)(2,1)}, u32[]{:S(2)}, u32[]{:S(2)}) collective-permute-start(bf16[1,24,3840]{2,1,0:T(8,128)(2,1)} %get-tuple-element.182), channel_id=1, source_target_pairs={{0,4},{1,5},{2,6},{3,7},{4,0},{5,1},{6,2},{7,3},{8,12},{9,13},{10,... | collective-permute-start | bytes 552968 | tf_op jit(solution)/shard_map/ppermute | solution.py:30
  289.0 11.8 %collective-permute-start.44 = (bf16[1,24,3840]{2,1,0:T(8,128)(2,1)}, bf16[1,24,3840]{2,1,0:T(8,128)(2,1)}, u32[]{:S(2)}, u32[]{:S(2)}) collective-permute-start(bf16[1,24,3840]{2,1,0:T(8,128)(2,1)} %get-tuple-element.181), channel_id=1, source_target_pairs={{0,12},{1,13},{2,14},{3,15},{4,8},{5,9},{6,10},{7,11},{8,4},{9,5},... | collective-permute-start | bytes 552968 | tf_op jit(solution)/shard_map/ppermute | solution.py:30
  293.7 25.5 %collective-permute-start.40 = (bf16[512,768]{1,0:T(8,128)(2,1)}, bf16[512,768]{1,0:T(8,128)(2,1)}, u32[]{:S(2)}, u32[]{:S(2)}) collective-permute-start(bf16[512,768]{1,0:T(8,128)(2,1)} %fusion), channel_id=1, source_target_pairs={{0,16},{1,17},{2,18},{3,19},{4,20},{5,21},{6,22},{7,23},{8,24},{9,... | collective-permute-start | bytes 2359304 | tf_op jit(solution)/shard_map/ppermute | solution.py:30
  298.4 7.3 %collective-permute-start.41 = (bf16[4,24,1152]{2,1,0:T(8,128)(2,1)S(1)}, bf16[4,24,1152]{2,1,0:T(8,128)(2,1)S(1)}, u32[]{:S(2)}, u32[]{:S(2)}) collective-permute-start(bf16[4,24,1152]{2,1,0:T(8,128)(2,1)S(1)} %copy-done.35), channel_id=1, source_target_pairs={{0,2},{1,3},{2,0},{3,1},{4,6},{5,7},{6,4},{7,5},{8,10},{9,11},{10,... | collective-permute-start | bytes 663560 | tf_op jit(solution)/shard_map/ppermute | solution.py:30
  299.6 17.4 %collective-permute-start.46 = (bf16[4,24,1280]{2,1,0:T(8,128)(2,1)S(1)}, bf16[4,24,1280]{2,1,0:T(8,128)(2,1)S(1)}, u32[]{:S(2)}, u32[]{:S(2)}) collective-permute-start(bf16[4,24,1280]{2,1,0:T(8,128)(2,1)S(1)} %copy-done.34), channel_id=1, source_target_pairs={{0,16},{1,17},{2,18},{3,19},{4,20},{5,21},{6,22},{7,23},{8,24},{9,... | collective-permute-start | bytes 737288 | tf_op jit(solution)/shard_map/ppermute | solution.py:30
  307.6 17.9 %collective-permute-start.48 = (bf16[1,24,1152]{2,1,0:T(8,128)(2,1)}, bf16[1,24,1152]{2,1,0:T(8,128)(2,1)}, u32[]{:S(2)}, u32[]{:S(2)}) collective-permute-start(bf16[1,24,1152]{2,1,0:T(8,128)(2,1)} %get-tuple-element.192), channel_id=1, source_target_pairs={{0,8},{1,9},{2,10},{3,11},{4,12},{5,13},{6,14},{7,15},{8,0},{9,1},... | collective-permute-start | bytes 165896 | tf_op jit(solution)/shard_map/ppermute | solution.py:30
  309.2 18.1 %collective-permute-start.49 = (bf16[1,24,1152]{2,1,0:T(8,128)(2,1)}, bf16[1,24,1152]{2,1,0:T(8,128)(2,1)}, u32[]{:S(2)}, u32[]{:S(2)}) collective-permute-start(bf16[1,24,1152]{2,1,0:T(8,128)(2,1)} %get-tuple-element.191), channel_id=1, source_target_pairs={{0,4},{1,5},{2,6},{3,7},{4,0},{5,1},{6,2},{7,3},{8,12},{9,13},{10,... | collective-permute-start | bytes 165896 | tf_op jit(solution)/shard_map/ppermute | solution.py:30
  310.1 17.2 %collective-permute-start.50 = (bf16[1,24,1152]{2,1,0:T(8,128)(2,1)}, bf16[1,24,1152]{2,1,0:T(8,128)(2,1)}, u32[]{:S(2)}, u32[]{:S(2)}) collective-permute-start(bf16[1,24,1152]{2,1,0:T(8,128)(2,1)} %get-tuple-element.190), channel_id=1, source_target_pairs={{0,12},{1,13},{2,14},{3,15},{4,8},{5,9},{6,10},{7,11},{8,4},{9,5},... | collective-permute-start | bytes 165896 | tf_op jit(solution)/shard_map/ppermute | solution.py:30
  318.3 10.0 %collective-permute-start.51 = (bf16[1,24,1280]{2,1,0:T(8,128)(2,1)S(1)}, bf16[1,24,1280]{2,1,0:T(8,128)(2,1)S(1)}, u32[]{:S(2)}, u32[]{:S(2)}) collective-permute-start(bf16[1,24,1280]{2,1,0:T(8,128)(2,1)S(1)} %get-tuple-element.189), channel_id=1, source_target_pairs={{0,8},{1,9},{2,10},{3,11},{4,12},{5,13},{6,14},{7,15},{8,0},{9,1},... | collective-permute-start | bytes 184328 | tf_op jit(solution)/shard_map/ppermute | solution.py:30
  319.2 9.1 %collective-permute-start.52 = (bf16[1,24,1280]{2,1,0:T(8,128)(2,1)S(1)}, bf16[1,24,1280]{2,1,0:T(8,128)(2,1)}, u32[]{:S(2)}, u32[]{:S(2)}) collective-permute-start(bf16[1,24,1280]{2,1,0:T(8,128)(2,1)S(1)} %get-tuple-element.188), channel_id=1, source_target_pairs={{0,4},{1,5},{2,6},{3,7},{4,0},{5,1},{6,2},{7,3},{8,12},{9,13},{10,... | collective-permute-start | bytes 184328 | tf_op jit(solution)/shard_map/ppermute | solution.py:30
  (51 other events, 566.4 us)
